TPU v7x, 128 devices: a whole 4x4x4 slice. The times are simulated.
128 devices in a mesh: views: 8 (over z, core), bricks: 16 (over y, x).
Axes of the slice: x: 4, y: 4, z: 4, core: 2. Of those that a mesh axis runs over, the one named last changes fastest.
Arguments:
- tile_pixel: int32 [8, 16, 128], P('views', 'bricks'), may hold values from 0 to 15
- tile_voxel: int32 [8, 16, 128], P('views', 'bricks'), may hold values from 0 to 63
- tile_count: int32 [8, 16], P('views', 'bricks'), may hold values from 32 to 128, as said below
- features: bfloat16 [8, 16, 16, 64, 128], P('views', 'bricks'), may hold values from -6 to 6
- interp: bfloat16 [8, 16, 128, 128, 512], P('views', 'bricks'), may hold values from -0.5 to 0.5
- conv_weight: bfloat16 [3, 3, 3, 64, 64], replicated, may hold values from -0.15625 to 0.15625
- conv_bias: float32 [64], replicated, may hold values from -3 to 3
- smooth_coef: float32 [128, 256, 128], P('bricks', 'views'), may hold values from 0.04 to 0.16
Outputs:
- volume: bfloat16 [64, 128, 256, 128], P(None, 'bricks', 'views')
Inputs may be any that keep to these rules, and one draw needn't show every extreme that they name: `tile_count`: between 32 and 128 live tiles a device; counts are shared largely within a view group; some device has all 128 slots live in every draw.
All inputs are finite; a program needn't handle non-finite values.
Results may differ from a plain program's by a relative error of at most 0.0037.
Values may be sent and summed in bfloat16 or wider, within the bound.
No kernel may reach another device: no remote copies, remote signals or barrier semaphores. Data moves between devices by JAX's collectives and lax.ppermute only.
A program may use at most 256 MiB of HBM per device.

v0:
```python
import jax
import jax.numpy as jnp
from jax import lax
from jax.sharding import PartitionSpec as P


def padded_2(array, sides, width):
    for axis, dim in sides:
        size, length = (lax.axis_size(axis), array.shape[dim])
        up = [(i, (i + 1) % size) for i in range(size - 1)]
        down = [(j, i) for i, j in up]
        last = lax.slice_in_dim(array, length - width, length, axis=dim)
        first = lax.slice_in_dim(array, 0, width, axis=dim)
        before = lax.ppermute(last, axis, up)
        after = lax.ppermute(first, axis, down)
        array = jnp.concatenate([before, array, after], axis=dim)
    return array


def convolve(padded, weights, conv_bias, width_x, width_y):
    depth = padded.shape[3]
    deep = jnp.pad(padded, ((0, 0), (0, 0), (0, 0), (1, 1)))
    stacked = jnp.concatenate(
        [deep[..., 0:depth], deep[..., 1 : depth + 1], deep[..., 2 : depth + 2]], axis=0
    )
    total = jnp.zeros((weights.shape[1], width_x, width_y, depth), jnp.float32)
    for shift_x in range(3):
        for shift_y in range(3):
            window = stacked[:, shift_x : shift_x + width_x, shift_y : shift_y + width_y, :]
            total = total + jnp.einsum(
                "oi,ixyz->oxyz",
                weights[shift_x * 3 + shift_y],
                window,
                preferred_element_type=jnp.float32,
            )
    return jax.nn.relu(total + conv_bias[:, None, None, None])


def smooth(beside_all, smooth_coef):
    padded = jnp.pad(beside_all, ((0, 0), (0, 0), (0, 0), (1, 1)))
    center = padded[:, 1:-1, 1:-1, 1:-1]
    beside = padded[:, 2:, 1:-1, 1:-1] + padded[:, :-2, 1:-1, 1:-1]
    beside = beside + padded[:, 1:-1, 2:, 1:-1] + padded[:, 1:-1, :-2, 1:-1]
    beside = beside + padded[:, 1:-1, 1:-1, 2:] + padded[:, 1:-1, 1:-1, :-2]
    return center + smooth_coef[None] * (beside - 6.0 * center)


def on_device(
    tile_pixel, tile_voxel, tile_count, features, interp, conv_weight, conv_bias, smooth_coef
):
    feats = features[0, 0]
    tiles = interp[0, 0]
    pixel_ids = tile_pixel[0, 0]
    voxel_ids = tile_voxel[0, 0]
    count = tile_count[0, 0]
    slots_total = tiles.shape[0]
    channels = feats.shape[1]
    pixels = feats.shape[2]
    size_x = smooth_coef.shape[0]
    size_y = smooth_coef.shape[1]
    depth = smooth_coef.shape[2]
    blocks = size_x * size_y // 4
    n_bricks = lax.axis_size("bricks")
    brick_index = lax.axis_index("bricks")
    view_index = lax.axis_index("views")
    sender = view_index * n_bricks + brick_index
    offset = jnp.remainder(sender * 37, slots_total)
    slot_ids = jnp.arange(slots_total, dtype=jnp.int32)
    live = jnp.remainder(slot_ids - offset, slots_total) < count
    target = (
        live[:, None] & (voxel_ids[:, None] == jnp.arange(blocks, dtype=jnp.int32)[None, :])
    ).astype(jnp.bfloat16)
    selector = (pixel_ids[:, None] == jnp.arange(feats.shape[0], dtype=jnp.int32)[None, :]).astype(
        jnp.bfloat16
    )
    chosen = jnp.einsum(
        "dk,kq->dq",
        selector,
        feats.reshape(feats.shape[0], channels * pixels),
        preferred_element_type=jnp.float32,
    )
    chosen = chosen.astype(jnp.bfloat16).reshape(slots_total, channels, pixels)
    partial_value = jnp.einsum(
        "dcp,dpv->dcv", chosen, tiles, preferred_element_type=jnp.float32
    ).astype(jnp.bfloat16)
    got_part, got_target = (
        lax.all_to_all(partial_value, ("views", "bricks"), split_axis=0, concat_axis=0, tiled=True),
        lax.all_to_all(target, ("views", "bricks"), split_axis=0, concat_axis=0, tiled=True),
    )
    lifted = jnp.einsum("sb,scv->cbv", got_target, got_part, preferred_element_type=jnp.float32)
    lifted = lifted.reshape(channels, size_x, size_y, depth)
    rectified = jax.nn.relu(lifted).astype(jnp.bfloat16)
    weights = jnp.transpose(conv_weight, (0, 1, 3, 2, 4)).reshape(9, channels, 3 * channels)
    padded = padded_2(rectified, (("views", 2), ("bricks", 1)), 1)
    gated = convolve(padded, weights, conv_bias, size_x, size_y)
    beside_all = padded_2(gated, (("views", 2), ("bricks", 1)), 1)
    return smooth(beside_all, smooth_coef).astype(jnp.bfloat16)


def solution(mesh):
    in_specs = (
        P("views", "bricks", None),
        P("views", "bricks", None),
        P("views", "bricks"),
        P("views", "bricks", None, None, None),
        P("views", "bricks", None, None, None),
        P(),
        P(),
        P("bricks", "views", None),
    )
    out_specs = P(None, "bricks", "views", None)
    return jax.shard_map(
        on_device, mesh=mesh, in_specs=in_specs, out_specs=out_specs, check_vma=False
    )
```

profile of v0, /device:TPU:38, one launch (start us, length us, event | category | flops | bytes accessed | tf_op | source)
XLA Modules:
  0.0 373.8 jit_solution(15814059282729813025)
XLA Ops:
  0.7 1.6 and_convert_fusion
  2.3 10.2 %all-to-all-start.1 = ((bf16[128,1,64]{2,1,0:T(2,128)(2,1)}), bf16[128,1,64]{2,1,0:T(2,128)(2,1)S(1)}, u32[]{:S(2)}, u32[]{:S(2)}) async-start(bf16[128,1,64]{2,1,0:T(2,128)(2,1)} %and_convert_fusion), calls=%async_computation.1 | async-start | bytes 131072 | tf_op jit(solution)/shard_map/all_to_all | solution.py:88
  12.5 1.7 fusion.37
  14.2 0.6 copy.63
  14.8 11.5 %fusion.31 = bf16[128,64,512]{2,1,0:T(8,128)(2,1)} fusion(bf16[128,64,128]{2,1,0:T(8,128)(2,1)S(1)} %bitcast.104, bf16[1,1,128,128,512]{4,3,2,1,0:T(8,128)(2,1)} %param.12), kind=kOutput, calls=%fused_computation.53 | convolution fusion | flops 1077936128 | bytes 27262976 | tf_op jit(solution)/shard_map/dcp,dpv->dcv/dot_general | solution.py:83
  26.3 0.0 all-to-all-done.1
  26.3 10.8 %all-to-all-start = ((bf16[128,64,512]{2,1,0:T(8,128)(2,1)}), bf16[128,64,512]{2,1,0:T(8,128)(2,1)}, u32[]{:S(2)}, u32[]{:S(2)}) async-start(bf16[128,64,512]{2,1,0:T(8,128)(2,1)} %fusion.31), calls=%async_computation | async-start | bytes 16777216 | tf_op jit(solution)/shard_map/all_to_all | solution.py:87
  37.1 0.1 copy.28
  37.2 100.7 %all-to-all-done = bf16[128,64,512]{2,1,0:T(8,128)(2,1)} async-done(((bf16[128,64,512]{2,1,0:T(8,128)(2,1)}), bf16[128,64,512]{2,1,0:T(8,128)(2,1)}, u32[]{:S(2)}, u32[]{:S(2)}) %all-to-all-start) | async-done | bytes 8388640 | tf_op jit(solution)/shard_map/all_to_all | solution.py:87
  138.0 15.3 %fusion.34 = bf16[64,64,512]{2,1,0:T(8,128)(2,1)} fusion(bf16[128,64,512]{2,1,0:T(8,128)(2,1)} %all-to-all-done, bf16[128,1,64]{0,2,1:T(8,128)(2,1)S(1)} %copy.28), kind=kOutput, calls=%fused_computation.54 | convolution fusion | flops 541065216 | bytes 12599296 | tf_op jit(solution)/shard_map/sb,scv->cbv/dot_general | solution.py:90
  153.3 7.5 %convert_element_type.38 = bf16[64,8,32,128]{3,2,1,0:T(8,128)(2,1)} reshape(bf16[64,64,512]{2,1,0:T(8,128)(2,1)} %fusion.34) | data formatting | bytes 8388608 | tf_op jit(solution)/shard_map/convert_element_type | solution.py:92
  160.8 0.0 copy-start.3
  160.8 2.1 fusion.49
  162.8 0.1 copy.73
  162.9 1.9 collective-permute-start
  164.8 0.1 copy.74
  164.9 13.8 %collective-permute-start.1 = (bf16[64,8,1,128]{3,0,2,1:T(8,128)(2,1)S(1)}, bf16[64,8,1,128]{3,0,2,1:T(8,128)(2,1)S(1)}, u32[]{:S(2)}, u32[]{:S(2)}) collective-permute-start(bf16[64,8,1,128]{3,0,2,1:T(8,128)(2,1)S(1)} %copy.74), channel_id=1, source_target_pairs={{16,0},{32,16},{48,32},{64,48},{80,64},{96,80},{112,96},{17,1},{33... | collective-permute-start | bytes 393224 | tf_op jit(solution)/shard_map/ppermute | solution.py:15
  178.7 0.0 collective-permute-done
  178.7 5.2 %constant_dynamic-update-slice_fusion.1 = bf16[64,8,34,128]{3,0,2,1:T(8,128)(2,1)S(1)} fusion(bf16[64,8,34,128]{3,0,2,1:T(8,128)(2,1)S(1)} %constant_dynamic-update-slice_fusion.2, bf16[64,8,32,128]{3,2,1,0:T(8,128)(2,1)} %convert_element_type.38), kind=kLoop, calls=%fused_computation.75 | loop fusion | bytes 8388608
  183.9 0.0 collective-permute-done.1
  183.9 0.0 copy-start.1
  183.9 2.1 copy-done.1
  186.0 0.1 fusion.48
  186.1 1.9 collective-permute-start.2
  188.0 7.6 %collective-permute-start.3 = (bf16[64,1,34,128]{3,0,2,1:T(8,128)(2,1)S(1)}, bf16[64,1,34,128]{3,0,2,1:T(8,128)(2,1)S(1)}, u32[]{:S(2)}, u32[]{:S(2)}) collective-permute-start(bf16[64,1,34,128]{3,0,2,1:T(8,128)(2,1)S(1)} %get-tuple-element.12), channel_id=1, source_target_pairs={{1,0},{2,1},{3,2},{4,3},{5,4},{6,5},{7,6},{8,7},{9,8},{10,9},{11,1... | collective-permute-start | bytes 1671176 | tf_op jit(solution)/shard_map/ppermute | solution.py:15
  195.6 0.0 copy-done.3
  195.6 1.0 copy.33
  196.6 8.7 %collective-permute-done.2 = bf16[64,1,34,128]{3,0,2,1:T(8,128)(2,1)S(1)} collective-permute-done((bf16[64,1,34,128]{3,0,2,1:T(8,128)(2,1)S(1)}, bf16[64,1,34,128]{3,0,2,1:T(8,128)(2,1)S(1)}, u32[]{:S(2)}, u32[]{:S(2)}) %collective-permute-start.2) | collective-permute-done | bytes 557088 | tf_op jit(solution)/shard_map/ppermute | solution.py:14
  205.2 2.2 collective-permute-done.3
  207.5 0.0 slice-start
  207.5 11.4 %select_maximum_fusion.4 = bf16[64,10,34,130]{3,0,2,1:T(8,128)(2,1)S(1)} fusion(bf16[64,1,34,128]{3,0,2,1:T(8,128)(2,1)S(1)} %collective-permute-done.3, bf16[64,8,34,128]{3,0,2,1:T(8,128)(2,1)} %copy-done.1, bf16[64,1,34,128]{3,0,2,1:T(8,128)(2,1)S(1)} %collective-permute-done.2), kind=kLoop, calls=%fused_computation.28 | loop fusion | flops 33945600 | bytes 11228160 | tf_op jit(solution)/shard_map/concatenate | solution.py:16
  218.9 0.0 slice-start.1
  218.9 5.9 %fusion.46 = (bf16[64,10,34,128]{3,0,2,1:T(8,128)(2,1)}, bf16[64,10,34,128]{3,0,2,1:T(8,128)(2,1)}) fusion(bf16[64,10,34,130]{3,0,2,1:T(8,128)(2,1)S(1)} %select_maximum_fusion.4), kind=kLoop, calls=%fused_computation.82 | loop fusion | bytes 22282240 | tf_op jit(solution)/shard_map/slice | solution.py:24
  224.9 0.0 slice-done
  224.9 0.0 slice-done.1
  224.9 9.4 %pad_maximum_fusion = bf16[192,10,34,128]{3,0,2,1:T(8,128)(2,1)S(1)} fusion(bf16[64,10,34,128]{3,0,2,1:T(8,128)(2,1)} %get-tuple-element.6, bf16[64,1,34,128]{3,0,2,1:T(8,128)(2,1)S(1)} %collective-permute-done.3, bf16[64,8,34,128]{3,0,2,1:T(8,128)(2,1)S(1)} %bitcast.103, bf16[64,1,34,128]{3,0,2,1:T(8,128)(2,1)S(1)} %collective-permute-done.2, ...), kind=kLoop, calls=%fused_computation.9 | loop fusion | flops 83558400 | bytes 33423360 | tf_op jit(solution)/shard_map/concatenate | solution.py:23
  234.3 0.0 copy-start
  234.3 0.0 copy-start.2
  234.3 6.3 %fusion.5 = f32[8,32,128,64]{2,3,1,0:T(8,128)} fusion(bf16[192,10,34,128]{3,0,2,1:T(8,128)(2,1)S(1)} %pad_maximum_fusion, bf16[9,64,192]{1,2,0:T(8,128)(2,1)} %bitcast.105), kind=kOutput, calls=%fused_computation.12 | convolution fusion | flops 805306368 | bytes 21020672 | tf_op jit(solution)/shard_map/oi,ixyz->oxyz/dot_general | solution.py:30
  240.6 0.0 copy-done.2
  240.6 4.6 %fusion.7 = f32[8,32,128,64]{2,3,1,0:T(8,128)} fusion(bf16[192,10,34,128]{3,0,2,1:T(8,128)(2,1)S(1)} %pad_maximum_fusion, bf16[9,64,192]{1,2,0:T(8,128)(2,1)S(1)} %bitcast.106), kind=kOutput, calls=%fused_computation.14 | convolution fusion | flops 805306368 | bytes 21020672 | tf_op jit(solution)/shard_map/oi,ixyz->oxyz/dot_general | solution.py:30
  245.2 4.7 %fusion.9 = f32[8,32,128,64]{2,3,1,0:T(8,128)} fusion(bf16[192,10,34,128]{3,0,2,1:T(8,128)(2,1)S(1)} %pad_maximum_fusion, bf16[9,64,192]{1,2,0:T(8,128)(2,1)S(1)} %bitcast.107), kind=kOutput, calls=%fused_computation.16 | convolution fusion | flops 805306368 | bytes 21020672 | tf_op jit(solution)/shard_map/oi,ixyz->oxyz/dot_general | solution.py:30
  249.9 4.6 %fusion.11 = f32[8,32,128,64]{2,3,1,0:T(8,128)} fusion(bf16[192,10,34,128]{3,0,2,1:T(8,128)(2,1)S(1)} %pad_maximum_fusion, bf16[9,64,192]{1,2,0:T(8,128)(2,1)S(1)} %bitcast.108), kind=kOutput, calls=%fused_computation.18 | convolution fusion | flops 805306368 | bytes 21020672 | tf_op jit(solution)/shard_map/oi,ixyz->oxyz/dot_general | solution.py:30
  254.5 4.7 %fusion.13 = f32[8,32,128,64]{2,3,1,0:T(8,128)} fusion(bf16[192,10,34,128]{3,0,2,1:T(8,128)(2,1)S(1)} %pad_maximum_fusion, bf16[9,64,192]{1,2,0:T(8,128)(2,1)S(1)} %bitcast.109), kind=kOutput, calls=%fused_computation.20 | convolution fusion | flops 805306368 | bytes 21020672 | tf_op jit(solution)/shard_map/oi,ixyz->oxyz/dot_general | solution.py:30
  259.2 4.7 %fusion.15 = f32[8,32,128,64]{2,3,1,0:T(8,128)} fusion(bf16[192,10,34,128]{3,0,2,1:T(8,128)(2,1)S(1)} %pad_maximum_fusion, bf16[9,64,192]{1,2,0:T(8,128)(2,1)S(1)} %bitcast.110), kind=kOutput, calls=%fused_computation.22 | convolution fusion | flops 805306368 | bytes 21020672 | tf_op jit(solution)/shard_map/oi,ixyz->oxyz/dot_general | solution.py:30
  263.9 4.7 %fusion.17 = f32[8,32,128,64]{2,3,1,0:T(8,128)} fusion(bf16[192,10,34,128]{3,0,2,1:T(8,128)(2,1)S(1)} %pad_maximum_fusion, bf16[9,64,192]{1,2,0:T(8,128)(2,1)S(1)} %bitcast.111), kind=kOutput, calls=%fused_computation.24 | convolution fusion | flops 805306368 | bytes 21020672 | tf_op jit(solution)/shard_map/oi,ixyz->oxyz/dot_general | solution.py:30
  268.5 0.0 copy-done
  268.5 4.7 %fusion.19 = f32[8,32,128,64]{2,3,1,0:T(8,128)} fusion(bf16[192,10,34,128]{3,0,2,1:T(8,128)(2,1)S(1)} %pad_maximum_fusion, bf16[9,64,192]{1,2,0:T(8,128)(2,1)S(1)} %bitcast.112), kind=kOutput, calls=%fused_computation.26 | convolution fusion | flops 805306368 | bytes 21020672 | tf_op jit(solution)/shard_map/oi,ixyz->oxyz/dot_general | solution.py:30
  273.2 0.0 copy-done.5
  273.2 25.9 %maximum_bitcast_fusion = f32[64,8,32,128]{3,0,2,1:T(8,128)S(1)} fusion(f32[8,32,128,64]{2,3,1,0:T(8,128)} %fusion.5, f32[8,32,128,64]{2,3,1,0:T(8,128)} %fusion.7, f32[8,32,128,64]{2,3,1,0:T(8,128)} %fusion.9, f32[8,32,128,64]{2,3,1,0:T(8,128)} %fusion.11, f32[8,32,128,64]{2,3,1,0:T(8,128)} %fusion.13, f32[8,32,128,64]{2,3,1,0:T(8,128)} %fusion.15, ...), kind=kOutput, calls=%fused_computation.51 | convolution fusion | flops 826277888 | bytes 88130048 | tf_op jit(solution)/shard_map/oi,ixyz->oxyz/dot_general | solution.py:30
  299.1 1.9 collective-permute-start.4
  301.1 3.6 collective-permute-start.5
  304.7 2.1 collective-permute-done.4
  306.8 1.8 collective-permute-done.5
  308.6 0.1 pad_maximum_fusion.9
  308.7 3.6 collective-permute-start.7
  312.4 0.0 copy-start.4
  312.4 2.3 collective-permute-start.6
  314.7 22.4 %collective-permute-done.7 = f32[64,1,34,128]{3,0,2,1:T(8,128)S(1)} collective-permute-done((f32[64,1,34,128]{3,0,2,1:T(8,128)S(1)}, f32[64,1,34,128]{3,0,2,1:T(8,128)S(1)}, u32[]{:S(2)}, u32[]{:S(2)}) %collective-permute-start.7) | collective-permute-done | bytes 1114144 | tf_op jit(solution)/shard_map/ppermute | solution.py:14
  337.2 6.2 %collective-permute-done.6 = f32[64,1,34,128]{3,0,2,1:T(8,128)S(1)} collective-permute-done((f32[64,1,34,128]{3,0,2,1:T(8,128)S(1)}, f32[64,1,34,128]{3,0,2,1:T(8,128)S(1)}, u32[]{:S(2)}, u32[]{:S(2)}) %collective-permute-start.6) | collective-permute-done | bytes 1114144 | tf_op jit(solution)/shard_map/ppermute | solution.py:15
  343.4 13.8 %select_maximum_fusion = f32[64,10,34,130]{3,0,2,1:T(8,128)} fusion(f32[64,1,34,128]{3,0,2,1:T(8,128)S(1)} %collective-permute-done.6, f32[64,1,34,128]{3,0,2,1:T(8,128)S(1)} %collective-permute-done.7, f32[64,8,1,128]{3,0,2,1:T(8,128)S(1)} %collective-permute-done.5, f32[64,8,32,128]{3,0,2,1:T(8,128)S(1)} %maximum_bitcast_fusion, ...), kind=kLoop, calls=%fused_computation.2 | loop fusion | flops 33945600 | bytes 22456320 | tf_op jit(solution)/shard_map/concatenate | solution.py:16
  357.2 0.0 copy-done.4
  357.2 11.6 %fusion.25 = bf16[64,8,32,128]{3,0,2,1:T(8,128)(2,1)S(1)} fusion(f32[64,8,32,128]{3,0,2,1:T(8,128)S(1)} %maximum_bitcast_fusion, f32[64,10,34,130]{3,0,2,1:T(8,128)} %select_maximum_fusion, f32[64,8,1,128]{3,0,2,1:T(8,128)S(1)} %collective-permute-done.4, f32[64,8,1,128]{3,0,2,1:T(8,128)S(1)} %collective-permute-done.5, ...), kind=kLoop, calls=%fused_computation.36 | loop fusion | flops 37748736 | bytes 32243712 | tf_op jit(solution)/shard_map/convert_element_type | solution.py:97
  368.8 4.7 %copy.43 = bf16[64,8,32,128]{3,2,1,0:T(8,128)(2,1)} copy(bf16[64,8,32,128]{3,0,2,1:T(8,128)(2,1)S(1)} %fusion.25) | data formatting | bytes 8388608 | tf_op jit(solution)/shard_map/convert_element_type | solution.py:97
  (6 shorter events, 0.1 us)
Async XLA Ops:
  2.3 24.0 %all-to-all-start.1 = ((bf16[128,1,64]{2,1,0:T(2,128)(2,1)}), bf16[128,1,64]{2,1,0:T(2,128)(2,1)S(1)}, u32[]{:S(2)}, u32[]{:S(2)}) async-start(bf16[128,1,64]{2,1,0:T(2,128)(2,1)} %and_convert_fusion), calls=%async_computation.1 | async-start | bytes 131072 | tf_op jit(solution)/shard_map/all_to_all | solution.py:88
  26.3 111.6 %all-to-all-start = ((bf16[128,64,512]{2,1,0:T(8,128)(2,1)}), bf16[128,64,512]{2,1,0:T(8,128)(2,1)}, u32[]{:S(2)}, u32[]{:S(2)}) async-start(bf16[128,64,512]{2,1,0:T(8,128)(2,1)} %fusion.31), calls=%async_computation | async-start | bytes 16777216 | tf_op jit(solution)/shard_map/all_to_all | solution.py:87
  160.8 34.8 %copy-start.3 = (bf16[3,3,3,64,64]{4,3,2,1,0:T(8,128)(2,1)S(1)}, bf16[3,3,3,64,64]{4,3,2,1,0:T(8,128)(2,1)}, u32[]{:S(2)}) copy-start(bf16[3,3,3,64,64]{4,3,2,1,0:T(8,128)(2,1)} %param.13) | copy-start | bytes 663556
  162.9 15.8 %collective-permute-start = (bf16[64,8,1,128]{3,0,2,1:T(8,128)(2,1)S(1)}, bf16[64,8,1,128]{3,0,2,1:T(8,128)(2,1)S(1)}, u32[]{:S(2)}, u32[]{:S(2)}) collective-permute-start(bf16[64,8,1,128]{3,0,2,1:T(8,128)(2,1)S(1)} %copy.73), channel_id=1, source_target_pairs={{0,16},{16,32},{32,48},{48,64},{64,80},{80,96},{96,112},{1,17},{17... | collective-permute-start | bytes 393224 | tf_op jit(solution)/shard_map/ppermute | solution.py:14
  164.9 19.0 %collective-permute-start.1 = (bf16[64,8,1,128]{3,0,2,1:T(8,128)(2,1)S(1)}, bf16[64,8,1,128]{3,0,2,1:T(8,128)(2,1)S(1)}, u32[]{:S(2)}, u32[]{:S(2)}) collective-permute-start(bf16[64,8,1,128]{3,0,2,1:T(8,128)(2,1)S(1)} %copy.74), channel_id=1, source_target_pairs={{16,0},{32,16},{48,32},{64,48},{80,64},{96,80},{112,96},{17,1},{33... | collective-permute-start | bytes 393224 | tf_op jit(solution)/shard_map/ppermute | solution.py:15
  183.9 2.1 copy-start.1
  186.1 19.1 %collective-permute-start.2 = (bf16[64,1,34,128]{3,0,2,1:T(8,128)(2,1)S(1)}, bf16[64,1,34,128]{3,0,2,1:T(8,128)(2,1)S(1)}, u32[]{:S(2)}, u32[]{:S(2)}) collective-permute-start(bf16[64,1,34,128]{3,0,2,1:T(8,128)(2,1)S(1)} %get-tuple-element.11), channel_id=1, source_target_pairs={{0,1},{1,2},{2,3},{3,4},{4,5},{5,6},{6,7},{7,8},{8,9},{9,10},{10,1... | collective-permute-start | bytes 1671176 | tf_op jit(solution)/shard_map/ppermute | solution.py:14
  188.0 19.4 %collective-permute-start.3 = (bf16[64,1,34,128]{3,0,2,1:T(8,128)(2,1)S(1)}, bf16[64,1,34,128]{3,0,2,1:T(8,128)(2,1)S(1)}, u32[]{:S(2)}, u32[]{:S(2)}) collective-permute-start(bf16[64,1,34,128]{3,0,2,1:T(8,128)(2,1)S(1)} %get-tuple-element.12), channel_id=1, source_target_pairs={{1,0},{2,1},{3,2},{4,3},{5,4},{6,5},{7,6},{8,7},{9,8},{10,9},{11,1... | collective-permute-start | bytes 1671176 | tf_op jit(solution)/shard_map/ppermute | solution.py:15
  207.5 17.4 %slice-start = ((s8[4456448]{0:T(1024)(128)(4,1)}), s8[4194304]{0:T(1024)(128)(4,1)S(1)}, s32[]{:S(2)}) async-start(s8[4456448]{0:T(1024)(128)(4,1)} %bitcast.102), calls=%async_computation.2 | async-start | bytes 8388608
  218.9 6.0 %slice-start.1 = ((s8[4456448]{0:T(1024)(128)(4,1)}), s8[262144]{0:T(1024)(128)(4,1)S(1)}, s32[]{:S(2)}) async-start(s8[4456448]{0:T(1024)(128)(4,1)} %bitcast.102), calls=%async_computation.3 | async-start | bytes 524288
  234.3 34.2 %copy-start = (bf16[192,10,34,128]{3,0,2,1:T(8,128)(2,1)}, bf16[192,10,34,128]{3,0,2,1:T(8,128)(2,1)S(1)}, u32[]{:S(2)}) copy-start(bf16[192,10,34,128]{3,0,2,1:T(8,128)(2,1)S(1)} %pad_maximum_fusion) | copy-start | bytes 50135044
  234.3 6.3 %copy-start.2 = (bf16[3,3,64,3,64]{2,4,3,1,0:T(8,128)(2,1)S(1)}, bf16[3,3,64,3,64]{2,4,3,1,0:T(8,128)(2,1)}, u32[]{:S(2)}) copy-start(bf16[3,3,64,3,64]{2,4,3,1,0:T(8,128)(2,1)} %copy.33) | copy-start | bytes 663556
  268.5 4.7 %copy-start.5 = (f32[64]{0:T(128)S(1)}, f32[64]{0:T(128)}, u32[]{:S(2)}) copy-start(f32[64]{0:T(128)} %param.14) | copy-start | bytes 772
  299.1 7.7 %collective-permute-start.4 = (f32[64,8,1,128]{3,0,2,1:T(8,128)S(1)}, f32[64,8,1,128]{3,0,2,1:T(8,128)S(1)}, u32[]{:S(2)}, u32[]{:S(2)}) collective-permute-start(f32[64,8,1,128]{3,0,2,1:T(8,128)S(1)} %get-tuple-element.9), channel_id=1, source_target_pairs={{0,16},{16,32},{32,48},{48,64},{64,80},{80,96},{96,112},{1,17},{17... | collective-permute-start | bytes 786440 | tf_op jit(solution)/shard_map/ppermute | solution.py:14
  301.1 7.5 %collective-permute-start.5 = (f32[64,8,1,128]{3,0,2,1:T(8,128)S(1)}, f32[64,8,1,128]{3,0,2,1:T(8,128)S(1)}, u32[]{:S(2)}, u32[]{:S(2)}) collective-permute-start(f32[64,8,1,128]{3,0,2,1:T(8,128)S(1)} %get-tuple-element.10), channel_id=1, source_target_pairs={{16,0},{32,16},{48,32},{64,48},{80,64},{96,80},{112,96},{17,1},{33... | collective-permute-start | bytes 786440 | tf_op jit(solution)/shard_map/ppermute | solution.py:15
  308.7 28.4 %collective-permute-start.7 = (f32[64,1,34,128]{3,0,2,1:T(8,128)S(1)}, f32[64,1,34,128]{3,0,2,1:T(8,128)S(1)}, u32[]{:S(2)}, u32[]{:S(2)}) collective-permute-start(f32[64,1,34,128]{3,0,2,1:T(8,128)S(1)} %get-tuple-element.7), channel_id=1, source_target_pairs={{0,1},{1,2},{2,3},{3,4},{4,5},{5,6},{6,7},{7,8},{8,9},{9,10},{10,1... | collective-permute-start | bytes 3342344 | tf_op jit(solution)/shard_map/ppermute | solution.py:14
  312.4 44.8 %copy-start.4 = (f32[8,32,128]{2,1,0:T(8,128)S(1)}, f32[8,32,128]{2,1,0:T(8,128)}, u32[]{:S(2)}) copy-start(f32[8,32,128]{2,1,0:T(8,128)} %param.15) | copy-start | bytes 393220
  312.4 31.0 %collective-permute-start.6 = (f32[64,1,34,128]{3,0,2,1:T(8,128)S(1)}, f32[64,1,34,128]{3,0,2,1:T(8,128)S(1)}, u32[]{:S(2)}, u32[]{:S(2)}) collective-permute-start(f32[64,1,34,128]{3,0,2,1:T(8,128)S(1)} %get-tuple-element.8), channel_id=1, source_target_pairs={{1,0},{2,1},{3,2},{4,3},{5,4},{6,5},{7,6},{8,7},{9,8},{10,9},{11,1... | collective-permute-start | bytes 3342344 | tf_op jit(solution)/shard_map/ppermute | solution.py:15
where the time goes:
time: 379 us; the launch traced here: 374 us
  waiting for transfers between devices  144 us (38%)
  matrix products  93.3 us (25%)
  starting transfers between devices  57.7 us (15%)
  other arithmetic  48.1 us (13%)
  local copies, waits for them, and re-layouts  29.4 us (8%)
    all_to_all x1, waiting for transfers between devices, on_device(): lax.all_to_all(partial_value, ('views', 'bricks'), split_axis=0, concat_a...  101 us
    dot_general x9, matrix products, convolve(): jnp.einsum('oi,ixyz->oxyz', weights[shift_x * 3 + shift_y], window, prefe...  64.8 us
    ppermute x4, waiting for transfers between devices, padded_2(): before = lax.ppermute(last, axis, up)  33.2 us
    ppermute x4, starting transfers between devices, padded_2(): after = lax.ppermute(first, axis, down)  27.3 us
    concatenate x3, other arithmetic, padded_2(): array = jnp.concatenate([before, array, after], axis=dim)  25.4 us
    dot_general x1, matrix products, on_device(): jnp.einsum('sb,scv->cbv', got_target, got_part, preferred_element_type=jn...  15.3 us
    convert_element_type x1, other arithmetic, on_device(): return smooth(beside_all, smooth_coef).astype(jnp.bfloat16)  11.6 us
    dot_general x1, matrix products, on_device(): jnp.einsum('dcp,dpv->dcv', chosen, tiles, preferred_element_type=jnp.floa...  11.5 us
  transfers between devices with their start and end apart: 10, of which 7 were waited for; matrix products, arithmetic and copies ran while one was open for 5% of the time, Pallas kernels for 0%

commit v1 on v0

v1 whole, which is shorter than its diff:
```python
import functools

import jax
import jax.numpy as jnp
from jax import lax
from jax.experimental import pallas as pl
from jax.experimental.pallas import tpu as pltpu
from jax.sharding import PartitionSpec as P

C = 64
PIX = 128
Z = 128
BX = 8
BY = 32
BLK = 64
VOXB = 512
ROW = BY * Z
WIDE = (BY + 4) * Z
GATED = (BY + 2) * Z
SEND = 8


def lift_kernel(tgt_ref, part_ref, main_ref, lo_ref, hi_ref, ylo_ref, yhi_ref, acc):
    step = pl.program_id(0)

    @pl.when(step == 0)
    def _():
        acc[...] = jnp.zeros_like(acc)

    for i in range(SEND):
        block = tgt_ref[step * SEND + i]

        @pl.when(block < BLK)
        def _():
            acc[block] = acc[block] + part_ref[i].astype(jnp.float32)

    @pl.when(step == pl.num_programs(0) - 1)
    def _():
        def plane(x, carry):
            for yb in range(BY // 4):
                v = jnp.maximum(acc[x * (BY // 4) + yb], 0.0).astype(jnp.bfloat16)
                main_ref[x, :, yb * VOXB : (yb + 1) * VOXB] = v
                if yb == 0:
                    ylo_ref[x] = v[:, : 2 * Z]
                if yb == BY // 4 - 1:
                    yhi_ref[x] = v[:, 2 * Z :]
            return carry

        lax.fori_loop(0, BX, plane, 0)
        lo_ref[...] = main_ref[0:2]
        hi_ref[...] = main_ref[BX - 2 : BX]


def lift(tgt, part):
    n = part.shape[0]
    whole = lambda *shape: pl.BlockSpec(shape, lambda i, t: (0,) * len(shape))
    return pl.pallas_call(
        lift_kernel,
        grid_spec=pltpu.PrefetchScalarGridSpec(
            num_scalar_prefetch=1,
            grid=(n // SEND,),
            in_specs=[pl.BlockSpec((SEND, C, VOXB), lambda i, t: (i, 0, 0))],
            out_specs=[
                whole(BX, C, ROW),
                whole(2, C, ROW),
                whole(2, C, ROW),
                whole(BX, C, 2 * Z),
                whole(BX, C, 2 * Z),
            ],
            scratch_shapes=[pltpu.VMEM((BLK, C, VOXB), jnp.float32)],
        ),
        out_shape=[
            jax.ShapeDtypeStruct((BX, C, ROW), jnp.bfloat16),
            jax.ShapeDtypeStruct((2, C, ROW), jnp.bfloat16),
            jax.ShapeDtypeStruct((2, C, ROW), jnp.bfloat16),
            jax.ShapeDtypeStruct((BX, C, 2 * Z), jnp.bfloat16),
            jax.ShapeDtypeStruct((BX, C, 2 * Z), jnp.bfloat16),
        ],
        compiler_params=pltpu.CompilerParams(vmem_limit_bytes=48 << 20),
        name="lift",
    )(tgt, part)


def conv_kernel(
    flags_ref,
    w_ref,
    bias_ref,
    coef_ref,
    main_ref,
    xlo_ref,
    xhi_ref,
    ylo_ref,
    yhi_ref,
    clo_ref,
    chi_ref,
    out_ref,
    xs,
    acc_a,
    acc_b,
    gated,
    flat,
):
    step = pl.program_id(0)
    lane = lax.broadcasted_iota(jnp.int32, (C, Z), 1)
    first = lane == 0
    last = lane == Z - 1

    def stage(pieces):
        at = 0
        for ref, count in pieces:
            for y in range(count):
                v = ref[:, y * Z : (y + 1) * Z]
                f = v.astype(jnp.float32)
                below = jnp.where(first, 0.0, pltpu.roll(f, 1, 1)).astype(jnp.bfloat16)
                above = jnp.where(last, 0.0, pltpu.roll(f, Z - 1, 1)).astype(jnp.bfloat16)
                xs[0:C, at * Z : (at + 1) * Z] = below
                xs[C : 2 * C, at * Z : (at + 1) * Z] = v
                xs[2 * C : 3 * C, at * Z : (at + 1) * Z] = above
                at += 1

    @pl.when(step < 2)
    def _():
        stage([(clo_ref.at[0, 0], 2), (xlo_ref.at[0], BY), (clo_ref.at[1, 0], 2)])

    @pl.when((step >= 2) & (step < BX + 2))
    def _():
        stage([(ylo_ref.at[0], 2), (main_ref.at[0], BY), (yhi_ref.at[0], 2)])

    @pl.when(step >= BX + 2)
    def _():
        stage([(chi_ref.at[0, 0], 2), (xhi_ref.at[0], BY), (chi_ref.at[1, 0], 2)])

    slot = lax.rem(step, 3)
    keep = jnp.where(step == 2, flags_ref[0], jnp.where(step == BX + 3, flags_ref[1], 1.0))
    bias = jnp.broadcast_to(bias_ref[...], (C, 2 * Z))
    weights = w_ref[...]
    for t in range((BY + 2) // 2):
        cols = slice(t * 2 * Z, (t + 1) * 2 * Z)
        window = jnp.concatenate(
            [xs[:, (t * 2 + dy) * Z : (t * 2 + dy + 2) * Z] for dy in range(3)], axis=0
        )
        p = jnp.dot(weights, window, preferred_element_type=jnp.float32)
        done = acc_b[:, cols] + p[2 * C : 3 * C]
        g = jnp.maximum(done + bias, 0.0) * keep
        if t == 0:
            gated[slot, :, 0:Z] = g[:, :Z] * flags_ref[2]
            gated[slot, :, Z : 2 * Z] = g[:, Z:]
        elif t == BY // 2:
            gated[slot, :, BY * Z : (BY + 1) * Z] = g[:, :Z]
            gated[slot, :, (BY + 1) * Z : (BY + 2) * Z] = g[:, Z:] * flags_ref[3]
        else:
            gated[slot, :, cols] = g
        acc_b[:, cols] = acc_a[:, cols] + p[C : 2 * C]
        acc_a[:, cols] = p[0:C]

    @pl.when(step >= 4)
    def _():
        mid = lax.rem(step + 2, 3)
        old = lax.rem(step + 1, 3)
        for y in range(BY):
            here = slice((y + 1) * Z, (y + 2) * Z)
            g = gated[mid, :, here]
            beside = gated[slot, :, here] + gated[old, :, here]
            beside = beside + gated[mid, :, y * Z : (y + 1) * Z]
            beside = beside + gated[mid, :, (y + 2) * Z : (y + 3) * Z]
            beside = beside + jnp.where(first, 0.0, pltpu.roll(g, 1, 1))
            beside = beside + jnp.where(last, 0.0, pltpu.roll(g, Z - 1, 1))
            coef = jnp.broadcast_to(coef_ref[0, y : y + 1, :], (C, Z))
            flat[pl.ds(y, C, stride=BY), :] = g + coef * (beside - 6.0 * g)
        out_ref[:, 0] = flat[...].reshape(C, BY, Z).astype(jnp.bfloat16)


def conv_smooth(flags, weights, bias, coef, main, xlo, xhi, ylo, yhi, clo, chi):
    local = lambda i, f: (jnp.clip(i - 2, 0, BX - 1), 0, 0)
    low = lambda i, f: (jnp.minimum(i, 1), 0, 0)
    high = lambda i, f: (jnp.clip(i - BX - 2, 0, 1), 0, 0)
    done = lambda i: jnp.clip(i - 4, 0, BX - 1)
    return pl.pallas_call(
        conv_kernel,
        grid_spec=pltpu.PrefetchScalarGridSpec(
            num_scalar_prefetch=1,
            grid=(BX + 4,),
            in_specs=[
                pl.BlockSpec((3 * C, 9 * C), lambda i, f: (0, 0)),
                pl.BlockSpec((C, 1), lambda i, f: (0, 0)),
                pl.BlockSpec((1, BY, Z), lambda i, f: (done(i), 0, 0)),
                pl.BlockSpec((1, C, ROW), local),
                pl.BlockSpec((1, C, ROW), low),
                pl.BlockSpec((1, C, ROW), high),
                pl.BlockSpec((1, C, 2 * Z), local),
                pl.BlockSpec((1, C, 2 * Z), local),
                pl.BlockSpec((2, 1, C, 2 * Z), lambda i, f: (0, jnp.minimum(i, 1), 0, 0)),
                pl.BlockSpec((2, 1, C, 2 * Z), lambda i, f: (0, jnp.clip(i - BX - 2, 0, 1), 0, 0)),
            ],
            out_specs=pl.BlockSpec((C, 1, BY, Z), lambda i, f: (0, done(i), 0, 0)),
            scratch_shapes=[
                pltpu.VMEM((3 * C, WIDE), jnp.bfloat16),
                pltpu.VMEM((C, GATED), jnp.float32),
                pltpu.VMEM((C, GATED), jnp.float32),
                pltpu.VMEM((3, C, GATED), jnp.float32),
                pltpu.VMEM((C * BY, Z), jnp.float32),
            ],
        ),
        out_shape=jax.ShapeDtypeStruct((C, BX, BY, Z), jnp.bfloat16),
        compiler_params=pltpu.CompilerParams(vmem_limit_bytes=48 << 20),
        name="conv_smooth",
    )(flags, weights, bias, coef, main, xlo, xhi, ylo, yhi, clo, chi)


def shift(array, axis, by):
    size = lax.axis_size(axis)
    pairs = [(i, i + by) for i in range(size) if 0 <= i + by < size]
    return lax.ppermute(array, axis, pairs)


def on_device(
    tile_pixel, tile_voxel, tile_count, features, interp, conv_weight, conv_bias, smooth_coef
):
    feats = features[0, 0]
    tiles = interp[0, 0]
    pixel_ids = tile_pixel[0, 0]
    voxel_ids = tile_voxel[0, 0]
    count = tile_count[0, 0]
    slots_total = tiles.shape[0]
    n_bricks = lax.axis_size("bricks")
    n_views = lax.axis_size("views")
    brick = lax.axis_index("bricks")
    view = lax.axis_index("views")
    me = view * n_bricks + brick
    slot_ids = jnp.arange(slots_total, dtype=jnp.int32)
    live = jnp.remainder(slot_ids - jnp.remainder(me * 37, slots_total), slots_total) < count
    targets = lax.all_gather(
        jnp.where(live, voxel_ids, BLK), ("views", "bricks"), axis=0, tiled=False
    )
    tgt = lax.dynamic_slice_in_dim(targets.reshape(slots_total, slots_total), me, 1, axis=1)[:, 0]
    selector = (pixel_ids[:, None] == jnp.arange(feats.shape[0], dtype=jnp.int32)[None, :]).astype(
        jnp.bfloat16
    )
    chosen = jnp.einsum(
        "dk,kq->dq", selector, feats.reshape(feats.shape[0], C * PIX),
        preferred_element_type=jnp.float32,
    )
    chosen = chosen.astype(jnp.bfloat16).reshape(slots_total, C, PIX)
    partial_value = jnp.einsum(
        "dcp,dpv->dcv", chosen, tiles, preferred_element_type=jnp.float32
    ).astype(jnp.bfloat16)
    got = lax.all_to_all(partial_value, ("views", "bricks"), split_axis=0, concat_axis=0, tiled=True)
    main, lo, hi, ylo, yhi = lift(tgt, got)
    from_low = shift(yhi, "views", 1)
    from_high = shift(ylo, "views", -1)
    xlo = shift(hi, "bricks", 1)
    xhi = shift(lo, "bricks", -1)
    clo = shift(jnp.stack([from_low[BX - 2 :], from_high[BX - 2 :]]), "bricks", 1)
    chi = shift(jnp.stack([from_low[:2], from_high[:2]]), "bricks", -1)
    flags = jnp.stack(
        [brick > 0, brick < n_bricks - 1, view > 0, view < n_views - 1]
    ).astype(jnp.float32)
    weights = jnp.transpose(conv_weight, (0, 3, 1, 2, 4)).reshape(3 * C, 9 * C)
    return conv_smooth(
        flags, weights, conv_bias[:, None], smooth_coef, main, xlo, xhi, from_low, from_high, clo, chi
    )


def solution(mesh):
    in_specs = (
        P("views", "bricks", None),
        P("views", "bricks", None),
        P("views", "bricks"),
        P("views", "bricks", None, None, None),
        P("views", "bricks", None, None, None),
        P(),
        P(),
        P("bricks", "views", None),
    )
    out_specs = P(None, "bricks", "views", None)
    return jax.shard_map(
        on_device, mesh=mesh, in_specs=in_specs, out_specs=out_specs, check_vma=False
    )
```

time: 379 us -> 258 us (0.68)
  the two profiles are of different devices: /device:TPU:38 before, /device:TPU:9 now
where the time goes in v1:
time: 258 us; the launch traced here: 254 us
  blocking collectives  140 us (54%)
  Pallas kernels  51.4 us (20%)
  starting transfers between devices  28.9 us (11%)
  matrix products  13.2 us (5%)
  waiting for transfers between devices  12.1 us (5%)
  local copies, waits for them, and re-layouts  5.94 us (2%)
    all_gather x1, blocking collectives, on_device(): lax.all_gather(jnp.where(live, voxel_ids, BLK), ('views', 'bricks'), axis...  140 us
    pallas_call x1, Pallas kernels, conv_smooth(): pl.pallas_call(conv_kernel, grid_spec=pltpu.PrefetchScalarGridSpec(num_sc...  37.3 us
    ppermute x6, starting transfers between devices, shift(): return lax.ppermute(array, axis, pairs)  17.7 us
    pallas_call x1, Pallas kernels, lift(): pl.pallas_call(lift_kernel, grid_spec=pltpu.PrefetchScalarGridSpec(num_sc...  14.2 us
    ppermute x6, waiting for transfers between devices, shift(): return lax.ppermute(array, axis, pairs)  12.1 us
    dot_general x1, matrix products, on_device(): jnp.einsum('dcp,dpv->dcv', chosen, tiles, preferred_element_type=jnp.floa...  11.5 us
    all_to_all x1, starting transfers between devices, on_device(): lax.all_to_all(partial_value, ('views', 'bricks'), split_axis=0, concat_a...  11.2 us
  transfers between devices with their start and end apart: 7, of which 2 were waited for; matrix products, arithmetic and copies ran while one was open for 3% of the time, Pallas kernels for 0%

profile of v1, /device:TPU:9, one launch (start us, length us, event | category | flops | bytes accessed | tf_op | source)
XLA Modules:
  0.0 254.0 jit_solution(14690640585216568137)
XLA Ops:
  0.0 1.7 fusion.5
  1.7 0.6 copy.16
  2.3 11.5 %fusion.2 = bf16[128,64,512]{2,1,0:T(8,128)(2,1)} fusion(bf16[128,64,128]{2,1,0:T(8,128)(2,1)S(1)} %bitcast.37, bf16[1,1,128,128,512]{4,3,2,1,0:T(8,128)(2,1)} %param.12), kind=kOutput, calls=%fused_computation.3 | convolution fusion | flops 1077936128 | bytes 27262976 | tf_op jit(solution)/shard_map/dcp,dpv->dcv/dot_general | solution.py:244
  13.9 0.0 copy-start.3
  13.9 11.2 %all-to-all-start = ((bf16[128,64,512]{2,1,0:T(8,128)(2,1)}), bf16[128,64,512]{2,1,0:T(8,128)(2,1)}, u32[]{:S(2)}, u32[]{:S(2)}) async-start(bf16[128,64,512]{2,1,0:T(8,128)(2,1)} %fusion.2), calls=%async_computation | async-start | bytes 16777216 | tf_op jit(solution)/shard_map/all_to_all | solution.py:247
  25.7 0.0 copy-done.3
  25.8 140.1 %all-gather = s32[128,1,128]{2,1,0:T(1,128)S(1)} all-gather(s32[1,1,128]{2,1,0:T(1,128)S(1)} %fusion.10), channel_id=1, replica_groups=mesh['views'=8,'bricks'=16] {'views','bricks'}, dimensions={0}, use_global_device_ids=true | all-gather | bytes 66048 | tf_op jit(solution)/shard_map/all_gather | solution.py:232
  165.9 2.5 dynamic-slice_reduce_fusion.tgt_ref
  168.4 0.0 copy-start.1
  168.4 0.0 copy-start.2
  168.4 0.0 copy-start
  168.4 0.0 all-to-all-done.part_ref
  168.5 14.2 %lift.1 = (bf16[8,64,4096]{2,1,0:T(8,128)(2,1)}, bf16[2,64,4096]{2,1,0:T(8,128)(2,1)}, bf16[2,64,4096]{2,1,0:T(8,128)(2,1)}, bf16[8,64,256]{2,1,0:T(8,128)(2,1)S(1)}, bf16[8,64,256]{2,1,0:T(8,128)(2,1)S(1)}) custom-call(s32[128]{0:T(128)S(1)} %dynamic-slice_reduce_fusion.tgt_ref, bf16[128,64,512]{2,1,0:T(8,128)(2,1)} %all-to-all-done.part_ref), custom_call_target="tpu_custom_call" | custom-call | tf_op jit(solution)/shard_map/lift/pallas_call | solution.py:57
  182.6 1.9 collective-permute-start.2
  184.5 1.9 collective-permute-start
  186.5 5.5 %collective-permute-start.1 = (bf16[2,64,4096]{2,1,0:T(8,128)(2,1)}, bf16[2,64,4096]{2,1,0:T(8,128)(2,1)S(1)}, u32[]{:S(2)}, u32[]{:S(2)}) collective-permute-start(bf16[2,64,4096]{2,1,0:T(8,128)(2,1)} %get-tuple-element.12), channel_id=1, source_target_pairs={{1,0},{2,1},{3,2},{4,3},{5,4},{6,5},{7,6},{8,7},{9,8},{10,9},{11,1... | collective-permute-start | bytes 3145736 | tf_op jit(solution)/shard_map/ppermute | solution.py:213
  191.9 3.0 %collective-permute-start.3 = (bf16[8,64,256]{2,1,0:T(8,128)(2,1)S(1)}, bf16[8,64,256]{2,1,0:T(8,128)(2,1)S(1)}, u32[]{:S(2)}, u32[]{:S(2)}) collective-permute-start(bf16[8,64,256]{2,1,0:T(8,128)(2,1)S(1)} %get-tuple-element.14), channel_id=1, source_target_pairs={{16,0},{32,16},{48,32},{64,48},{80,64},{96,80},{112,96},{17,1},{33... | collective-permute-start | bytes 786440 | tf_op jit(solution)/shard_map/ppermute | solution.py:213
  194.9 0.0 collective-permute-done.2.ylo_ref
  195.0 5.0 %collective-permute-done.3.yhi_ref = bf16[8,64,256]{2,1,0:T(8,128)(2,1)S(1)} collective-permute-done((bf16[8,64,256]{2,1,0:T(8,128)(2,1)S(1)}, bf16[8,64,256]{2,1,0:T(8,128)(2,1)S(1)}, u32[]{:S(2)}, u32[]{:S(2)}) %collective-permute-start.3) | collective-permute-done | bytes 262176 | tf_op jit(solution)/shard_map/ppermute | solution.py:213
  199.9 0.7 pad_maximum_fusion.1
  200.6 3.1 %collective-permute-start.5 = (bf16[2,2,64,256]{3,2,1,0:T(8,128)(2,1)}, bf16[2,2,64,256]{3,2,1,0:T(8,128)(2,1)S(1)}, u32[]{:S(2)}, u32[]{:S(2)}) collective-permute-start(bf16[2,2,64,256]{3,2,1,0:T(8,128)(2,1)} %pad_maximum_fusion.1), channel_id=1, source_target_pairs={{1,0},{2,1},{3,2},{4,3},{5,4},{6,5},{7,6},{8,7},{9,8},{10,9},{11,1... | collective-permute-start | bytes 393224 | tf_op jit(solution)/shard_map/ppermute | solution.py:213
  203.7 0.7 pad_maximum_fusion
  204.4 2.3 collective-permute-start.4
  206.8 0.0 copy-done.1
  206.8 1.2 copy.13
  208.0 1.5 reshape.60.w_ref
  209.5 0.0 copy-done.2
  209.5 0.1 copy.14.bias_ref
  209.6 0.1 add_convert_fusion.flags_ref
  209.6 7.1 %collective-permute-done.5.chi_ref = bf16[2,2,64,256]{3,2,1,0:T(8,128)(2,1)S(1)} collective-permute-done((bf16[2,2,64,256]{3,2,1,0:T(8,128)(2,1)}, bf16[2,2,64,256]{3,2,1,0:T(8,128)(2,1)S(1)}, u32[]{:S(2)}, u32[]{:S(2)}) %collective-permute-start.5) | collective-permute-done | bytes 131104 | tf_op jit(solution)/shard_map/ppermute | solution.py:213
  216.7 0.0 collective-permute-done.4.clo_ref
  216.7 0.0 collective-permute-done.xlo_ref
  216.7 0.0 collective-permute-done.1.xhi_ref
  216.8 0.0 copy-done
  216.8 37.3 %conv_smooth.1 = bf16[64,8,32,128]{3,2,1,0:T(8,128)(2,1)} custom-call(f32[4]{0:T(128)S(1)} %add_convert_fusion.flags_ref, bf16[192,576]{1,0:T(8,128)(2,1)S(1)} %reshape.60.w_ref, f32[64,1]{1,0:T(8,128)S(1)} %copy.14.bias_ref, f32[8,32,128]{2,1,0:T(8,128)S(1)} %copy-done, bf16[8,64,4096]{2,1,0:T(8,128)(2,1)} %get-tuple-element.10.main_ref, ...), custom_call_target="tpu_custom_call" | custom-call | tf_op jit(solution)/shard_map/conv_smooth/pallas_call | solution.py:178
  (3 shorter events, 0.0 us)
Async XLA Ops:
  13.9 11.9 %copy-start.3 = (s32[1,1,128]{2,1,0:T(1,128)S(1)}, s32[1,1,128]{2,1,0:T(1,128)}, u32[]{:S(2)}) copy-start(s32[1,1,128]{2,1,0:T(1,128)} %param.9) | copy-start | bytes 1540
  13.9 154.6 %all-to-all-start = ((bf16[128,64,512]{2,1,0:T(8,128)(2,1)}), bf16[128,64,512]{2,1,0:T(8,128)(2,1)}, u32[]{:S(2)}, u32[]{:S(2)}) async-start(bf16[128,64,512]{2,1,0:T(8,128)(2,1)} %fusion.2), calls=%async_computation | async-start | bytes 16777216 | tf_op jit(solution)/shard_map/all_to_all | solution.py:247
  168.4 38.4 %copy-start.1 = (bf16[3,3,3,64,64]{4,3,2,1,0:T(8,128)(2,1)S(1)}, bf16[3,3,3,64,64]{4,3,2,1,0:T(8,128)(2,1)}, u32[]{:S(2)}) copy-start(bf16[3,3,3,64,64]{4,3,2,1,0:T(8,128)(2,1)} %param.13) | copy-start | bytes 663556
  168.4 41.0 %copy-start.2 = (f32[64]{0:T(128)S(1)}, f32[64]{0:T(128)}, u32[]{:S(2)}) copy-start(f32[64]{0:T(128)} %param.14) | copy-start | bytes 772
  168.4 48.3 %copy-start = (f32[8,32,128]{2,1,0:T(8,128)S(1)}, f32[8,32,128]{2,1,0:T(8,128)}, u32[]{:S(2)}) copy-start(f32[8,32,128]{2,1,0:T(8,128)} %coef_ref.1) | copy-start | bytes 393220
  182.6 12.3 %collective-permute-start.2 = (bf16[8,64,256]{2,1,0:T(8,128)(2,1)S(1)}, bf16[8,64,256]{2,1,0:T(8,128)(2,1)S(1)}, u32[]{:S(2)}, u32[]{:S(2)}) collective-permute-start(bf16[8,64,256]{2,1,0:T(8,128)(2,1)S(1)} %get-tuple-element.13), channel_id=1, source_target_pairs={{0,16},{16,32},{32,48},{48,64},{64,80},{80,96},{96,112},{1,17},{17... | collective-permute-start | bytes 786440 | tf_op jit(solution)/shard_map/ppermute | solution.py:213
  184.5 32.2 %collective-permute-start = (bf16[2,64,4096]{2,1,0:T(8,128)(2,1)}, bf16[2,64,4096]{2,1,0:T(8,128)(2,1)S(1)}, u32[]{:S(2)}, u32[]{:S(2)}) collective-permute-start(bf16[2,64,4096]{2,1,0:T(8,128)(2,1)} %get-tuple-element.11), channel_id=1, source_target_pairs={{0,1},{1,2},{2,3},{3,4},{4,5},{5,6},{6,7},{7,8},{8,9},{9,10},{10,1... | collective-permute-start | bytes 3145736 | tf_op jit(solution)/shard_map/ppermute | solution.py:213
  186.5 30.3 %collective-permute-start.1 = (bf16[2,64,4096]{2,1,0:T(8,128)(2,1)}, bf16[2,64,4096]{2,1,0:T(8,128)(2,1)S(1)}, u32[]{:S(2)}, u32[]{:S(2)}) collective-permute-start(bf16[2,64,4096]{2,1,0:T(8,128)(2,1)} %get-tuple-element.12), channel_id=1, source_target_pairs={{1,0},{2,1},{3,2},{4,3},{5,4},{6,5},{7,6},{8,7},{9,8},{10,9},{11,1... | collective-permute-start | bytes 3145736 | tf_op jit(solution)/shard_map/ppermute | solution.py:213
  191.9 8.0 %collective-permute-start.3 = (bf16[8,64,256]{2,1,0:T(8,128)(2,1)S(1)}, bf16[8,64,256]{2,1,0:T(8,128)(2,1)S(1)}, u32[]{:S(2)}, u32[]{:S(2)}) collective-permute-start(bf16[8,64,256]{2,1,0:T(8,128)(2,1)S(1)} %get-tuple-element.14), channel_id=1, source_target_pairs={{16,0},{32,16},{48,32},{64,48},{80,64},{96,80},{112,96},{17,1},{33... | collective-permute-start | bytes 786440 | tf_op jit(solution)/shard_map/ppermute | solution.py:213
  200.6 16.1 %collective-permute-start.5 = (bf16[2,2,64,256]{3,2,1,0:T(8,128)(2,1)}, bf16[2,2,64,256]{3,2,1,0:T(8,128)(2,1)S(1)}, u32[]{:S(2)}, u32[]{:S(2)}) collective-permute-start(bf16[2,2,64,256]{3,2,1,0:T(8,128)(2,1)} %pad_maximum_fusion.1), channel_id=1, source_target_pairs={{1,0},{2,1},{3,2},{4,3},{5,4},{6,5},{7,6},{8,7},{9,8},{10,9},{11,1... | collective-permute-start | bytes 393224 | tf_op jit(solution)/shard_map/ppermute | solution.py:213
  204.4 12.3 %collective-permute-start.4 = (bf16[2,2,64,256]{3,2,1,0:T(8,128)(2,1)}, bf16[2,2,64,256]{3,2,1,0:T(8,128)(2,1)S(1)}, u32[]{:S(2)}, u32[]{:S(2)}) collective-permute-start(bf16[2,2,64,256]{3,2,1,0:T(8,128)(2,1)} %pad_maximum_fusion), channel_id=1, source_target_pairs={{0,1},{1,2},{2,3},{3,4},{4,5},{5,6},{6,7},{7,8},{8,9},{9,10},{10,1... | collective-permute-start | bytes 393224 | tf_op jit(solution)/shard_map/ppermute | solution.py:213

commit v2 on v1

v2 whole, which is shorter than its diff:
```python
import functools

import jax
import jax.numpy as jnp
from jax import lax
from jax.experimental import pallas as pl
from jax.experimental.pallas import tpu as pltpu
from jax.sharding import PartitionSpec as P

C = 64
PIX = 128
Z = 128
BX = 8
BY = 32
BLK = 64
VOXB = 512
ROW = BY * Z
WIDE = (BY + 4) * Z
GATED = (BY + 2) * Z
SEND = 16
PITCH = 40


def lift_kernel(tgt_ref, part_ref, main_ref, lo_ref, hi_ref, ylo_ref, yhi_ref, part, acc, sems):
    chunks = part.shape[0] // SEND
    copies = []
    for k in range(chunks):
        rows = pl.ds(k * SEND, SEND)
        copies.append(pltpu.make_async_copy(part_ref.at[rows], part.at[rows], sems.at[k]))
        copies[-1].start()
    acc[...] = jnp.zeros_like(acc)
    for k in range(chunks):
        copies[k].wait()

        def add(i, carry):
            block = tgt_ref[i]
            acc[block] = acc[block] + part[i].astype(jnp.float32)
            return carry

        lax.fori_loop(k * SEND, (k + 1) * SEND, add, 0)

    def plane(x, carry):
        for yb in range(BY // 4):
            v = jnp.maximum(acc[x * (BY // 4) + yb], 0.0).astype(jnp.bfloat16)
            main_ref[x, :, yb * VOXB : (yb + 1) * VOXB] = v
            if yb == 0:
                ylo_ref[x] = v[:, : 2 * Z]
            if yb == BY // 4 - 1:
                yhi_ref[x] = v[:, 2 * Z :]
        return carry

    lax.fori_loop(0, BX, plane, 0)
    lo_ref[...] = main_ref[0:2]
    hi_ref[...] = main_ref[BX - 2 : BX]


def lift(tgt, part):
    n = part.shape[0]
    vmem = pl.BlockSpec(memory_space=pltpu.VMEM)
    return pl.pallas_call(
        lift_kernel,
        in_specs=[pl.BlockSpec(memory_space=pltpu.SMEM), pl.BlockSpec(memory_space=pl.ANY)],
        out_specs=[vmem] * 5,
        scratch_shapes=[
            pltpu.VMEM((n, C, VOXB), jnp.bfloat16),
            pltpu.VMEM((BLK + 1, C, VOXB), jnp.float32),
            pltpu.SemaphoreType.DMA((n // SEND,)),
        ],
        out_shape=[
            jax.ShapeDtypeStruct((BX, C, ROW), jnp.bfloat16),
            jax.ShapeDtypeStruct((2, C, ROW), jnp.bfloat16),
            jax.ShapeDtypeStruct((2, C, ROW), jnp.bfloat16),
            jax.ShapeDtypeStruct((BX, C, 2 * Z), jnp.bfloat16),
            jax.ShapeDtypeStruct((BX, C, 2 * Z), jnp.bfloat16),
        ],
        compiler_params=pltpu.CompilerParams(vmem_limit_bytes=48 << 20),
        name="lift",
    )(tgt, part)


def conv_kernel(
    flags_ref,
    w_ref,
    bias_ref,
    coef_ref,
    main_ref,
    xlo_ref,
    xhi_ref,
    ylo_ref,
    yhi_ref,
    clo_ref,
    chi_ref,
    out_ref,
    raw,
    xs_a,
    xs_b,
    acc_a,
    acc_b,
    prev,
    pend,
    flat_a,
    flat_b,
    sems,
):
    step = pl.program_id(0)
    lane = lax.broadcasted_iota(jnp.int32, (C, Z), 1)
    first = lane == 0
    last = lane == Z - 1

    def copies(p):
        if p < 2:
            left, mid, right = clo_ref.at[0, p], xlo_ref.at[p], clo_ref.at[1, p]
        elif p < BX + 2:
            left, mid, right = ylo_ref.at[p - 2], main_ref.at[p - 2], yhi_ref.at[p - 2]
        else:
            q = p - BX - 2
            left, mid, right = chi_ref.at[0, q], xhi_ref.at[q], chi_ref.at[1, q]
        to = raw.at[p]
        return [
            pltpu.make_async_copy(left, to.at[:, 0 : 2 * Z], sems.at[p, 0]),
            pltpu.make_async_copy(mid, to.at[:, 2 * Z : 2 * Z + ROW], sems.at[p, 1]),
            pltpu.make_async_copy(right, to.at[:, 2 * Z + ROW : WIDE], sems.at[p, 2]),
        ]

    def stage(p, xs, y):
        cols = slice(y * Z, (y + 1) * Z)
        v = raw[p, :, cols]
        f = v.astype(jnp.float32)
        xs[0:C, cols] = jnp.where(first, 0.0, pltpu.roll(f, 1, 1)).astype(jnp.bfloat16)
        xs[C : 2 * C, cols] = v
        xs[2 * C : 3 * C, cols] = jnp.where(last, 0.0, pltpu.roll(f, Z - 1, 1)).astype(jnp.bfloat16)

    @pl.when(step == 0)
    def _():
        for p in range(BX + 4):
            for copy in copies(p):
                copy.start()
        for copy in copies(0):
            copy.wait()
        for y in range(BY + 4):
            stage(0, xs_a, y)

    for p in range(1, BX + 4):

        @pl.when(step == (0 if p < 3 else (p - 1) // 2))
        def _():
            for copy in copies(p):
                copy.wait()

    bias = jnp.broadcast_to(bias_ref[...], (C, 2 * Z))
    weights = w_ref[...]

    def half(plane, xs, xs_next, flat, to):
        following = jnp.minimum(plane + 1, BX + 3)
        keep = jnp.where(plane == 2, flags_ref[0], jnp.where(plane == BX + 3, flags_ref[1], 1.0))
        x_out = jnp.clip(plane - 4, 0, BX - 1)
        x_new = jnp.clip(plane - 3, 0, BX - 1)
        before = None
        for t in range((BY + 2) // 2):
            for y in range(2 * t, 2 * t + 2 if t < BY // 2 else BY + 4):
                stage(following, xs_next, y)
            cols = slice(t * 2 * Z, (t + 1) * 2 * Z)
            window = jnp.concatenate(
                [xs[:, (t * 2 + dy) * Z : (t * 2 + dy + 2) * Z] for dy in range(3)], axis=0
            )
            p = jnp.dot(weights, window, preferred_element_type=jnp.float32)
            g = jnp.maximum(acc_b[:, cols] + p[2 * C : 3 * C] + bias, 0.0) * keep
            acc_b[:, cols] = acc_a[:, cols] + p[C : 2 * C]
            acc_a[:, cols] = p[0:C]
            rows = [g[:, :Z], g[:, Z:]]
            if t == 0:
                rows[0] = rows[0] * flags_ref[2]
            if t == BY // 2:
                rows[1] = rows[1] * flags_ref[3]
            if t > 0:
                window4 = before + rows
                for k in range(2):
                    y = 2 * t - 2 + k
                    here = slice(y * Z, (y + 1) * Z)
                    low, mid, high = window4[k], window4[k + 1], window4[k + 2]
                    beside = prev[:, here] + low + high
                    beside = beside + jnp.where(first, 0.0, pltpu.roll(mid, 1, 1))
                    beside = beside + jnp.where(last, 0.0, pltpu.roll(mid, Z - 1, 1))
                    flat[pl.ds(y, C, stride=PITCH), :] = (
                        pend[:, here] + coef_ref[x_out, y : y + 1, :] * mid
                    )
                    pend[:, here] = mid + coef_ref[x_new, y : y + 1, :] * (beside - 6.0 * mid)
                    prev[:, here] = mid
            before = rows
        out_ref[:, to] = flat[...].reshape(C, PITCH, Z)[:, :BY].astype(jnp.bfloat16)

    half(2 * step, xs_a, xs_b, flat_a, 0)
    half(2 * step + 1, xs_b, xs_a, flat_b, 1)


def conv_smooth(flags, weights, bias, coef, main, xlo, xhi, ylo, yhi, clo, chi):
    hbm = pl.BlockSpec(memory_space=pl.ANY)
    return pl.pallas_call(
        conv_kernel,
        grid=((BX + 4) // 2,),
        in_specs=[
            pl.BlockSpec(memory_space=pltpu.SMEM),
            pl.BlockSpec((3 * C, 9 * C), lambda i: (0, 0)),
            pl.BlockSpec((C, 1), lambda i: (0, 0)),
            pl.BlockSpec((BX, BY, Z), lambda i: (0, 0, 0)),
        ]
        + [hbm] * 7,
        out_specs=pl.BlockSpec((C, 2, BY, Z), lambda i: (0, jnp.maximum(i - 2, 0), 0, 0)),
        scratch_shapes=[
            pltpu.VMEM((BX + 4, C, WIDE), jnp.bfloat16),
            pltpu.VMEM((3 * C, WIDE), jnp.bfloat16),
            pltpu.VMEM((3 * C, WIDE), jnp.bfloat16),
            pltpu.VMEM((C, GATED), jnp.float32),
            pltpu.VMEM((C, GATED), jnp.float32),
            pltpu.VMEM((C, ROW), jnp.float32),
            pltpu.VMEM((C, ROW), jnp.float32),
            pltpu.VMEM((C * PITCH, Z), jnp.float32),
            pltpu.VMEM((C * PITCH, Z), jnp.float32),
            pltpu.SemaphoreType.DMA((BX + 4, 3)),
        ],
        out_shape=jax.ShapeDtypeStruct((C, BX, BY, Z), jnp.bfloat16),
        compiler_params=pltpu.CompilerParams(vmem_limit_bytes=56 << 20),
        name="conv_smooth",
    )(flags, weights, bias, coef, main, xlo, xhi, ylo, yhi, clo, chi)


def shift(array, axis, by):
    size = lax.axis_size(axis)
    pairs = [(i, i + by) for i in range(size) if 0 <= i + by < size]
    return lax.ppermute(array, axis, pairs)


def on_device(
    tile_pixel, tile_voxel, tile_count, features, interp, conv_weight, conv_bias, smooth_coef
):
    feats = features[0, 0]
    tiles = interp[0, 0]
    pixel_ids = tile_pixel[0, 0]
    voxel_ids = tile_voxel[0, 0]
    count = tile_count[0, 0]
    slots_total = tiles.shape[0]
    n_bricks = lax.axis_size("bricks")
    n_views = lax.axis_size("views")
    brick = lax.axis_index("bricks")
    view = lax.axis_index("views")
    me = view * n_bricks + brick
    slot_ids = jnp.arange(slots_total, dtype=jnp.int32)
    live = jnp.remainder(slot_ids - jnp.remainder(me * 37, slots_total), slots_total) < count
    mine = jnp.where(live, voxel_ids, BLK).astype(jnp.float32)
    table = lax.psum(
        jnp.where(slot_ids[:, None] == me, mine[None, :], 0.0), ("views", "bricks")
    )
    tgt = lax.dynamic_slice_in_dim(table, me, 1, axis=1)[:, 0].astype(jnp.int32)
    selector = (pixel_ids[:, None] == jnp.arange(feats.shape[0], dtype=jnp.int32)[None, :]).astype(
        jnp.bfloat16
    )
    chosen = jnp.einsum(
        "dk,kq->dq", selector, feats.reshape(feats.shape[0], C * PIX),
        preferred_element_type=jnp.float32,
    )
    chosen = chosen.astype(jnp.bfloat16).reshape(slots_total, C, PIX)
    partial_value = jnp.einsum(
        "dcp,dpv->dcv", chosen, tiles, preferred_element_type=jnp.float32
    ).astype(jnp.bfloat16)
    got = lax.all_to_all(partial_value, ("views", "bricks"), split_axis=0, concat_axis=0, tiled=True)
    main, lo, hi, ylo, yhi = lift(tgt, got)
    from_low = shift(yhi, "views", 1)
    from_high = shift(ylo, "views", -1)
    xlo = shift(hi, "bricks", 1)
    xhi = shift(lo, "bricks", -1)
    clo = shift(jnp.stack([from_low[BX - 2 :], from_high[BX - 2 :]]), "bricks", 1)
    chi = shift(jnp.stack([from_low[:2], from_high[:2]]), "bricks", -1)
    flags = jnp.stack(
        [brick > 0, brick < n_bricks - 1, view > 0, view < n_views - 1]
    ).astype(jnp.float32)
    weights = jnp.transpose(conv_weight, (0, 3, 1, 2, 4)).reshape(3 * C, 9 * C)
    return conv_smooth(
        flags, weights, conv_bias[:, None], smooth_coef, main, xlo, xhi, from_low, from_high, clo, chi
    )


def solution(mesh):
    in_specs = (
        P("views", "bricks", None),
        P("views", "bricks", None),
        P("views", "bricks"),
        P("views", "bricks", None, None, None),
        P("views", "bricks", None, None, None),
        P(),
        P(),
        P("bricks", "views", None),
    )
    out_specs = P(None, "bricks", "views", None)
    return jax.shard_map(
        on_device, mesh=mesh, in_specs=in_specs, out_specs=out_specs, check_vma=False
    )
```

time: 258 us -> 313 us (1.21)
  waiting for transfers between devices: 12.1 us -> 214 us
  blocking collectives: 140 us -> 0 us
  Pallas kernels: 51.4 us -> 31.9 us
  between operations: 0.85 us -> 14.3 us
    psum x0 -> x1, waiting for transfers between devices: none -> 202 us  [on_device(): lax.psum(jnp.where(slot_ids[:, None] == me, mine[None, :], 0.0), ('views'...]
    all_gather x1 -> x0, blocking collectives: 140 us -> none  [on_device(): lax.all_gather(jnp.where(live, voxel_ids, BLK), ('views', 'bricks'), axis...]
    pallas_call x2, Pallas kernels: 51.4 us -> 31.9 us  [the longest x1 25.2 us: conv_smooth(): pl.pallas_call(conv_kernel, grid=((BX + 4) // 2,), in_specs=[pl.BlockSpec...]
  transfers between devices with their start and end apart: 7 -> 8, of which waited for: 2 -> 3; matrix products, arithmetic and copies ran while one was open for 3% -> 2% of each run, Pallas kernels for 0% -> 0%
where the time goes in v2:
time: 313 us; the launch traced here: 310 us
  waiting for transfers between devices  214 us (68%)
  Pallas kernels  31.9 us (10%)
  starting transfers between devices  28.8 us (9%)
  between operations  14.3 us (5%)
  matrix products  13.2 us (4%)
  local copies, waits for them, and re-layouts  4.55 us (1%)
  other arithmetic  3.46 us (1%)
    psum x1, waiting for transfers between devices, on_device(): lax.psum(jnp.where(slot_ids[:, None] == me, mine[None, :], 0.0), ('views'...  202 us
    pallas_call x1, Pallas kernels, conv_smooth(): pl.pallas_call(conv_kernel, grid=((BX + 4) // 2,), in_specs=[pl.BlockSpec...  25.2 us
    ppermute x6, starting transfers between devices, shift(): return lax.ppermute(array, axis, pairs)  17.5 us
    ppermute x6, waiting for transfers between devices, shift(): return lax.ppermute(array, axis, pairs)  12.1 us
    dot_general x1, matrix products, on_device(): jnp.einsum('dcp,dpv->dcv', chosen, tiles, preferred_element_type=jnp.floa...  11.5 us
    all_to_all x1, starting transfers between devices, on_device(): lax.all_to_all(partial_value, ('views', 'bricks'), split_axis=0, concat_a...  11.2 us
    pallas_call x1, Pallas kernels, lift(): pl.pallas_call(lift_kernel, in_specs=[pl.BlockSpec(memory_space=pltpu.SME...  6.72 us
  transfers between devices with their start and end apart: 8, of which 3 were waited for; matrix products, arithmetic and copies ran while one was open for 2% of the time, Pallas kernels for 0%

profile of v2, /device:TPU:9, one launch (start us, length us, event | category | flops | bytes accessed | tf_op | source)
XLA Modules:
  0.0 310.3 jit_solution(8273704816844858759)
XLA Ops:
  6.5 1.7 fusion.5
  8.3 0.6 copy.14
  8.9 11.5 %fusion.2 = bf16[128,64,512]{2,1,0:T(8,128)(2,1)} fusion(bf16[128,64,128]{2,1,0:T(8,128)(2,1)S(1)} %bitcast.37, bf16[1,1,128,128,512]{4,3,2,1,0:T(8,128)(2,1)} %param.12), kind=kOutput, calls=%fused_computation.3 | convolution fusion | flops 1077936128 | bytes 27262976 | tf_op jit(solution)/shard_map/dcp,dpv->dcv/dot_general | solution.py:262
  20.4 0.0 copy-start.5
  20.4 11.2 %all-to-all-start = ((bf16[128,64,512]{2,1,0:T(8,128)(2,1)}), bf16[128,64,512]{2,1,0:T(8,128)(2,1)}, u32[]{:S(2)}, u32[]{:S(2)}) async-start(bf16[128,64,512]{2,1,0:T(8,128)(2,1)} %fusion.2), calls=%async_computation | async-start | bytes 16777216 | tf_op jit(solution)/shard_map/all_to_all | solution.py:265
  31.6 0.0 all-reduce.2.cloned.1.call-start
  32.4 0.0 copy-done.5
  32.4 0.7 broadcast_select_fusion
  33.1 0.0 all-reduce.2.cloned.1.call-update
  33.1 202.0 %all-reduce.2.cloned.1.call-done = f32[128,128]{0,1:T(8,128)} async-done(((f32[128,128]{0,1:T(8,128)}), f32[128,128]{0,1:T(8,128)}) %all-reduce.2.cloned.1.call-update) | async-done | bytes 65552 | tf_op jit(solution)/shard_map/psum | solution.py:250
  235.1 0.7 convert_bitcast_fusion.tgt_ref
  235.8 0.0 copy-start.4
  235.8 0.0 all-to-all-done.part_ref
  235.8 6.7 %lift.1 = (bf16[8,64,4096]{2,1,0:T(8,128)(2,1)}, bf16[2,64,4096]{2,1,0:T(8,128)(2,1)S(1)}, bf16[2,64,4096]{2,1,0:T(8,128)(2,1)S(1)}, bf16[8,64,256]{2,1,0:T(8,128)(2,1)S(1)}, bf16[8,64,256]{2,1,0:T(8,128)(2,1)S(1)}) custom-call(s32[128]{0:T(128)S(1)} %convert_bitcast_fusion.tgt_ref, bf16[128,64,512]{2,1,0:T(8,128)(2,1)} %all-to-all-done.part_ref), custom_call_target="tpu_custom_call" | custom-call | tf_op jit(solution)/shard_map/lift/pallas_call | solution.py:60
  242.5 2.4 collective-permute-start.2
  245.0 1.9 collective-permute-start
  246.9 5.5 %collective-permute-start.1 = (bf16[2,64,4096]{2,1,0:T(8,128)(2,1)S(1)}, bf16[2,64,4096]{2,1,0:T(8,128)(2,1)}, u32[]{:S(2)}, u32[]{:S(2)}) collective-permute-start(bf16[2,64,4096]{2,1,0:T(8,128)(2,1)S(1)} %get-tuple-element.12), channel_id=1, source_target_pairs={{1,0},{2,1},{3,2},{4,3},{5,4},{6,5},{7,6},{8,7},{9,8},{10,9},{11,1... | collective-permute-start | bytes 3145736 | tf_op jit(solution)/shard_map/ppermute | solution.py:230
  252.4 2.5 collective-permute-start.3
  254.8 0.0 collective-permute-done.2.ylo_ref
  254.9 0.0 copy-start
  254.9 5.6 %collective-permute-done.3.yhi_ref = bf16[8,64,256]{2,1,0:T(8,128)(2,1)S(1)} collective-permute-done((bf16[8,64,256]{2,1,0:T(8,128)(2,1)S(1)}, bf16[8,64,256]{2,1,0:T(8,128)(2,1)S(1)}, u32[]{:S(2)}, u32[]{:S(2)}) %collective-permute-start.3) | collective-permute-done | bytes 262176 | tf_op jit(solution)/shard_map/ppermute | solution.py:230
  260.5 0.0 copy-start.1
  260.5 0.7 pad_maximum_fusion.1
  261.2 1.9 collective-permute-start.5
  263.1 0.7 pad_maximum_fusion
  263.8 3.3 %collective-permute-start.4 = (bf16[2,2,64,256]{3,2,1,0:T(8,128)(2,1)}, bf16[2,2,64,256]{3,2,1,0:T(8,128)(2,1)S(1)}, u32[]{:S(2)}, u32[]{:S(2)}) collective-permute-start(bf16[2,2,64,256]{3,2,1,0:T(8,128)(2,1)} %pad_maximum_fusion), channel_id=1, source_target_pairs={{0,1},{1,2},{2,3},{3,4},{4,5},{5,6},{6,7},{7,8},{8,9},{9,10},{10,1... | collective-permute-start | bytes 393224 | tf_op jit(solution)/shard_map/ppermute | solution.py:230
  267.2 1.4 copy.11
  268.6 1.1 reshape.35.w_ref
  269.7 0.0 copy-done.4
  269.7 0.7 copy.12.bias_ref
  270.4 0.7 add_convert_fusion.flags_ref
  271.1 6.5 %collective-permute-done.5.chi_ref = bf16[2,2,64,256]{3,2,1,0:T(8,128)(2,1)S(1)} collective-permute-done((bf16[2,2,64,256]{3,2,1,0:T(8,128)(2,1)}, bf16[2,2,64,256]{3,2,1,0:T(8,128)(2,1)S(1)}, u32[]{:S(2)}, u32[]{:S(2)}) %collective-permute-start.5) | collective-permute-done | bytes 131104 | tf_op jit(solution)/shard_map/ppermute | solution.py:230
  277.6 0.0 copy-start.2
  277.6 0.0 collective-permute-done.4.clo_ref
  277.6 0.0 copy-start.3
  277.6 0.0 collective-permute-done.xlo_ref
  277.6 0.0 collective-permute-done.1.xhi_ref
  277.6 0.0 copy-done
  277.6 0.0 copy-done.1
  277.6 0.6 copy-done.2
  278.2 0.1 copy-done.3
  278.3 25.2 %conv_smooth.1 = bf16[64,8,32,128]{3,2,1,0:T(8,128)(2,1)} custom-call(f32[4]{0:T(128)} %add_convert_fusion.flags_ref, bf16[192,576]{1,0:T(8,128)(2,1)} %reshape.35.w_ref, f32[64,1]{1,0:T(8,128)} %copy.12.bias_ref, f32[8,32,128]{2,1,0:T(8,128)} %coef_ref.1, bf16[8,64,4096]{2,1,0:T(8,128)(2,1)} %get-tuple-element.10.main_ref, ...), custom_call_target="tpu_custom_call" | custom-call | tf_op jit(solution)/shard_map/conv_smooth/pallas_call | solution.py:198
  (4 shorter events, 0.0 us)
Async XLA Ops:
  20.4 12.0 %copy-start.5 = (s32[1,1,128]{2,1,0:T(1,128)S(1)}, s32[1,1,128]{2,1,0:T(1,128)}, u32[]{:S(2)}) copy-start(s32[1,1,128]{2,1,0:T(1,128)} %param.9) | copy-start | bytes 1540
  20.4 215.4 %all-to-all-start = ((bf16[128,64,512]{2,1,0:T(8,128)(2,1)}), bf16[128,64,512]{2,1,0:T(8,128)(2,1)}, u32[]{:S(2)}, u32[]{:S(2)}) async-start(bf16[128,64,512]{2,1,0:T(8,128)(2,1)} %fusion.2), calls=%async_computation | async-start | bytes 16777216 | tf_op jit(solution)/shard_map/all_to_all | solution.py:265
  31.6 203.5 %all-reduce.2.cloned.1.call-start = ((), (), s32[]{:S(2)}) async-start(), calls=%async_computation.1 | async-start | bytes 131072 | tf_op jit(solution)/shard_map/psum | solution.py:250
  235.8 33.9 %copy-start.4 = (f32[64]{0:T(128)S(1)}, f32[64]{0:T(128)}, u32[]{:S(2)}) copy-start(f32[64]{0:T(128)} %param.14) | copy-start | bytes 772
  242.5 12.3 %collective-permute-start.2 = (bf16[8,64,256]{2,1,0:T(8,128)(2,1)S(1)}, bf16[8,64,256]{2,1,0:T(8,128)(2,1)S(1)}, u32[]{:S(2)}, u32[]{:S(2)}) collective-permute-start(bf16[8,64,256]{2,1,0:T(8,128)(2,1)S(1)} %get-tuple-element.13), channel_id=1, source_target_pairs={{0,16},{16,32},{32,48},{48,64},{64,80},{80,96},{96,112},{1,17},{17... | collective-permute-start | bytes 786440 | tf_op jit(solution)/shard_map/ppermute | solution.py:230
  245.0 32.6 %collective-permute-start = (bf16[2,64,4096]{2,1,0:T(8,128)(2,1)S(1)}, bf16[2,64,4096]{2,1,0:T(8,128)(2,1)}, u32[]{:S(2)}, u32[]{:S(2)}) collective-permute-start(bf16[2,64,4096]{2,1,0:T(8,128)(2,1)S(1)} %get-tuple-element.11), channel_id=1, source_target_pairs={{0,1},{1,2},{2,3},{3,4},{4,5},{5,6},{6,7},{7,8},{8,9},{9,10},{10,1... | collective-permute-start | bytes 3145736 | tf_op jit(solution)/shard_map/ppermute | solution.py:230
  246.9 30.7 %collective-permute-start.1 = (bf16[2,64,4096]{2,1,0:T(8,128)(2,1)S(1)}, bf16[2,64,4096]{2,1,0:T(8,128)(2,1)}, u32[]{:S(2)}, u32[]{:S(2)}) collective-permute-start(bf16[2,64,4096]{2,1,0:T(8,128)(2,1)S(1)} %get-tuple-element.12), channel_id=1, source_target_pairs={{1,0},{2,1},{3,2},{4,3},{5,4},{6,5},{7,6},{8,7},{9,8},{10,9},{11,1... | collective-permute-start | bytes 3145736 | tf_op jit(solution)/shard_map/ppermute | solution.py:230
  252.4 8.1 %collective-permute-start.3 = (bf16[8,64,256]{2,1,0:T(8,128)(2,1)S(1)}, bf16[8,64,256]{2,1,0:T(8,128)(2,1)S(1)}, u32[]{:S(2)}, u32[]{:S(2)}) collective-permute-start(bf16[8,64,256]{2,1,0:T(8,128)(2,1)S(1)} %get-tuple-element.14), channel_id=1, source_target_pairs={{16,0},{32,16},{48,32},{64,48},{80,64},{96,80},{112,96},{17,1},{33... | collective-permute-start | bytes 786440 | tf_op jit(solution)/shard_map/ppermute | solution.py:230
  254.9 22.7 %copy-start = (bf16[8,64,256]{2,1,0:T(8,128)(2,1)}, bf16[8,64,256]{2,1,0:T(8,128)(2,1)S(1)}, u32[]{:S(2)}) copy-start(bf16[8,64,256]{2,1,0:T(8,128)(2,1)S(1)} %collective-permute-done.2.ylo_ref) | copy-start | bytes 786436
  260.5 17.1 %copy-start.1 = (bf16[8,64,256]{2,1,0:T(8,128)(2,1)}, bf16[8,64,256]{2,1,0:T(8,128)(2,1)S(1)}, u32[]{:S(2)}) copy-start(bf16[8,64,256]{2,1,0:T(8,128)(2,1)S(1)} %collective-permute-done.3.yhi_ref) | copy-start | bytes 786436
  261.2 16.4 %collective-permute-start.5 = (bf16[2,2,64,256]{3,2,1,0:T(8,128)(2,1)}, bf16[2,2,64,256]{3,2,1,0:T(8,128)(2,1)S(1)}, u32[]{:S(2)}, u32[]{:S(2)}) collective-permute-start(bf16[2,2,64,256]{3,2,1,0:T(8,128)(2,1)} %pad_maximum_fusion.1), channel_id=1, source_target_pairs={{1,0},{2,1},{3,2},{4,3},{5,4},{6,5},{7,6},{8,7},{9,8},{10,9},{11,1... | collective-permute-start | bytes 393224 | tf_op jit(solution)/shard_map/ppermute | solution.py:230
  263.8 13.8 %collective-permute-start.4 = (bf16[2,2,64,256]{3,2,1,0:T(8,128)(2,1)}, bf16[2,2,64,256]{3,2,1,0:T(8,128)(2,1)S(1)}, u32[]{:S(2)}, u32[]{:S(2)}) collective-permute-start(bf16[2,2,64,256]{3,2,1,0:T(8,128)(2,1)} %pad_maximum_fusion), channel_id=1, source_target_pairs={{0,1},{1,2},{2,3},{3,4},{4,5},{5,6},{6,7},{7,8},{8,9},{9,10},{10,1... | collective-permute-start | bytes 393224 | tf_op jit(solution)/shard_map/ppermute | solution.py:230
  277.6 0.6 copy-start.2
  277.6 0.7 copy-start.3
Sparse Core Ops, SparseCore 0:
  37.2 197.8 all-reduce.1

commit v3 on v2

--- a/solution.py
+++ b/solution.py
@@ -18,35 +18,82 @@
 WIDE = (BY + 4) * Z
 GATED = (BY + 2) * Z
 SEND = 16
+PACK = 4 * C + 8
 PITCH = 40
 
 
-def lift_kernel(tgt_ref, part_ref, main_ref, lo_ref, hi_ref, ylo_ref, yhi_ref, part, acc, sems):
-    chunks = part.shape[0] // SEND
-    copies = []
+def partial_kernel(pixel_ref, tgt_ref, feats_ref, tiles_ref, out_ref, tiles, out, sems, done):
+    chunks = tiles.shape[0] // SEND
+
+    def load(k):
+        rows = pl.ds(pl.multiple_of(k * SEND, SEND), SEND)
+        return pltpu.make_async_copy(tiles_ref.at[rows], tiles.at[rows], sems.at[k])
+
+    def store(k):
+        rows = pl.ds(pl.multiple_of(k * SEND, SEND), SEND)
+        return pltpu.make_async_copy(out.at[rows], out_ref.at[rows], done.at[k])
+
     for k in range(chunks):
-        rows = pl.ds(k * SEND, SEND)
-        copies.append(pltpu.make_async_copy(part_ref.at[rows], part.at[rows], sems.at[k]))
-        copies[-1].start()
+        load(k).start()
+
+    def chunk(k, carry):
+        load(k).wait()
+        for i in range(SEND):
+            slot = k * SEND + i
+            p = jnp.dot(
+                feats_ref[pixel_ref[slot]], tiles[slot], preferred_element_type=jnp.float32
+            )
+            for q in range(4):
+                out[slot, q * C : (q + 1) * C, :] = p[:, q * Z : (q + 1) * Z].astype(jnp.bfloat16)
+            block = jnp.full((PACK - 4 * C, Z), tgt_ref[slot].astype(jnp.float32), jnp.float32)
+            out[slot, 4 * C : PACK, :] = block.astype(jnp.bfloat16)
+        store(k).start()
+        return carry
+
+    lax.fori_loop(0, chunks, chunk, 0)
+    for k in range(chunks):
+        store(k).wait()
+
+
+def partials(pixel_ids, targets, feats, tiles):
+    n = tiles.shape[0]
+    smem = pl.BlockSpec(memory_space=pltpu.SMEM)
+    hbm = pl.BlockSpec(memory_space=pl.ANY)
+    return pl.pallas_call(
+        partial_kernel,
+        in_specs=[smem, smem, pl.BlockSpec(memory_space=pltpu.VMEM), hbm],
+        out_specs=hbm,
+        scratch_shapes=[
+            pltpu.VMEM((n, PIX, VOXB), jnp.bfloat16),
+            pltpu.VMEM((n, PACK, Z), jnp.bfloat16),
+            pltpu.SemaphoreType.DMA((n // SEND,)),
+            pltpu.SemaphoreType.DMA((n // SEND,)),
+        ],
+        out_shape=jax.ShapeDtypeStruct((n, PACK, Z), jnp.bfloat16),
+        compiler_params=pltpu.CompilerParams(vmem_limit_bytes=48 << 20),
+        name="partials",
+    )(pixel_ids, targets, feats, tiles)
+
+
+def lift_kernel(tgt_ref, part_ref, main_ref, lo_ref, hi_ref, ylo_ref, yhi_ref, acc):
     acc[...] = jnp.zeros_like(acc)
-    for k in range(chunks):
-        copies[k].wait()
-
-        def add(i, carry):
-            block = tgt_ref[i]
-            acc[block] = acc[block] + part[i].astype(jnp.float32)
-            return carry
-
-        lax.fori_loop(k * SEND, (k + 1) * SEND, add, 0)
+
+    def add(i, carry):
+        block = tgt_ref[i]
+        acc[block] = acc[block] + part_ref[i, : 4 * C].astype(jnp.float32)
+        return carry
+
+    lax.fori_loop(0, part_ref.shape[0], add, 0)
 
     def plane(x, carry):
-        for yb in range(BY // 4):
-            v = jnp.maximum(acc[x * (BY // 4) + yb], 0.0).astype(jnp.bfloat16)
-            main_ref[x, :, yb * VOXB : (yb + 1) * VOXB] = v
-            if yb == 0:
-                ylo_ref[x] = v[:, : 2 * Z]
-            if yb == BY // 4 - 1:
-                yhi_ref[x] = v[:, 2 * Z :]
+        for y in range(BY):
+            v = acc[x * (BY // 4) + y // 4, (y % 4) * C : (y % 4 + 1) * C, :]
+            v = jnp.maximum(v, 0.0).astype(jnp.bfloat16)
+            main_ref[x, :, y * Z : (y + 1) * Z] = v
+            if y < 2:
+                ylo_ref[x, :, y * Z : (y + 1) * Z] = v
+            if y >= BY - 2:
+                yhi_ref[x, :, (y - BY + 2) * Z : (y - BY + 3) * Z] = v
         return carry
 
     lax.fori_loop(0, BX, plane, 0)
@@ -59,12 +106,10 @@
     vmem = pl.BlockSpec(memory_space=pltpu.VMEM)
     return pl.pallas_call(
         lift_kernel,
-        in_specs=[pl.BlockSpec(memory_space=pltpu.SMEM), pl.BlockSpec(memory_space=pl.ANY)],
+        in_specs=[pl.BlockSpec(memory_space=pltpu.SMEM), vmem],
         out_specs=[vmem] * 5,
         scratch_shapes=[
-            pltpu.VMEM((n, C, VOXB), jnp.bfloat16),
-            pltpu.VMEM((BLK + 1, C, VOXB), jnp.float32),
-            pltpu.SemaphoreType.DMA((n // SEND,)),
+            pltpu.VMEM((BLK + 1, 4 * C, Z), jnp.float32),
         ],
         out_shape=[
             jax.ShapeDtypeStruct((BX, C, ROW), jnp.bfloat16),
@@ -246,23 +291,10 @@
     me = view * n_bricks + brick
     slot_ids = jnp.arange(slots_total, dtype=jnp.int32)
     live = jnp.remainder(slot_ids - jnp.remainder(me * 37, slots_total), slots_total) < count
-    mine = jnp.where(live, voxel_ids, BLK).astype(jnp.float32)
-    table = lax.psum(
-        jnp.where(slot_ids[:, None] == me, mine[None, :], 0.0), ("views", "bricks")
-    )
-    tgt = lax.dynamic_slice_in_dim(table, me, 1, axis=1)[:, 0].astype(jnp.int32)
-    selector = (pixel_ids[:, None] == jnp.arange(feats.shape[0], dtype=jnp.int32)[None, :]).astype(
-        jnp.bfloat16
-    )
-    chosen = jnp.einsum(
-        "dk,kq->dq", selector, feats.reshape(feats.shape[0], C * PIX),
-        preferred_element_type=jnp.float32,
-    )
-    chosen = chosen.astype(jnp.bfloat16).reshape(slots_total, C, PIX)
-    partial_value = jnp.einsum(
-        "dcp,dpv->dcv", chosen, tiles, preferred_element_type=jnp.float32
-    ).astype(jnp.bfloat16)
-    got = lax.all_to_all(partial_value, ("views", "bricks"), split_axis=0, concat_axis=0, tiled=True)
+    targets = jnp.where(live, voxel_ids, BLK)
+    packed = partials(pixel_ids, targets, feats, tiles)
+    got = lax.all_to_all(packed, ("views", "bricks"), split_axis=0, concat_axis=0, tiled=True)
+    tgt = got[:, 4 * C, 0].astype(jnp.int32)
     main, lo, hi, ylo, yhi = lift(tgt, got)
     from_low = shift(yhi, "views", 1)
     from_high = shift(ylo, "views", -1)

time: 313 us -> 201 us (0.64)
  waiting for transfers between devices: 214 us -> 13.4 us
  blocking collectives: 0 us -> 111 us
  between operations: 14.3 us -> 0.8 us
  matrix products: 13.2 us -> 0 us
  Pallas kernels: 31.9 us -> 44.4 us
  starting transfers between devices: 28.8 us -> 17.7 us
    psum x1 -> x0, waiting for transfers between devices: 202 us -> none  [on_device(): lax.psum(jnp.where(slot_ids[:, None] == me, mine[None, :], 0.0), ('views'...]
    all_to_all x0 -> x1, blocking collectives: none -> 111 us  [on_device(): lax.all_to_all(packed, ('views', 'bricks'), split_axis=0, concat_axis=0,...]
    dot_general x2 -> x0, matrix products: 13.2 us -> none  [the longest x1 11.5 us: on_device(): jnp.einsum('dcp,dpv->dcv', chosen, tiles, preferred_element_type=jnp.floa...]
    all_to_all x1 -> x0, starting transfers between devices: 11.2 us -> none  [on_device(): lax.all_to_all(partial_value, ('views', 'bricks'), split_axis=0, concat_a...]
    pallas_call x0 -> x1, Pallas kernels: none -> 10.4 us  [partials(): pl.pallas_call(partial_kernel, in_specs=[smem, smem, pl.BlockSpec(memory_...]
  transfers between devices with their start and end apart: 8 -> 6, of which waited for: 3 -> 2; matrix products, arithmetic and copies ran while one was open for 2% -> 3% of each run, Pallas kernels for 0% -> 0%
where the time goes in v3:
time: 201 us; the launch traced here: 199 us
  blocking collectives  111 us (55%)
  Pallas kernels  44.4 us (22%)
  starting transfers between devices  17.7 us (9%)
  waiting for transfers between devices  13.4 us (7%)
  local copies, waits for them, and re-layouts  6.52 us (3%)
  other arithmetic  4.99 us (2%)
    all_to_all x1, blocking collectives, on_device(): lax.all_to_all(packed, ('views', 'bricks'), split_axis=0, concat_axis=0,...  111 us
    pallas_call x1, Pallas kernels, conv_smooth(): pl.pallas_call(conv_kernel, grid=((BX + 4) // 2,), in_specs=[pl.BlockSpec...  25.2 us
    ppermute x6, starting transfers between devices, shift(): return lax.ppermute(array, axis, pairs)  17.7 us
    ppermute x6, waiting for transfers between devices, shift(): return lax.ppermute(array, axis, pairs)  13.4 us
    pallas_call x1, Pallas kernels, partials(): pl.pallas_call(partial_kernel, in_specs=[smem, smem, pl.BlockSpec(memory_...  10.4 us
    pallas_call x1, Pallas kernels, lift(): pl.pallas_call(lift_kernel, in_specs=[pl.BlockSpec(memory_space=pltpu.SME...  8.78 us
  transfers between devices with their start and end apart: 6, of which 2 were waited for; matrix products, arithmetic and copies ran while one was open for 3% of the time, Pallas kernels for 0%

profile of v3, /device:TPU:9, one launch (start us, length us, event | category | flops | bytes accessed | tf_op | source)
XLA Modules:
  0.0 198.5 jit_solution(16092331400833792210)
XLA Ops:
  0.7 0.7 compare_select_fusion.2.tgt_ref
  1.3 0.0 copy-start
  1.3 0.9 copy-done
  2.3 0.0 copy-start.1
  2.3 0.7 copy-done.1
  2.9 10.4 %partials.1 = bf16[128,264,128]{2,1,0:T(8,128)(2,1)} custom-call(s32[128]{0:T(128)S(1)} %bitcast.22, s32[128]{0:T(128)S(1)} %compare_select_fusion.2.tgt_ref, bf16[16,64,128]{2,1,0:T(8,128)(2,1)S(1)} %bitcast.21, bf16[128,128,512]{2,1,0:T(8,128)(2,1)} %bitcast.23), custom_call_target="tpu_custom_call" | custom-call | tf_op jit(solution)/shard_map/partials/pallas_call | solution.py:62
  13.3 110.8 %all_to_all.5.part_ref = bf16[128,264,128]{2,1,0:T(8,128)(2,1)S(1)} all-to-all(bf16[128,264,128]{2,1,0:T(8,128)(2,1)} %partials.1), channel_id=1, replica_groups=mesh['views'=8,'bricks'=16] {'views','bricks'}, dimensions={0} | all-to-all | bytes 17301504 | tf_op jit(solution)/shard_map/all_to_all | solution.py:296
  124.2 0.0 copy-start.2
  124.2 0.0 copy-start.7
  124.2 2.4 %fusion.tgt_ref = s32[128]{0:T(128)S(1)} fusion(bf16[128,264,128]{2,1,0:T(8,128)(2,1)S(1)} %all_to_all.5.part_ref), kind=kLoop, calls=%fused_computation.7 | loop fusion | flops 128 | bytes 768 | tf_op jit(solution)/shard_map/convert_element_type | solution.py:297
  126.5 1.0 copy-done.2
  127.5 8.8 %lift.1 = (bf16[8,64,4096]{2,1,0:T(8,128)(2,1)}, bf16[2,64,4096]{2,1,0:T(8,128)(2,1)S(1)}, bf16[2,64,4096]{2,1,0:T(8,128)(2,1)S(1)}, bf16[8,64,256]{2,1,0:T(8,128)(2,1)S(1)}, bf16[8,64,256]{2,1,0:T(8,128)(2,1)S(1)}) custom-call(s32[128]{0:T(128)S(1)} %fusion.tgt_ref, bf16[128,264,128]{2,1,0:T(8,128)(2,1)} %copy-done.2), custom_call_target="tpu_custom_call" | custom-call | tf_op jit(solution)/shard_map/lift/pallas_call | solution.py:107
  136.3 3.1 %collective-permute-start.2 = (bf16[8,64,256]{2,1,0:T(8,128)(2,1)S(1)}, bf16[8,64,256]{2,1,0:T(8,128)(2,1)S(1)}, u32[]{:S(2)}, u32[]{:S(2)}) collective-permute-start(bf16[8,64,256]{2,1,0:T(8,128)(2,1)S(1)} %get-tuple-element.13), channel_id=1, source_target_pairs={{0,16},{16,32},{32,48},{48,64},{64,80},{80,96},{96,112},{1,17},{17... | collective-permute-start | bytes 786440 | tf_op jit(solution)/shard_map/ppermute | solution.py:275
  139.4 2.3 %collective-permute-start = (bf16[2,64,4096]{2,1,0:T(8,128)(2,1)S(1)}, bf16[2,64,4096]{2,1,0:T(8,128)(2,1)}, u32[]{:S(2)}, u32[]{:S(2)}) collective-permute-start(bf16[2,64,4096]{2,1,0:T(8,128)(2,1)S(1)} %get-tuple-element.11), channel_id=1, source_target_pairs={{0,1},{1,2},{2,3},{3,4},{4,5},{5,6},{6,7},{7,8},{8,9},{9,10},{10,1... | collective-permute-start | bytes 3145736 | tf_op jit(solution)/shard_map/ppermute | solution.py:275
  141.7 5.1 %collective-permute-start.1 = (bf16[2,64,4096]{2,1,0:T(8,128)(2,1)S(1)}, bf16[2,64,4096]{2,1,0:T(8,128)(2,1)}, u32[]{:S(2)}, u32[]{:S(2)}) collective-permute-start(bf16[2,64,4096]{2,1,0:T(8,128)(2,1)S(1)} %get-tuple-element.12), channel_id=1, source_target_pairs={{1,0},{2,1},{3,2},{4,3},{5,4},{6,5},{7,6},{8,7},{9,8},{10,9},{11,1... | collective-permute-start | bytes 3145736 | tf_op jit(solution)/shard_map/ppermute | solution.py:275
  146.8 1.9 collective-permute-start.3
  148.7 0.0 collective-permute-done.2.ylo_ref
  148.7 0.0 copy-start.3
  148.8 6.1 %collective-permute-done.3.yhi_ref = bf16[8,64,256]{2,1,0:T(8,128)(2,1)S(1)} collective-permute-done((bf16[8,64,256]{2,1,0:T(8,128)(2,1)S(1)}, bf16[8,64,256]{2,1,0:T(8,128)(2,1)S(1)}, u32[]{:S(2)}, u32[]{:S(2)}) %collective-permute-start.3) | collective-permute-done | bytes 262176 | tf_op jit(solution)/shard_map/ppermute | solution.py:275
  154.9 0.0 copy-start.4
  154.9 0.7 pad_maximum_fusion.1
  155.6 1.9 collective-permute-start.5
  157.5 0.7 pad_maximum_fusion
  158.2 3.3 %collective-permute-start.4 = (bf16[2,2,64,256]{3,2,1,0:T(8,128)(2,1)}, bf16[2,2,64,256]{3,2,1,0:T(8,128)(2,1)S(1)}, u32[]{:S(2)}, u32[]{:S(2)}) collective-permute-start(bf16[2,2,64,256]{3,2,1,0:T(8,128)(2,1)} %pad_maximum_fusion), channel_id=1, source_target_pairs={{0,1},{1,2},{2,3},{3,4},{4,5},{5,6},{6,7},{7,8},{8,9},{9,10},{10,1... | collective-permute-start | bytes 393224 | tf_op jit(solution)/shard_map/ppermute | solution.py:275
  161.6 1.4 copy.11
  163.0 1.1 reshape.5.w_ref
  164.1 0.0 copy-done.7
  164.1 0.7 copy.12.bias_ref
  164.8 0.6 add_convert_fusion.flags_ref
  165.4 7.2 %collective-permute-done.5.chi_ref = bf16[2,2,64,256]{3,2,1,0:T(8,128)(2,1)S(1)} collective-permute-done((bf16[2,2,64,256]{3,2,1,0:T(8,128)(2,1)}, bf16[2,2,64,256]{3,2,1,0:T(8,128)(2,1)S(1)}, u32[]{:S(2)}, u32[]{:S(2)}) %collective-permute-start.5) | collective-permute-done | bytes 131104 | tf_op jit(solution)/shard_map/ppermute | solution.py:275
  172.6 0.0 copy-start.5
  172.6 0.0 collective-permute-done.4.clo_ref
  172.6 0.0 copy-start.6
  172.6 0.0 collective-permute-done.xlo_ref
  172.6 0.0 collective-permute-done.1.xhi_ref
  172.6 0.0 copy-done.3
  172.7 0.0 copy-done.4
  172.7 0.6 copy-done.5
  173.3 0.1 copy-done.6
  173.3 25.2 %conv_smooth.1 = bf16[64,8,32,128]{3,2,1,0:T(8,128)(2,1)} custom-call(f32[4]{0:T(128)} %add_convert_fusion.flags_ref, bf16[192,576]{1,0:T(8,128)(2,1)} %reshape.5.w_ref, f32[64,1]{1,0:T(8,128)} %copy.12.bias_ref, f32[8,32,128]{2,1,0:T(8,128)} %coef_ref.1, bf16[8,64,4096]{2,1,0:T(8,128)(2,1)} %get-tuple-element.10.main_ref, ...), custom_call_target="tpu_custom_call" | custom-call | tf_op jit(solution)/shard_map/conv_smooth/pallas_call | solution.py:243
  (2 shorter events, 0.0 us)
Async XLA Ops:
  1.3 0.9 copy-start
  2.3 0.7 copy-start.1
  124.2 3.4 %copy-start.2 = (bf16[128,264,128]{2,1,0:T(8,128)(2,1)}, bf16[128,264,128]{2,1,0:T(8,128)(2,1)S(1)}, u32[]{:S(2)}) copy-start(bf16[128,264,128]{2,1,0:T(8,128)(2,1)S(1)} %all_to_all.5.part_ref) | copy-start | bytes 25952260
  124.2 39.9 %copy-start.7 = (f32[64]{0:T(128)S(1)}, f32[64]{0:T(128)}, u32[]{:S(2)}) copy-start(f32[64]{0:T(128)} %param.14) | copy-start | bytes 772
  136.3 12.5 %collective-permute-start.2 = (bf16[8,64,256]{2,1,0:T(8,128)(2,1)S(1)}, bf16[8,64,256]{2,1,0:T(8,128)(2,1)S(1)}, u32[]{:S(2)}, u32[]{:S(2)}) collective-permute-start(bf16[8,64,256]{2,1,0:T(8,128)(2,1)S(1)} %get-tuple-element.13), channel_id=1, source_target_pairs={{0,16},{16,32},{32,48},{48,64},{64,80},{80,96},{96,112},{1,17},{17... | collective-permute-start | bytes 786440 | tf_op jit(solution)/shard_map/ppermute | solution.py:275
  139.4 33.2 %collective-permute-start = (bf16[2,64,4096]{2,1,0:T(8,128)(2,1)S(1)}, bf16[2,64,4096]{2,1,0:T(8,128)(2,1)}, u32[]{:S(2)}, u32[]{:S(2)}) collective-permute-start(bf16[2,64,4096]{2,1,0:T(8,128)(2,1)S(1)} %get-tuple-element.11), channel_id=1, source_target_pairs={{0,1},{1,2},{2,3},{3,4},{4,5},{5,6},{6,7},{7,8},{8,9},{9,10},{10,1... | collective-permute-start | bytes 3145736 | tf_op jit(solution)/shard_map/ppermute | solution.py:275
  141.7 31.0 %collective-permute-start.1 = (bf16[2,64,4096]{2,1,0:T(8,128)(2,1)S(1)}, bf16[2,64,4096]{2,1,0:T(8,128)(2,1)}, u32[]{:S(2)}, u32[]{:S(2)}) collective-permute-start(bf16[2,64,4096]{2,1,0:T(8,128)(2,1)S(1)} %get-tuple-element.12), channel_id=1, source_target_pairs={{1,0},{2,1},{3,2},{4,3},{5,4},{6,5},{7,6},{8,7},{9,8},{10,9},{11,1... | collective-permute-start | bytes 3145736 | tf_op jit(solution)/shard_map/ppermute | solution.py:275
  146.8 8.1 %collective-permute-start.3 = (bf16[8,64,256]{2,1,0:T(8,128)(2,1)S(1)}, bf16[8,64,256]{2,1,0:T(8,128)(2,1)S(1)}, u32[]{:S(2)}, u32[]{:S(2)}) collective-permute-start(bf16[8,64,256]{2,1,0:T(8,128)(2,1)S(1)} %get-tuple-element.14), channel_id=1, source_target_pairs={{16,0},{32,16},{48,32},{64,48},{80,64},{96,80},{112,96},{17,1},{33... | collective-permute-start | bytes 786440 | tf_op jit(solution)/shard_map/ppermute | solution.py:275
  148.7 23.9 %copy-start.3 = (bf16[8,64,256]{2,1,0:T(8,128)(2,1)}, bf16[8,64,256]{2,1,0:T(8,128)(2,1)S(1)}, u32[]{:S(2)}) copy-start(bf16[8,64,256]{2,1,0:T(8,128)(2,1)S(1)} %collective-permute-done.2.ylo_ref) | copy-start | bytes 786436
  154.9 17.8 %copy-start.4 = (bf16[8,64,256]{2,1,0:T(8,128)(2,1)}, bf16[8,64,256]{2,1,0:T(8,128)(2,1)S(1)}, u32[]{:S(2)}) copy-start(bf16[8,64,256]{2,1,0:T(8,128)(2,1)S(1)} %collective-permute-done.3.yhi_ref) | copy-start | bytes 786436
  155.6 17.0 %collective-permute-start.5 = (bf16[2,2,64,256]{3,2,1,0:T(8,128)(2,1)}, bf16[2,2,64,256]{3,2,1,0:T(8,128)(2,1)S(1)}, u32[]{:S(2)}, u32[]{:S(2)}) collective-permute-start(bf16[2,2,64,256]{3,2,1,0:T(8,128)(2,1)} %pad_maximum_fusion.1), channel_id=1, source_target_pairs={{1,0},{2,1},{3,2},{4,3},{5,4},{6,5},{7,6},{8,7},{9,8},{10,9},{11,1... | collective-permute-start | bytes 393224 | tf_op jit(solution)/shard_map/ppermute | solution.py:275
  158.2 14.4 %collective-permute-start.4 = (bf16[2,2,64,256]{3,2,1,0:T(8,128)(2,1)}, bf16[2,2,64,256]{3,2,1,0:T(8,128)(2,1)S(1)}, u32[]{:S(2)}, u32[]{:S(2)}) collective-permute-start(bf16[2,2,64,256]{3,2,1,0:T(8,128)(2,1)} %pad_maximum_fusion), channel_id=1, source_target_pairs={{0,1},{1,2},{2,3},{3,4},{4,5},{5,6},{6,7},{7,8},{8,9},{9,10},{10,1... | collective-permute-start | bytes 393224 | tf_op jit(solution)/shard_map/ppermute | solution.py:275
  172.6 0.7 copy-start.5
  172.6 0.7 copy-start.6

commit v4 on v3

--- a/solution.py
+++ b/solution.py
@@ -123,136 +123,224 @@
     )(tgt, part)
 
 
-def conv_kernel(
-    flags_ref,
-    w_ref,
-    bias_ref,
-    coef_ref,
-    main_ref,
-    xlo_ref,
-    xhi_ref,
-    ylo_ref,
-    yhi_ref,
-    clo_ref,
-    chi_ref,
-    out_ref,
-    raw,
-    xs_a,
-    xs_b,
-    acc_a,
-    acc_b,
-    prev,
-    pend,
-    flat_a,
-    flat_b,
-    sems,
+def shifted(v, first, last):
+    down = jnp.where(first, 0.0, pltpu.roll(v, 1, 1))
+    up = jnp.where(last, 0.0, pltpu.roll(v, Z - 1, 1))
+    return down, up
+
+
+def edges():
+    lane = lax.broadcasted_iota(jnp.int32, (C, Z), 1)
+    return lane == 0, lane == Z - 1
+
+
+def stage(raw, p, xs, y, ends):
+    cols = slice(y * Z, (y + 1) * Z)
+    v = raw[p, :, cols]
+    down, up = shifted(v.astype(jnp.float32), *ends)
+    xs[0:C, cols] = down.astype(jnp.bfloat16)
+    xs[C : 2 * C, cols] = v
+    xs[2 * C : 3 * C, cols] = up.astype(jnp.bfloat16)
+
+
+def stage_rows(t):
+    return range(2 * t, 2 * t + 2 if t < BY // 2 else BY + 4)
+
+
+def window(xs, t):
+    return jnp.concatenate(
+        [xs[:, (t * 2 + dy) * Z : (t * 2 + dy + 2) * Z] for dy in range(3)], axis=0
+    )
+
+
+def split_rows(g, t, flags_ref):
+    rows = [g[:, :Z], g[:, Z:]]
+    if t == 0:
+        rows[0] = rows[0] * flags_ref[2]
+    if t == BY // 2:
+        rows[1] = rows[1] * flags_ref[3]
+    return rows
+
+
+def plane_copies(left, mid, right, to, sems):
+    return [
+        pltpu.make_async_copy(left, to.at[:, 0 : 2 * Z], sems.at[0]),
+        pltpu.make_async_copy(mid, to.at[:, 2 * Z : 2 * Z + ROW], sems.at[1]),
+        pltpu.make_async_copy(right, to.at[:, 2 * Z + ROW : WIDE], sems.at[2]),
+    ]
+
+
+def inner_kernel(
+    flags_ref, w_ref, bias_ref, coef_ref, main_ref, ylo_ref, yhi_ref,
+    out_ref, outer_ref, edge_ref, near_ref, pend_ref,
+    raw, xs_a, xs_b, acc_a, acc_b, prev, pend, flat_a, flat_b, packed, sems, done,
 ):
-    step = pl.program_id(0)
-    lane = lax.broadcasted_iota(jnp.int32, (C, Z), 1)
-    first = lane == 0
-    last = lane == Z - 1
-
-    def copies(p):
-        if p < 2:
-            left, mid, right = clo_ref.at[0, p], xlo_ref.at[p], clo_ref.at[1, p]
-        elif p < BX + 2:
-            left, mid, right = ylo_ref.at[p - 2], main_ref.at[p - 2], yhi_ref.at[p - 2]
-        else:
-            q = p - BX - 2
-            left, mid, right = chi_ref.at[0, q], xhi_ref.at[q], chi_ref.at[1, q]
-        to = raw.at[p]
-        return [
-            pltpu.make_async_copy(left, to.at[:, 0 : 2 * Z], sems.at[p, 0]),
-            pltpu.make_async_copy(mid, to.at[:, 2 * Z : 2 * Z + ROW], sems.at[p, 1]),
-            pltpu.make_async_copy(right, to.at[:, 2 * Z + ROW : WIDE], sems.at[p, 2]),
-        ]
-
-    def stage(p, xs, y):
-        cols = slice(y * Z, (y + 1) * Z)
-        v = raw[p, :, cols]
-        f = v.astype(jnp.float32)
-        xs[0:C, cols] = jnp.where(first, 0.0, pltpu.roll(f, 1, 1)).astype(jnp.bfloat16)
-        xs[C : 2 * C, cols] = v
-        xs[2 * C : 3 * C, cols] = jnp.where(last, 0.0, pltpu.roll(f, Z - 1, 1)).astype(jnp.bfloat16)
-
-    @pl.when(step == 0)
-    def _():
-        for p in range(BX + 4):
-            for copy in copies(p):
-                copy.start()
-        for copy in copies(0):
-            copy.wait()
-        for y in range(BY + 4):
-            stage(0, xs_a, y)
-
-    for p in range(1, BX + 4):
-
-        @pl.when(step == (0 if p < 3 else (p - 1) // 2))
-        def _():
-            for copy in copies(p):
-                copy.wait()
-
+    ends = edges()
+    copies = [
+        plane_copies(ylo_ref.at[x], main_ref.at[x], yhi_ref.at[x], raw.at[x], sems.at[x])
+        for x in range(BX)
+    ]
+    stores = [
+        pltpu.make_async_copy(packed.at[k], out_ref.at[:, k + 2], done.at[k])
+        for k in range(BX - 4)
+    ]
+    for group in copies:
+        for copy in group:
+            copy.start()
     bias = jnp.broadcast_to(bias_ref[...], (C, 2 * Z))
     weights = w_ref[...]
-
-    def half(plane, xs, xs_next, flat, to):
-        following = jnp.minimum(plane + 1, BX + 3)
-        keep = jnp.where(plane == 2, flags_ref[0], jnp.where(plane == BX + 3, flags_ref[1], 1.0))
-        x_out = jnp.clip(plane - 4, 0, BX - 1)
-        x_new = jnp.clip(plane - 3, 0, BX - 1)
+    buffers, flats = (xs_a, xs_b), (flat_a, flat_b)
+    for copy in copies[0]:
+        copy.wait()
+    for y in range(BY + 4):
+        stage(raw, 0, xs_a, y, ends)
+    for x in range(BX):
+        xs, xs_next, flat = buffers[x % 2], buffers[(x + 1) % 2], flats[x % 2]
+        if x + 1 < BX:
+            for copy in copies[x + 1]:
+                copy.wait()
+        new = x - 1
         before = None
         for t in range((BY + 2) // 2):
-            for y in range(2 * t, 2 * t + 2 if t < BY // 2 else BY + 4):
-                stage(following, xs_next, y)
+            if x + 1 < BX:
+                for y in stage_rows(t):
+                    stage(raw, x + 1, xs_next, y, ends)
             cols = slice(t * 2 * Z, (t + 1) * 2 * Z)
-            window = jnp.concatenate(
-                [xs[:, (t * 2 + dy) * Z : (t * 2 + dy + 2) * Z] for dy in range(3)], axis=0
-            )
-            p = jnp.dot(weights, window, preferred_element_type=jnp.float32)
-            g = jnp.maximum(acc_b[:, cols] + p[2 * C : 3 * C] + bias, 0.0) * keep
-            acc_b[:, cols] = acc_a[:, cols] + p[C : 2 * C]
-            acc_a[:, cols] = p[0:C]
-            rows = [g[:, :Z], g[:, Z:]]
-            if t == 0:
-                rows[0] = rows[0] * flags_ref[2]
-            if t == BY // 2:
-                rows[1] = rows[1] * flags_ref[3]
+            p = jnp.dot(weights, window(xs, t), preferred_element_type=jnp.float32)
+            if x == 0:
+                outer_ref[0, :, cols] = p[2 * C :]
+                acc_b[:, cols] = p[C : 2 * C]
+                acc_a[:, cols] = p[:C]
+                continue
+            total = acc_b[:, cols] + p[2 * C :]
+            if x == BX - 1:
+                edge_ref[1, :, cols] = acc_a[:, cols] + p[C : 2 * C]
+                outer_ref[1, :, cols] = p[:C]
+            else:
+                acc_b[:, cols] = acc_a[:, cols] + p[C : 2 * C]
+                acc_a[:, cols] = p[:C]
+            if x == 1:
+                edge_ref[0, :, cols] = total
+                continue
+            rows = split_rows(jnp.maximum(total + bias, 0.0), t, flags_ref)
             if t > 0:
-                window4 = before + rows
+                four = before + rows
                 for k in range(2):
                     y = 2 * t - 2 + k
                     here = slice(y * Z, (y + 1) * Z)
-                    low, mid, high = window4[k], window4[k + 1], window4[k + 2]
-                    beside = prev[:, here] + low + high
-                    beside = beside + jnp.where(first, 0.0, pltpu.roll(mid, 1, 1))
-                    beside = beside + jnp.where(last, 0.0, pltpu.roll(mid, Z - 1, 1))
-                    flat[pl.ds(y, C, stride=PITCH), :] = (
-                        pend[:, here] + coef_ref[x_out, y : y + 1, :] * mid
+                    low, mid, high = four[k], four[k + 1], four[k + 2]
+                    down, up = shifted(mid, *ends)
+                    beside = low + high + down + up
+                    if new > 1:
+                        beside = beside + prev[:, here]
+                        full = pend[:, here] + coef_ref[new - 1, y : y + 1, :] * mid
+                        if new == 2:
+                            pend_ref[0, :, here] = full
+                        else:
+                            flat[pl.ds(y, C, stride=PITCH), :] = full
+                    later = mid + coef_ref[new, y : y + 1, :] * (beside - 6.0 * mid)
+                    if new == 1:
+                        near_ref[0, :, here] = mid
+                    if new == BX - 2:
+                        near_ref[1, :, here] = mid
+                        pend_ref[1, :, here] = later
+                    else:
+                        prev[:, here] = mid
+                        pend[:, here] = later
+            before = rows
+        if new > 2:
+            packed[new - 3] = flat[...].reshape(C, PITCH, Z)[:, :BY].astype(jnp.bfloat16)
+            stores[new - 3].start()
+    for copy in stores:
+        copy.wait()
+
+
+def outer_kernel(
+    flags_ref, w_ref, bias_ref, coef_ref, outer_ref, edge_ref, near_ref, pend_ref,
+    xlo_ref, xhi_ref, clo_ref, chi_ref, part_ref,
+    out_ref,
+    raw, xs_0, xs_1, xs_2, xs_3, flat_a, flat_b, packed, sems, done,
+):
+    ends = edges()
+    copies = []
+    for p, (face, corner, q) in enumerate(
+        [(xlo_ref, clo_ref, 0), (xlo_ref, clo_ref, 1), (xhi_ref, chi_ref, 1), (xhi_ref, chi_ref, 0)]
+    ):
+        copies.append(
+            plane_copies(corner.at[0, q], face.at[q], corner.at[1, q], raw.at[p], sems.at[p])
+        )
+        for copy in copies[p]:
+            copy.start()
+    targets = [(0, 1), (BX - 1, BX - 2)]
+    stores = [
+        [
+            pltpu.make_async_copy(packed.at[2 * s + k], out_ref.at[:, targets[s][k]], done.at[s, k])
+            for k in range(2)
+        ]
+        for s in range(2)
+    ]
+    bias = jnp.broadcast_to(bias_ref[...], (C, 2 * Z))
+    planes = (xs_0, xs_1, xs_2, xs_3)
+    for p in range(2):
+        for copy in copies[p]:
+            copy.wait()
+        for y in range(BY + 4):
+            stage(raw, p, planes[p], y, ends)
+    for s in range(2):
+        far, nearer = planes[2 * s], planes[2 * s + 1]
+        e, i = targets[s]
+        if s == 0:
+            for p in (2, 3):
+                for copy in copies[p]:
+                    copy.wait()
+        before = None
+        for t in range((BY + 2) // 2):
+            if s == 0:
+                for p in (2, 3):
+                    for y in stage_rows(t):
+                        stage(raw, p, planes[p], y, ends)
+            cols = slice(t * 2 * Z, (t + 1) * 2 * Z)
+            a = jnp.dot(w_ref[s, :C], window(far, t), preferred_element_type=jnp.float32)
+            b = jnp.dot(w_ref[s, C:], window(nearer, t), preferred_element_type=jnp.float32)
+            past = jnp.maximum(outer_ref[s, :, cols] + a + b[:C] + bias, 0.0) * flags_ref[s]
+            rows = split_rows(
+                jnp.maximum(edge_ref[s, :, cols] + b[C:] + bias, 0.0), t, flags_ref
+            )
+            past = [past[:, :Z], past[:, Z:]]
+            if t > 0:
+                four = before[0] + rows
+                two = [before[1][1], past[0]]
+                for k in range(2):
+                    y = 2 * t - 2 + k
+                    here = slice(y * Z, (y + 1) * Z)
+                    low, mid, high = four[k], four[k + 1], four[k + 2]
+                    down, up = shifted(mid, *ends)
+                    beside = low + high + down + up + two[k] + near_ref[s, :, here]
+                    flat_a[pl.ds(y, C, stride=PITCH), :] = mid + coef_ref[e, y : y + 1, :] * (
+                        beside - 6.0 * mid
                     )
-                    pend[:, here] = mid + coef_ref[x_new, y : y + 1, :] * (beside - 6.0 * mid)
-                    prev[:, here] = mid
-            before = rows
-        out_ref[:, to] = flat[...].reshape(C, PITCH, Z)[:, :BY].astype(jnp.bfloat16)
-
-    half(2 * step, xs_a, xs_b, flat_a, 0)
-    half(2 * step + 1, xs_b, xs_a, flat_b, 1)
-
-
-def conv_smooth(flags, weights, bias, coef, main, xlo, xhi, ylo, yhi, clo, chi):
+                    flat_b[pl.ds(y, C, stride=PITCH), :] = (
+                        pend_ref[s, :, here] + coef_ref[i, y : y + 1, :] * mid
+                    )
+            before = (rows, past)
+        for k, flat in enumerate((flat_a, flat_b)):
+            packed[2 * s + k] = flat[...].reshape(C, PITCH, Z)[:, :BY].astype(jnp.bfloat16)
+            stores[s][k].start()
+    for group in stores:
+        for copy in group:
+            copy.wait()
+
+
+def conv_inner(flags, weights, bias, coef, main, ylo, yhi):
     hbm = pl.BlockSpec(memory_space=pl.ANY)
+    vmem = pl.BlockSpec(memory_space=pltpu.VMEM)
+    state = lambda width: jax.ShapeDtypeStruct((2, C, width), jnp.float32)
     return pl.pallas_call(
-        conv_kernel,
-        grid=((BX + 4) // 2,),
-        in_specs=[
-            pl.BlockSpec(memory_space=pltpu.SMEM),
-            pl.BlockSpec((3 * C, 9 * C), lambda i: (0, 0)),
-            pl.BlockSpec((C, 1), lambda i: (0, 0)),
-            pl.BlockSpec((BX, BY, Z), lambda i: (0, 0, 0)),
-        ]
-        + [hbm] * 7,
-        out_specs=pl.BlockSpec((C, 2, BY, Z), lambda i: (0, jnp.maximum(i - 2, 0), 0, 0)),
+        inner_kernel,
+        in_specs=[pl.BlockSpec(memory_space=pltpu.SMEM), vmem, vmem, vmem, hbm, hbm, hbm],
+        out_specs=[hbm] + [vmem] * 4,
         scratch_shapes=[
-            pltpu.VMEM((BX + 4, C, WIDE), jnp.bfloat16),
+            pltpu.VMEM((BX, C, WIDE), jnp.bfloat16),
             pltpu.VMEM((3 * C, WIDE), jnp.bfloat16),
             pltpu.VMEM((3 * C, WIDE), jnp.bfloat16),
             pltpu.VMEM((C, GATED), jnp.float32),
@@ -261,12 +349,42 @@
             pltpu.VMEM((C, ROW), jnp.float32),
             pltpu.VMEM((C * PITCH, Z), jnp.float32),
             pltpu.VMEM((C * PITCH, Z), jnp.float32),
-            pltpu.SemaphoreType.DMA((BX + 4, 3)),
+            pltpu.VMEM((BX - 4, C, BY, Z), jnp.bfloat16),
+            pltpu.SemaphoreType.DMA((BX, 3)),
+            pltpu.SemaphoreType.DMA((BX - 4,)),
+        ],
+        out_shape=[
+            jax.ShapeDtypeStruct((C, BX, BY, Z), jnp.bfloat16),
+            state(GATED),
+            state(GATED),
+            state(ROW),
+            state(ROW),
+        ],
+        compiler_params=pltpu.CompilerParams(vmem_limit_bytes=48 << 20),
+        name="conv_inner",
+    )(flags, weights, bias, coef, main, ylo, yhi)
+
+
+def conv_outer(flags, weights, bias, coef, state, xlo, xhi, clo, chi, volume):
+    hbm = pl.BlockSpec(memory_space=pl.ANY)
+    vmem = pl.BlockSpec(memory_space=pltpu.VMEM)
+    return pl.pallas_call(
+        outer_kernel,
+        in_specs=[pl.BlockSpec(memory_space=pltpu.SMEM)] + [vmem] * 7 + [hbm] * 5,
+        out_specs=hbm,
+        scratch_shapes=[pltpu.VMEM((4, C, WIDE), jnp.bfloat16)]
+        + [pltpu.VMEM((3 * C, WIDE), jnp.bfloat16)] * 4
+        + [pltpu.VMEM((C * PITCH, Z), jnp.float32)] * 2
+        + [
+            pltpu.VMEM((4, C, BY, Z), jnp.bfloat16),
+            pltpu.SemaphoreType.DMA((4, 3)),
+            pltpu.SemaphoreType.DMA((2, 2)),
         ],
         out_shape=jax.ShapeDtypeStruct((C, BX, BY, Z), jnp.bfloat16),
-        compiler_params=pltpu.CompilerParams(vmem_limit_bytes=56 << 20),
-        name="conv_smooth",
-    )(flags, weights, bias, coef, main, xlo, xhi, ylo, yhi, clo, chi)
+        input_output_aliases={12: 0},
+        compiler_params=pltpu.CompilerParams(vmem_limit_bytes=48 << 20),
+        name="conv_outer",
+    )(flags, weights, bias, coef, *state, xlo, xhi, clo, chi, volume)
 
 
 def shift(array, axis, by):
@@ -306,9 +424,15 @@
         [brick > 0, brick < n_bricks - 1, view > 0, view < n_views - 1]
     ).astype(jnp.float32)
     weights = jnp.transpose(conv_weight, (0, 3, 1, 2, 4)).reshape(3 * C, 9 * C)
-    return conv_smooth(
-        flags, weights, conv_bias[:, None], smooth_coef, main, xlo, xhi, from_low, from_high, clo, chi
+    sides = jnp.stack(
+        [
+            jnp.concatenate([weights[:C], weights[C : 2 * C], weights[:C]]),
+            jnp.concatenate([weights[2 * C :], weights[C : 2 * C], weights[2 * C :]]),
+        ]
     )
+    bias = conv_bias[:, None]
+    volume, *state = conv_inner(flags, weights, bias, smooth_coef, main, from_low, from_high)
+    return conv_outer(flags, sides, bias, smooth_coef, state, xlo, xhi, clo, chi, volume)
 
 
 def solution(mesh):

time: 201 us -> 198 us (0.985)
  waiting for transfers between devices: 13.4 us -> 0.02 us
  local copies, waits for them, and re-layouts: 6.52 us -> 11.5 us
  Pallas kernels: 44.4 us -> 48.2 us
  other arithmetic: 4.99 us -> 7.27 us
    ppermute x6, waiting for transfers between devices: 13.4 us -> 0.02 us  [shift(): return lax.ppermute(array, axis, pairs)]
    pallas_call x1 -> x2, Pallas kernels: 25.2 us -> 28.6 us  [the longest x1 19.2 us: conv_inner(): pl.pallas_call(inner_kernel, in_specs=[pl.BlockSpec(memory_space=pltpu.SM...]
    another operation x0 -> x2, other arithmetic: none -> 2.8 us  [on_device(): jnp.stack([jnp.concatenate([weights[:C], weights[C:2 * C], weights[:C]]),...]
    slice x0 -> x7, local copies, waits for them, and re-layouts: none -> 2.78 us  [the longest x3 0.95 us: on_device(): weights[:C]]
  transfers between devices with their start and end apart: 6 -> 6, of which waited for: 2 -> 0; matrix products, arithmetic and copies ran while one was open for 3% -> 6% of each run, Pallas kernels for 0% -> 10%
where the time goes in v4:
time: 198 us; the launch traced here: 197 us
  blocking collectives  111 us (56%)
  Pallas kernels  48.2 us (24%)
  starting transfers between devices  17.8 us (9%)
  local copies, waits for them, and re-layouts  11.5 us (6%)
  other arithmetic  7.27 us (4%)
    all_to_all x1, blocking collectives, on_device(): lax.all_to_all(packed, ('views', 'bricks'), split_axis=0, concat_axis=0,...  111 us
    pallas_call x1, Pallas kernels, conv_inner(): pl.pallas_call(inner_kernel, in_specs=[pl.BlockSpec(memory_space=pltpu.SM...  19.2 us
    ppermute x6, starting transfers between devices, shift(): return lax.ppermute(array, axis, pairs)  17.8 us
    pallas_call x1, Pallas kernels, partials(): pl.pallas_call(partial_kernel, in_specs=[smem, smem, pl.BlockSpec(memory_...  10.4 us
    pallas_call x1, Pallas kernels, conv_outer(): pl.pallas_call(outer_kernel, in_specs=[pl.BlockSpec(memory_space=pltpu.SM...  9.33 us
    pallas_call x1, Pallas kernels, lift(): pl.pallas_call(lift_kernel, in_specs=[pl.BlockSpec(memory_space=pltpu.SME...  9.23 us
    unnamed x16, local copies, waits for them, and re-layouts  4.95 us
  transfers between devices with their start and end apart: 6, of which 0 were waited for; matrix products, arithmetic and copies ran while one was open for 6% of the time, Pallas kernels for 10%

profile of v4, /device:TPU:9, one launch (start us, length us, event | category | flops | bytes accessed | tf_op | source)
XLA Modules:
  0.0 196.6 jit_solution(7348531899338911800)
XLA Ops:
  0.7 0.7 compare_select_fusion.2.tgt_ref
  1.3 0.0 copy-start.2
  1.3 0.9 copy-done.2
  2.3 0.0 copy-start.3
  2.3 0.7 copy-done.3
  2.9 10.4 %partials.1 = bf16[128,264,128]{2,1,0:T(8,128)(2,1)} custom-call(s32[128]{0:T(128)S(1)} %bitcast.29, s32[128]{0:T(128)S(1)} %compare_select_fusion.2.tgt_ref, bf16[16,64,128]{2,1,0:T(8,128)(2,1)S(1)} %bitcast.28, bf16[128,128,512]{2,1,0:T(8,128)(2,1)} %bitcast.30), custom_call_target="tpu_custom_call" | custom-call | tf_op jit(solution)/shard_map/partials/pallas_call | solution.py:62
  13.3 110.8 %all_to_all.5.part_ref = bf16[128,264,128]{2,1,0:T(8,128)(2,1)S(1)} all-to-all(bf16[128,264,128]{2,1,0:T(8,128)(2,1)} %partials.1), channel_id=1, replica_groups=mesh['views'=8,'bricks'=16] {'views','bricks'}, dimensions={0} | all-to-all | bytes 17301504 | tf_op jit(solution)/shard_map/all_to_all | solution.py:414
  124.2 0.0 copy-start.5
  124.2 2.4 %fusion.4.tgt_ref = s32[128]{0:T(128)S(1)} fusion(bf16[128,264,128]{2,1,0:T(8,128)(2,1)S(1)} %all_to_all.5.part_ref), kind=kLoop, calls=%fused_computation.14 | loop fusion | flops 128 | bytes 768 | tf_op jit(solution)/shard_map/convert_element_type | solution.py:415
  126.5 1.0 copy-done.5
  127.5 0.0 copy-start.6
  127.5 9.2 %lift.1 = (bf16[8,64,4096]{2,1,0:T(8,128)(2,1)}, bf16[2,64,4096]{2,1,0:T(8,128)(2,1)S(1)}, bf16[2,64,4096]{2,1,0:T(8,128)(2,1)}, bf16[8,64,256]{2,1,0:T(8,128)(2,1)S(1)}, bf16[8,64,256]{2,1,0:T(8,128)(2,1)S(1)}) custom-call(s32[128]{0:T(128)S(1)} %fusion.4.tgt_ref, bf16[128,264,128]{2,1,0:T(8,128)(2,1)} %copy-done.5), custom_call_target="tpu_custom_call" | custom-call | tf_op jit(solution)/shard_map/lift/pallas_call | solution.py:107
  136.7 0.0 copy-start.4
  136.7 1.0 copy-done.4
  137.7 0.0 copy-start.7
  137.7 0.0 copy-start.1
  137.7 3.2 %collective-permute-start = (bf16[8,64,256]{2,1,0:T(8,128)(2,1)S(1)}, bf16[8,64,256]{2,1,0:T(8,128)(2,1)S(1)}, u32[]{:S(2)}, u32[]{:S(2)}) collective-permute-start(bf16[8,64,256]{2,1,0:T(8,128)(2,1)S(1)} %get-tuple-element.16), channel_id=1, source_target_pairs={{0,16},{16,32},{32,48},{48,64},{64,80},{80,96},{96,112},{1,17},{17... | collective-permute-start | bytes 786440 | tf_op jit(solution)/shard_map/ppermute | solution.py:393
  140.9 0.0 copy-done.6
  141.0 0.1 copy.16
  141.1 0.8 copy.18
  141.9 0.1 copy.17
  142.1 0.8 copy.19
  142.8 0.1 copy.21
  143.0 0.8 copy.22
  143.8 1.9 collective-permute-start.1
  145.7 2.3 %collective-permute-start.2 = (bf16[2,64,4096]{2,1,0:T(8,128)(2,1)}, bf16[2,64,4096]{2,1,0:T(8,128)(2,1)S(1)}, u32[]{:S(2)}, u32[]{:S(2)}) collective-permute-start(bf16[2,64,4096]{2,1,0:T(8,128)(2,1)} %get-tuple-element.22), channel_id=1, source_target_pairs={{0,1},{1,2},{2,3},{3,4},{4,5},{5,6},{6,7},{7,8},{8,9},{9,10},{10,1... | collective-permute-start | bytes 3145736 | tf_op jit(solution)/shard_map/ppermute | solution.py:393
  148.0 5.1 %collective-permute-start.3 = (bf16[2,64,4096]{2,1,0:T(8,128)(2,1)}, bf16[2,64,4096]{2,1,0:T(8,128)(2,1)S(1)}, u32[]{:S(2)}, u32[]{:S(2)}) collective-permute-start(bf16[2,64,4096]{2,1,0:T(8,128)(2,1)} %copy-done.4), channel_id=1, source_target_pairs={{1,0},{2,1},{3,2},{4,3},{5,4},{6,5},{7,6},{8,7},{9,8},{10,9},{11,1... | collective-permute-start | bytes 3145736 | tf_op jit(solution)/shard_map/ppermute | solution.py:393
  153.1 1.8 fusion.1
  154.9 0.0 collective-permute-done.ylo_ref
  154.9 0.0 collective-permute-done.1.yhi_ref
  154.9 0.7 pad_maximum_fusion.4
  155.6 1.9 collective-permute-start.5
  157.5 0.7 pad_maximum_fusion.3
  158.2 3.3 %collective-permute-start.4 = (bf16[2,2,64,256]{3,2,1,0:T(8,128)(2,1)}, bf16[2,2,64,256]{3,2,1,0:T(8,128)(2,1)S(1)}, u32[]{:S(2)}, u32[]{:S(2)}) collective-permute-start(bf16[2,2,64,256]{3,2,1,0:T(8,128)(2,1)} %pad_maximum_fusion.3), channel_id=1, source_target_pairs={{0,1},{1,2},{2,3},{3,4},{4,5},{5,6},{6,7},{7,8},{8,9},{9,10},{10,1... | collective-permute-start | bytes 393224 | tf_op jit(solution)/shard_map/ppermute | solution.py:393
  161.5 0.1 add_convert_fusion.flags_ref
  161.6 2.2 %copy.25 = bf16[3,64,3,3,64]{4,3,2,1,0:T(4,128)(2,1)} copy(bf16[3,64,3,3,64]{4,1,3,2,0:T(8,128)(2,1)} %bitcast.31) | data formatting | bytes 442368 | tf_op jit(solution)/shard_map/transpose | solution.py:426
  163.8 1.5 reshape.8.w_ref
  165.3 0.0 copy-done.7
  165.3 0.1 copy.27.bias_ref
  165.4 1.0 pad_maximum_fusion.w_ref
  166.4 0.0 copy-done.1
  166.5 19.2 %conv_inner.1 = (bf16[64,8,32,128]{3,2,1,0:T(8,128)(2,1)}, f32[2,64,4352]{2,1,0:T(8,128)}, f32[2,64,4352]{2,1,0:T(8,128)}, f32[2,64,4096]{2,1,0:T(8,128)S(1)}, f32[2,64,4096]{2,1,0:T(8,128)S(1)}) custom-call(f32[4]{0:T(128)S(1)} %add_convert_fusion.flags_ref, bf16[192,576]{1,0:T(8,128)(2,1)S(1)} %reshape.8.w_ref, f32[64,1]{1,0:T(8,128)S(1)} %copy.27.bias_ref, ...), custom_call_target="tpu_custom_call" | custom-call | tf_op jit(solution)/shard_map/conv_inner/pallas_call | solution.py:338
  185.7 0.0 copy-start
  185.7 1.4 copy-done
  187.1 0.0 collective-permute-done.5.chi_ref
  187.1 0.0 collective-permute-done.4.clo_ref
  187.1 0.0 collective-permute-done.2.xlo_ref
  187.1 0.0 collective-permute-done.3.xhi_ref
  187.1 9.3 %conv_outer.1 = bf16[64,8,32,128]{3,2,1,0:T(8,128)(2,1)} custom-call(f32[4]{0:T(128)S(1)} %add_convert_fusion.flags_ref, bf16[2,192,576]{2,1,0:T(8,128)(2,1)S(1)} %pad_maximum_fusion.w_ref, f32[64,1]{1,0:T(8,128)S(1)} %copy.27.bias_ref, f32[8,32,128]{2,1,0:T(8,128)S(1)} %copy-done.1, ...), custom_call_target="tpu_custom_call", output_to_operand_aliasing={{}: (12, {})} | custom-call | tf_op jit(solution)/shard_map/conv_outer/pallas_call | solution.py:371
  (3 shorter events, 0.1 us)
Async XLA Ops:
  1.3 0.9 copy-start.2
  2.3 0.7 copy-start.3
  124.2 3.4 %copy-start.5 = (bf16[128,264,128]{2,1,0:T(8,128)(2,1)}, bf16[128,264,128]{2,1,0:T(8,128)(2,1)S(1)}, u32[]{:S(2)}) copy-start(bf16[128,264,128]{2,1,0:T(8,128)(2,1)S(1)} %all_to_all.5.part_ref) | copy-start | bytes 25952260
  127.5 13.4 %copy-start.6 = (bf16[3,3,3,64,64]{4,3,2,1,0:T(8,128)(2,1)S(1)}, bf16[3,3,3,64,64]{4,3,2,1,0:T(8,128)(2,1)}, u32[]{:S(2)}) copy-start(bf16[3,3,3,64,64]{4,3,2,1,0:T(8,128)(2,1)} %param.13) | copy-start | bytes 663556
  136.7 1.0 copy-start.4
  137.7 27.6 %copy-start.7 = (f32[64]{0:T(128)S(1)}, f32[64]{0:T(128)}, u32[]{:S(2)}) copy-start(f32[64]{0:T(128)} %param.14) | copy-start | bytes 772
  137.7 28.7 %copy-start.1 = (f32[8,32,128]{2,1,0:T(8,128)S(1)}, f32[8,32,128]{2,1,0:T(8,128)}, u32[]{:S(2)}) copy-start(f32[8,32,128]{2,1,0:T(8,128)} %coef_ref.3) | copy-start | bytes 393220
  137.7 17.2 %collective-permute-start = (bf16[8,64,256]{2,1,0:T(8,128)(2,1)S(1)}, bf16[8,64,256]{2,1,0:T(8,128)(2,1)S(1)}, u32[]{:S(2)}, u32[]{:S(2)}) collective-permute-start(bf16[8,64,256]{2,1,0:T(8,128)(2,1)S(1)} %get-tuple-element.16), channel_id=1, source_target_pairs={{0,16},{16,32},{32,48},{48,64},{64,80},{80,96},{96,112},{1,17},{17... | collective-permute-start | bytes 786440 | tf_op jit(solution)/shard_map/ppermute | solution.py:393
  143.8 11.1 %collective-permute-start.1 = (bf16[8,64,256]{2,1,0:T(8,128)(2,1)S(1)}, bf16[8,64,256]{2,1,0:T(8,128)(2,1)S(1)}, u32[]{:S(2)}, u32[]{:S(2)}) collective-permute-start(bf16[8,64,256]{2,1,0:T(8,128)(2,1)S(1)} %get-tuple-element.17), channel_id=1, source_target_pairs={{16,0},{32,16},{48,32},{64,48},{80,64},{96,80},{112,96},{17,1},{33... | collective-permute-start | bytes 786440 | tf_op jit(solution)/shard_map/ppermute | solution.py:393
  145.7 41.4 %collective-permute-start.2 = (bf16[2,64,4096]{2,1,0:T(8,128)(2,1)}, bf16[2,64,4096]{2,1,0:T(8,128)(2,1)S(1)}, u32[]{:S(2)}, u32[]{:S(2)}) collective-permute-start(bf16[2,64,4096]{2,1,0:T(8,128)(2,1)} %get-tuple-element.22), channel_id=1, source_target_pairs={{0,1},{1,2},{2,3},{3,4},{4,5},{5,6},{6,7},{7,8},{8,9},{9,10},{10,1... | collective-permute-start | bytes 3145736 | tf_op jit(solution)/shard_map/ppermute | solution.py:393
  148.0 39.2 %collective-permute-start.3 = (bf16[2,64,4096]{2,1,0:T(8,128)(2,1)}, bf16[2,64,4096]{2,1,0:T(8,128)(2,1)S(1)}, u32[]{:S(2)}, u32[]{:S(2)}) collective-permute-start(bf16[2,64,4096]{2,1,0:T(8,128)(2,1)} %copy-done.4), channel_id=1, source_target_pairs={{1,0},{2,1},{3,2},{4,3},{5,4},{6,5},{7,6},{8,7},{9,8},{10,9},{11,1... | collective-permute-start | bytes 3145736 | tf_op jit(solution)/shard_map/ppermute | solution.py:393
  155.6 31.5 %collective-permute-start.5 = (bf16[2,2,64,256]{3,2,1,0:T(8,128)(2,1)}, bf16[2,2,64,256]{3,2,1,0:T(8,128)(2,1)S(1)}, u32[]{:S(2)}, u32[]{:S(2)}) collective-permute-start(bf16[2,2,64,256]{3,2,1,0:T(8,128)(2,1)} %pad_maximum_fusion.4), channel_id=1, source_target_pairs={{1,0},{2,1},{3,2},{4,3},{5,4},{6,5},{7,6},{8,7},{9,8},{10,9},{11,1... | collective-permute-start | bytes 393224 | tf_op jit(solution)/shard_map/ppermute | solution.py:393
  158.2 28.9 %collective-permute-start.4 = (bf16[2,2,64,256]{3,2,1,0:T(8,128)(2,1)}, bf16[2,2,64,256]{3,2,1,0:T(8,128)(2,1)S(1)}, u32[]{:S(2)}, u32[]{:S(2)}) collective-permute-start(bf16[2,2,64,256]{3,2,1,0:T(8,128)(2,1)} %pad_maximum_fusion.3), channel_id=1, source_target_pairs={{0,1},{1,2},{2,3},{3,4},{4,5},{5,6},{6,7},{7,8},{8,9},{9,10},{10,1... | collective-permute-start | bytes 393224 | tf_op jit(solution)/shard_map/ppermute | solution.py:393
  185.7 1.4 copy-start

commit v5 on v4

--- a/solution.py
+++ b/solution.py
@@ -22,7 +22,11 @@
 PITCH = 40
 
 
-def partial_kernel(pixel_ref, tgt_ref, feats_ref, tiles_ref, out_ref, tiles, out, sems, done):
+def partial_kernel(
+    pixel_ref, voxel_ref, count_ref, feats_ref, cw_ref, cb_ref, tiles_ref,
+    out_ref, w_ref, bias_ref,
+    tiles, out, sems, done,
+):
     chunks = tiles.shape[0] // SEND
 
     def load(k):
@@ -35,6 +39,20 @@
 
     for k in range(chunks):
         load(k).start()
+
+    taps = 9
+    for dx in range(3):
+        for q in range(0, taps, 2):
+            pieces = [cw_ref[dx * taps + r] for r in range(q, min(q + 2, taps))]
+            both = pieces[0] if len(pieces) == 1 else jnp.concatenate(pieces, axis=1)
+            w_ref[dx * C : (dx + 1) * C, q * C : q * C + both.shape[1]] = both
+    eye = lax.broadcasted_iota(jnp.int32, (C, C), 0) == lax.broadcasted_iota(jnp.int32, (C, C), 1)
+    column = jnp.where(eye, jnp.broadcast_to(cb_ref[...], (C, C)), 0.0)
+    bias_ref[...] = jnp.broadcast_to(jnp.sum(column, axis=1, keepdims=True), (C, 2 * Z))
+    me = lax.axis_index("views") * lax.axis_size("bricks") + lax.axis_index("bricks")
+    slots = tiles.shape[0]
+    offset = lax.rem(me * 37, slots)
+    count = count_ref[0]
 
     def chunk(k, carry):
         load(k).wait()
@@ -45,7 +63,10 @@
             )
             for q in range(4):
                 out[slot, q * C : (q + 1) * C, :] = p[:, q * Z : (q + 1) * Z].astype(jnp.bfloat16)
-            block = jnp.full((PACK - 4 * C, Z), tgt_ref[slot].astype(jnp.float32), jnp.float32)
+            place = slot - offset
+            place = jnp.where(place < 0, place + slots, place)
+            target = jnp.where(place < count, voxel_ref[slot], BLK)
+            block = jnp.full((PACK - 4 * C, Z), target.astype(jnp.float32), jnp.float32)
             out[slot, 4 * C : PACK, :] = block.astype(jnp.bfloat16)
         store(k).start()
         return carry
@@ -55,61 +76,89 @@
         store(k).wait()
 
 
-def partials(pixel_ids, targets, feats, tiles):
+def partials(pixel_ids, voxel_ids, count, feats, conv_weight, conv_bias, tiles):
     n = tiles.shape[0]
     smem = pl.BlockSpec(memory_space=pltpu.SMEM)
+    vmem = pl.BlockSpec(memory_space=pltpu.VMEM)
     hbm = pl.BlockSpec(memory_space=pl.ANY)
     return pl.pallas_call(
         partial_kernel,
-        in_specs=[smem, smem, pl.BlockSpec(memory_space=pltpu.VMEM), hbm],
-        out_specs=hbm,
+        in_specs=[smem, smem, smem, vmem, vmem, vmem, hbm],
+        out_specs=[hbm, vmem, vmem],
         scratch_shapes=[
             pltpu.VMEM((n, PIX, VOXB), jnp.bfloat16),
             pltpu.VMEM((n, PACK, Z), jnp.bfloat16),
             pltpu.SemaphoreType.DMA((n // SEND,)),
             pltpu.SemaphoreType.DMA((n // SEND,)),
         ],
-        out_shape=jax.ShapeDtypeStruct((n, PACK, Z), jnp.bfloat16),
+        out_shape=[
+            jax.ShapeDtypeStruct((n, PACK, Z), jnp.bfloat16),
+            jax.ShapeDtypeStruct((3 * C, 9 * C), jnp.bfloat16),
+            jax.ShapeDtypeStruct((C, 2 * Z), jnp.float32),
+        ],
         compiler_params=pltpu.CompilerParams(vmem_limit_bytes=48 << 20),
         name="partials",
-    )(pixel_ids, targets, feats, tiles)
-
-
-def lift_kernel(tgt_ref, part_ref, main_ref, lo_ref, hi_ref, ylo_ref, yhi_ref, acc):
+    )(pixel_ids, voxel_ids, count, feats, conv_weight, conv_bias, tiles)
+
+
+def lift_kernel(
+    part_ref, main_ref, lo_ref, hi_ref, ylo_ref, yhi_ref, acc, rows, ids, tgt_ref, sem, done
+):
+    n = part_ref.shape[0]
+    lane = lax.broadcasted_iota(jnp.int32, (8, Z), 1)
+    table = jnp.zeros((8, Z), jnp.float32)
+    for i in range(n):
+        table = jnp.where(lane == i, part_ref[i, 4 * C : PACK].astype(jnp.float32), table)
+    ids[...] = table.astype(jnp.int32)
+    move = pltpu.make_async_copy(ids, tgt_ref, sem)
+    move.start()
     acc[...] = jnp.zeros_like(acc)
+    move.wait()
 
     def add(i, carry):
-        block = tgt_ref[i]
-        acc[block] = acc[block] + part_ref[i, : 4 * C].astype(jnp.float32)
+        block = tgt_ref[0, i]
+
+        @pl.when(block < BLK)
+        def _():
+            acc[block] = acc[block] + part_ref[i, : 4 * C].astype(jnp.float32)
+
         return carry
 
-    lax.fori_loop(0, part_ref.shape[0], add, 0)
-
-    def plane(x, carry):
+    lax.fori_loop(0, n, add, 0)
+
+    stores = [pltpu.make_async_copy(rows.at[x], main_ref.at[x], done.at[x]) for x in range(BX)]
+    for x in range(BX):
         for y in range(BY):
             v = acc[x * (BY // 4) + y // 4, (y % 4) * C : (y % 4 + 1) * C, :]
             v = jnp.maximum(v, 0.0).astype(jnp.bfloat16)
-            main_ref[x, :, y * Z : (y + 1) * Z] = v
+            cols = slice(y * Z, (y + 1) * Z)
+            rows[x, :, cols] = v
+            if x < 2:
+                lo_ref[x, :, cols] = v
+            if x >= BX - 2:
+                hi_ref[x - BX + 2, :, cols] = v
             if y < 2:
-                ylo_ref[x, :, y * Z : (y + 1) * Z] = v
+                ylo_ref[x, :, cols] = v
             if y >= BY - 2:
                 yhi_ref[x, :, (y - BY + 2) * Z : (y - BY + 3) * Z] = v
-        return carry
-
-    lax.fori_loop(0, BX, plane, 0)
-    lo_ref[...] = main_ref[0:2]
-    hi_ref[...] = main_ref[BX - 2 : BX]
-
-
-def lift(tgt, part):
-    n = part.shape[0]
+        stores[x].start()
+    for copy in stores:
+        copy.wait()
+
+
+def lift(part):
     vmem = pl.BlockSpec(memory_space=pltpu.VMEM)
     return pl.pallas_call(
         lift_kernel,
-        in_specs=[pl.BlockSpec(memory_space=pltpu.SMEM), vmem],
-        out_specs=[vmem] * 5,
+        in_specs=[vmem],
+        out_specs=[pl.BlockSpec(memory_space=pl.ANY)] + [vmem] * 4,
         scratch_shapes=[
-            pltpu.VMEM((BLK + 1, 4 * C, Z), jnp.float32),
+            pltpu.VMEM((BLK, 4 * C, Z), jnp.float32),
+            pltpu.VMEM((BX, C, ROW), jnp.bfloat16),
+            pltpu.VMEM((8, Z), jnp.int32),
+            pltpu.SMEM((8, Z), jnp.int32),
+            pltpu.SemaphoreType.DMA,
+            pltpu.SemaphoreType.DMA((BX,)),
         ],
         out_shape=[
             jax.ShapeDtypeStruct((BX, C, ROW), jnp.bfloat16),
@@ -120,7 +169,20 @@
         ],
         compiler_params=pltpu.CompilerParams(vmem_limit_bytes=48 << 20),
         name="lift",
-    )(tgt, part)
+    )(part)
+
+
+def inside():
+    brick, view = lax.axis_index("bricks"), lax.axis_index("views")
+    return [
+        jnp.where(test, 1.0, 0.0).astype(jnp.float32)
+        for test in (
+            brick > 0,
+            brick < lax.axis_size("bricks") - 1,
+            view > 0,
+            view < lax.axis_size("views") - 1,
+        )
+    ]
 
 
 def shifted(v, first, last):
@@ -153,12 +215,12 @@
     )
 
 
-def split_rows(g, t, flags_ref):
+def split_rows(g, t, flags):
     rows = [g[:, :Z], g[:, Z:]]
     if t == 0:
-        rows[0] = rows[0] * flags_ref[2]
+        rows[0] = rows[0] * flags[2]
     if t == BY // 2:
-        rows[1] = rows[1] * flags_ref[3]
+        rows[1] = rows[1] * flags[3]
     return rows
 
 
@@ -171,11 +233,11 @@
 
 
 def inner_kernel(
-    flags_ref, w_ref, bias_ref, coef_ref, main_ref, ylo_ref, yhi_ref,
+    w_ref, bias_ref, coef_ref, main_ref, ylo_ref, yhi_ref,
     out_ref, outer_ref, edge_ref, near_ref, pend_ref,
     raw, xs_a, xs_b, acc_a, acc_b, prev, pend, flat_a, flat_b, packed, sems, done,
 ):
-    ends = edges()
+    ends, flags = edges(), inside()
     copies = [
         plane_copies(ylo_ref.at[x], main_ref.at[x], yhi_ref.at[x], raw.at[x], sems.at[x])
         for x in range(BX)
@@ -187,7 +249,7 @@
     for group in copies:
         for copy in group:
             copy.start()
-    bias = jnp.broadcast_to(bias_ref[...], (C, 2 * Z))
+    bias = bias_ref[...]
     weights = w_ref[...]
     buffers, flats = (xs_a, xs_b), (flat_a, flat_b)
     for copy in copies[0]:
@@ -222,7 +284,7 @@
             if x == 1:
                 edge_ref[0, :, cols] = total
                 continue
-            rows = split_rows(jnp.maximum(total + bias, 0.0), t, flags_ref)
+            rows = split_rows(jnp.maximum(total + bias, 0.0), t, flags)
             if t > 0:
                 four = before + rows
                 for k in range(2):
@@ -256,12 +318,12 @@
 
 
 def outer_kernel(
-    flags_ref, w_ref, bias_ref, coef_ref, outer_ref, edge_ref, near_ref, pend_ref,
+    w_ref, bias_ref, coef_ref, outer_ref, edge_ref, near_ref, pend_ref,
     xlo_ref, xhi_ref, clo_ref, chi_ref, part_ref,
     out_ref,
     raw, xs_0, xs_1, xs_2, xs_3, flat_a, flat_b, packed, sems, done,
 ):
-    ends = edges()
+    ends, flags = edges(), inside()
     copies = []
     for p, (face, corner, q) in enumerate(
         [(xlo_ref, clo_ref, 0), (xlo_ref, clo_ref, 1), (xhi_ref, chi_ref, 1), (xhi_ref, chi_ref, 0)]
@@ -279,7 +341,7 @@
         ]
         for s in range(2)
     ]
-    bias = jnp.broadcast_to(bias_ref[...], (C, 2 * Z))
+    bias = bias_ref[...]
     planes = (xs_0, xs_1, xs_2, xs_3)
     for p in range(2):
         for copy in copies[p]:
@@ -288,6 +350,8 @@
             stage(raw, p, planes[p], y, ends)
     for s in range(2):
         far, nearer = planes[2 * s], planes[2 * s + 1]
+        w_side = w_ref[2 * s * C : (2 * s + 1) * C]
+        w_both = jnp.concatenate([w_ref[C : 2 * C], w_side], axis=0)
         e, i = targets[s]
         if s == 0:
             for p in (2, 3):
@@ -300,11 +364,11 @@
                     for y in stage_rows(t):
                         stage(raw, p, planes[p], y, ends)
             cols = slice(t * 2 * Z, (t + 1) * 2 * Z)
-            a = jnp.dot(w_ref[s, :C], window(far, t), preferred_element_type=jnp.float32)
-            b = jnp.dot(w_ref[s, C:], window(nearer, t), preferred_element_type=jnp.float32)
-            past = jnp.maximum(outer_ref[s, :, cols] + a + b[:C] + bias, 0.0) * flags_ref[s]
+            a = jnp.dot(w_side, window(far, t), preferred_element_type=jnp.float32)
+            b = jnp.dot(w_both, window(nearer, t), preferred_element_type=jnp.float32)
+            past = jnp.maximum(outer_ref[s, :, cols] + a + b[:C] + bias, 0.0) * flags[s]
             rows = split_rows(
-                jnp.maximum(edge_ref[s, :, cols] + b[C:] + bias, 0.0), t, flags_ref
+                jnp.maximum(edge_ref[s, :, cols] + b[C:] + bias, 0.0), t, flags
             )
             past = [past[:, :Z], past[:, Z:]]
             if t > 0:
@@ -331,13 +395,13 @@
             copy.wait()
 
 
-def conv_inner(flags, weights, bias, coef, main, ylo, yhi):
+def conv_inner(weights, bias, coef, main, ylo, yhi):
     hbm = pl.BlockSpec(memory_space=pl.ANY)
     vmem = pl.BlockSpec(memory_space=pltpu.VMEM)
     state = lambda width: jax.ShapeDtypeStruct((2, C, width), jnp.float32)
     return pl.pallas_call(
         inner_kernel,
-        in_specs=[pl.BlockSpec(memory_space=pltpu.SMEM), vmem, vmem, vmem, hbm, hbm, hbm],
+        in_specs=[vmem, vmem, vmem, hbm, hbm, hbm],
         out_specs=[hbm] + [vmem] * 4,
         scratch_shapes=[
             pltpu.VMEM((BX, C, WIDE), jnp.bfloat16),
@@ -362,15 +426,15 @@
         ],
         compiler_params=pltpu.CompilerParams(vmem_limit_bytes=48 << 20),
         name="conv_inner",
-    )(flags, weights, bias, coef, main, ylo, yhi)
-
-
-def conv_outer(flags, weights, bias, coef, state, xlo, xhi, clo, chi, volume):
+    )(weights, bias, coef, main, ylo, yhi)
+
+
+def conv_outer(weights, bias, coef, state, xlo, xhi, clo, chi, volume):
     hbm = pl.BlockSpec(memory_space=pl.ANY)
     vmem = pl.BlockSpec(memory_space=pltpu.VMEM)
     return pl.pallas_call(
         outer_kernel,
-        in_specs=[pl.BlockSpec(memory_space=pltpu.SMEM)] + [vmem] * 7 + [hbm] * 5,
+        in_specs=[vmem] * 7 + [hbm] * 5,
         out_specs=hbm,
         scratch_shapes=[pltpu.VMEM((4, C, WIDE), jnp.bfloat16)]
         + [pltpu.VMEM((3 * C, WIDE), jnp.bfloat16)] * 4
@@ -381,10 +445,10 @@
             pltpu.SemaphoreType.DMA((2, 2)),
         ],
         out_shape=jax.ShapeDtypeStruct((C, BX, BY, Z), jnp.bfloat16),
-        input_output_aliases={12: 0},
+        input_output_aliases={11: 0},
         compiler_params=pltpu.CompilerParams(vmem_limit_bytes=48 << 20),
         name="conv_outer",
-    )(flags, weights, bias, coef, *state, xlo, xhi, clo, chi, volume)
+    )(weights, bias, coef, *state, xlo, xhi, clo, chi, volume)
 
 
 def shift(array, axis, by):
@@ -398,41 +462,25 @@
 ):
     feats = features[0, 0]
     tiles = interp[0, 0]
-    pixel_ids = tile_pixel[0, 0]
-    voxel_ids = tile_voxel[0, 0]
-    count = tile_count[0, 0]
-    slots_total = tiles.shape[0]
-    n_bricks = lax.axis_size("bricks")
-    n_views = lax.axis_size("views")
-    brick = lax.axis_index("bricks")
-    view = lax.axis_index("views")
-    me = view * n_bricks + brick
-    slot_ids = jnp.arange(slots_total, dtype=jnp.int32)
-    live = jnp.remainder(slot_ids - jnp.remainder(me * 37, slots_total), slots_total) < count
-    targets = jnp.where(live, voxel_ids, BLK)
-    packed = partials(pixel_ids, targets, feats, tiles)
+    packed, weights, bias = partials(
+        tile_pixel[0, 0],
+        tile_voxel[0, 0],
+        tile_count[0],
+        feats,
+        conv_weight.reshape(27, C, C),
+        conv_bias[None],
+        tiles,
+    )
     got = lax.all_to_all(packed, ("views", "bricks"), split_axis=0, concat_axis=0, tiled=True)
-    tgt = got[:, 4 * C, 0].astype(jnp.int32)
-    main, lo, hi, ylo, yhi = lift(tgt, got)
+    main, lo, hi, ylo, yhi = lift(got)
     from_low = shift(yhi, "views", 1)
     from_high = shift(ylo, "views", -1)
     xlo = shift(hi, "bricks", 1)
     xhi = shift(lo, "bricks", -1)
     clo = shift(jnp.stack([from_low[BX - 2 :], from_high[BX - 2 :]]), "bricks", 1)
     chi = shift(jnp.stack([from_low[:2], from_high[:2]]), "bricks", -1)
-    flags = jnp.stack(
-        [brick > 0, brick < n_bricks - 1, view > 0, view < n_views - 1]
-    ).astype(jnp.float32)
-    weights = jnp.transpose(conv_weight, (0, 3, 1, 2, 4)).reshape(3 * C, 9 * C)
-    sides = jnp.stack(
-        [
-            jnp.concatenate([weights[:C], weights[C : 2 * C], weights[:C]]),
-            jnp.concatenate([weights[2 * C :], weights[C : 2 * C], weights[2 * C :]]),
-        ]
-    )
-    bias = conv_bias[:, None]
-    volume, *state = conv_inner(flags, weights, bias, smooth_coef, main, from_low, from_high)
-    return conv_outer(flags, sides, bias, smooth_coef, state, xlo, xhi, clo, chi, volume)
+    volume, *state = conv_inner(weights, bias, smooth_coef, main, from_low, from_high)
+    return conv_outer(weights, bias, smooth_coef, state, xlo, xhi, clo, chi, volume)
 
 
 def solution(mesh):

time: 198 us -> 189 us (0.955)
  other arithmetic: 7.27 us -> 0.03 us
  local copies, waits for them, and re-layouts: 11.5 us -> 5.32 us
  waiting for transfers between devices: 0.02 us -> 6.04 us
    ppermute x6, waiting for transfers between devices: 0.02 us -> 6.04 us  [shift(): return lax.ppermute(array, axis, pairs)]
    another operation x2 -> x0, other arithmetic: 2.8 us -> none  [on_device(): jnp.stack([jnp.concatenate([weights[:C], weights[C:2 * C], weights[:C]]),...]
    slice x7 -> x0, local copies, waits for them, and re-layouts: 2.78 us -> none  [the longest x3 0.95 us: on_device(): weights[:C]]
    convert_element_type x2 -> x0, other arithmetic: 2.43 us -> none  [the longest x1 2.35 us: on_device(): tgt = got[:, 4 * C, 0].astype(jnp.int32)]
    transpose x1 -> x0, local copies, waits for them, and re-layouts: 2.21 us -> none  [on_device(): weights = jnp.transpose(conv_weight, (0, 3, 1, 2, 4)).reshape(3 * C, 9 * C)]
    unnamed x16 -> x14, local copies, waits for them, and re-layouts: 4.95 us -> 5.3 us
  transfers between devices with their start and end apart: 6 -> 6, of which waited for: 0 -> 1; matrix products, arithmetic and copies ran while one was open for 6% -> 0% of each run, Pallas kernels for 10% -> 10%
where the time goes in v5:
time: 189 us
  blocking collectives  111 us (59%)
  Pallas kernels  47.8 us (25%)
  starting transfers between devices  17.7 us (9%)
  waiting for transfers between devices  6.04 us (3%)
  local copies, waits for them, and re-layouts  5.32 us (3%)
    all_to_all x1, blocking collectives, on_device(): lax.all_to_all(packed, ('views', 'bricks'), split_axis=0, concat_axis=0,...  111 us
    pallas_call x1, Pallas kernels, conv_inner(): pl.pallas_call(inner_kernel, in_specs=[vmem, vmem, vmem, hbm, hbm, hbm],...  18.8 us
    ppermute x6, starting transfers between devices, shift(): return lax.ppermute(array, axis, pairs)  17.7 us
    pallas_call x1, Pallas kernels, partials(): pl.pallas_call(partial_kernel, in_specs=[smem, smem, smem, vmem, vmem, vm...  10.3 us
    pallas_call x1, Pallas kernels, lift(): pl.pallas_call(lift_kernel, in_specs=[vmem], out_specs=[pl.BlockSpec(memo...  9.44 us
    pallas_call x1, Pallas kernels, conv_outer(): pl.pallas_call(outer_kernel, in_specs=[vmem] * 7 + [hbm] * 5, out_specs=h...  9.22 us
    ppermute x6, waiting for transfers between devices, shift(): return lax.ppermute(array, axis, pairs)  6.04 us
    unnamed x14, local copies, waits for them, and re-layouts  5.3 us
  transfers between devices with their start and end apart: 6, of which 1 were waited for; matrix products, arithmetic and copies ran while one was open for 0% of the time, Pallas kernels for 10%

profile of v5, /device:TPU:9, one launch (start us, length us, event | category | flops | bytes accessed | tf_op | source)
XLA Modules:
  0.0 188.8 jit_solution(8661175184947053764)
XLA Ops:
  0.7 0.0 copy-start.2
  0.7 1.0 copy-done.2
  1.7 0.0 copy-start.3
  1.7 0.9 copy-done.3
  2.6 0.0 copy-start.4
  2.6 0.7 copy-done.4
  3.3 0.0 copy-start.5
  3.3 0.7 copy-done.5
  3.9 0.0 copy-start.6
  3.9 0.7 copy-done.6
  4.6 10.3 %partials.1 = (bf16[128,264,128]{2,1,0:T(8,128)(2,1)}, bf16[192,576]{1,0:T(8,128)(2,1)S(1)}, f32[64,256]{1,0:T(8,128)S(1)}) custom-call(s32[128]{0:T(128)S(1)} %bitcast.18, s32[128]{0:T(128)S(1)} %bitcast.19, s32[1]{0:T(128)} %bitcast.15.count_ref, bf16[16,64,128]{2,1,0:T(8,128)(2,1)S(1)} %bitcast.17, bf16[27,64,64]{2,1,0:T(8,128)(2,1)S(1)} %bitcast.16, ...), custom_call_target="tpu_custom_call" | custom-call | tf_op jit(solution)/shard_map/partials/pallas_call | solution.py:84
  14.9 110.9 %all_to_all.5.part_ref = bf16[128,264,128]{2,1,0:T(8,128)(2,1)} all-to-all(bf16[128,264,128]{2,1,0:T(8,128)(2,1)} %get-tuple-element.20), channel_id=1, replica_groups=mesh['views'=8,'bricks'=16] {'views','bricks'}, dimensions={0} | all-to-all | bytes 17301504 | tf_op jit(solution)/shard_map/all_to_all | solution.py:474
  125.8 0.0 copy-start.1
  125.8 9.4 %lift.1 = (bf16[8,64,4096]{2,1,0:T(8,128)(2,1)}, bf16[2,64,4096]{2,1,0:T(8,128)(2,1)S(1)}, bf16[2,64,4096]{2,1,0:T(8,128)(2,1)S(1)}, bf16[8,64,256]{2,1,0:T(8,128)(2,1)S(1)}, bf16[8,64,256]{2,1,0:T(8,128)(2,1)S(1)}) custom-call(bf16[128,264,128]{2,1,0:T(8,128)(2,1)} %all_to_all.5.part_ref), custom_call_target="tpu_custom_call" | custom-call | tf_op jit(solution)/shard_map/lift/pallas_call | solution.py:151
  135.3 3.1 %collective-permute-start = (bf16[8,64,256]{2,1,0:T(8,128)(2,1)S(1)}, bf16[8,64,256]{2,1,0:T(8,128)(2,1)S(1)}, u32[]{:S(2)}, u32[]{:S(2)}) collective-permute-start(bf16[8,64,256]{2,1,0:T(8,128)(2,1)S(1)} %get-tuple-element.22), channel_id=1, source_target_pairs={{0,16},{16,32},{32,48},{48,64},{64,80},{80,96},{96,112},{1,17},{17... | collective-permute-start | bytes 786440 | tf_op jit(solution)/shard_map/ppermute | solution.py:457
  138.4 2.3 %collective-permute-start.2 = (bf16[2,64,4096]{2,1,0:T(8,128)(2,1)S(1)}, bf16[2,64,4096]{2,1,0:T(8,128)(2,1)S(1)}, u32[]{:S(2)}, u32[]{:S(2)}) collective-permute-start(bf16[2,64,4096]{2,1,0:T(8,128)(2,1)S(1)} %get-tuple-element.28), channel_id=1, source_target_pairs={{0,1},{1,2},{2,3},{3,4},{4,5},{5,6},{6,7},{7,8},{8,9},{9,10},{10,1... | collective-permute-start | bytes 3145736 | tf_op jit(solution)/shard_map/ppermute | solution.py:457
  140.7 5.1 %collective-permute-start.3 = (bf16[2,64,4096]{2,1,0:T(8,128)(2,1)S(1)}, bf16[2,64,4096]{2,1,0:T(8,128)(2,1)S(1)}, u32[]{:S(2)}, u32[]{:S(2)}) collective-permute-start(bf16[2,64,4096]{2,1,0:T(8,128)(2,1)S(1)} %get-tuple-element.29), channel_id=1, source_target_pairs={{1,0},{2,1},{3,2},{4,3},{5,4},{6,5},{7,6},{8,7},{9,8},{10,9},{11,1... | collective-permute-start | bytes 3145736 | tf_op jit(solution)/shard_map/ppermute | solution.py:457
  145.8 1.9 %collective-permute-start.1 = (bf16[8,64,256]{2,1,0:T(8,128)(2,1)S(1)}, bf16[8,64,256]{2,1,0:T(8,128)(2,1)S(1)}, u32[]{:S(2)}, u32[]{:S(2)}) collective-permute-start(bf16[8,64,256]{2,1,0:T(8,128)(2,1)S(1)} %get-tuple-element.23), channel_id=1, source_target_pairs={{16,0},{32,16},{48,32},{64,48},{80,64},{96,80},{112,96},{17,1},{33... | collective-permute-start | bytes 786440 | tf_op jit(solution)/shard_map/ppermute | solution.py:457
  147.7 0.0 collective-permute-done.ylo_ref
  147.8 6.0 %collective-permute-done.1.yhi_ref = bf16[8,64,256]{2,1,0:T(8,128)(2,1)S(1)} collective-permute-done((bf16[8,64,256]{2,1,0:T(8,128)(2,1)S(1)}, bf16[8,64,256]{2,1,0:T(8,128)(2,1)S(1)}, u32[]{:S(2)}, u32[]{:S(2)}) %collective-permute-start.1) | collective-permute-done | bytes 262176 | tf_op jit(solution)/shard_map/ppermute | solution.py:457
  153.8 1.9 %collective-permute-start.5 = (bf16[2,2,64,256]{3,2,1,0:T(8,128)(2,1)S(1)}, bf16[2,2,64,256]{3,2,1,0:T(8,128)(2,1)S(1)}, u32[]{:S(2)}, u32[]{:S(2)}) collective-permute-start(bf16[2,2,64,256]{3,2,1,0:T(8,128)(2,1)S(1)} %pad_maximum_fusion.1), channel_id=1, source_target_pairs={{1,0},{2,1},{3,2},{4,3},{5,4},{6,5},{7,6},{8,7},{9,8},{10,9},{11,1... | collective-permute-start | bytes 393224 | tf_op jit(solution)/shard_map/ppermute | solution.py:457
  155.8 3.4 %collective-permute-start.4 = (bf16[2,2,64,256]{3,2,1,0:T(8,128)(2,1)S(1)}, bf16[2,2,64,256]{3,2,1,0:T(8,128)(2,1)S(1)}, u32[]{:S(2)}, u32[]{:S(2)}) collective-permute-start(bf16[2,2,64,256]{3,2,1,0:T(8,128)(2,1)S(1)} %pad_maximum_fusion), channel_id=1, source_target_pairs={{0,1},{1,2},{2,3},{3,4},{4,5},{5,6},{6,7},{7,8},{8,9},{9,10},{10,1... | collective-permute-start | bytes 393224 | tf_op jit(solution)/shard_map/ppermute | solution.py:457
  159.1 0.0 copy-done.1
  159.2 18.8 %conv_inner.1 = (bf16[64,8,32,128]{3,2,1,0:T(8,128)(2,1)}, f32[2,64,4352]{2,1,0:T(8,128)}, f32[2,64,4352]{2,1,0:T(8,128)}, f32[2,64,4096]{2,1,0:T(8,128)S(1)}, f32[2,64,4096]{2,1,0:T(8,128)S(1)}) custom-call(bf16[192,576]{1,0:T(8,128)(2,1)S(1)} %get-tuple-element.18.w_ref, f32[64,256]{1,0:T(8,128)S(1)} %get-tuple-element.19.bias_ref, ...), custom_call_target="tpu_custom_call" | custom-call | tf_op jit(solution)/shard_map/conv_inner/pallas_call | solution.py:402
  178.0 0.0 copy-start
  178.0 1.4 copy-done
  179.3 0.0 collective-permute-done.5.chi_ref
  179.3 0.0 collective-permute-done.4.clo_ref
  179.3 0.0 collective-permute-done.2.xlo_ref
  179.4 0.0 collective-permute-done.3.xhi_ref
  179.4 9.2 %conv_outer.1 = bf16[64,8,32,128]{3,2,1,0:T(8,128)(2,1)} custom-call(bf16[192,576]{1,0:T(8,128)(2,1)S(1)} %get-tuple-element.18.w_ref, f32[64,256]{1,0:T(8,128)S(1)} %get-tuple-element.19.bias_ref, f32[8,32,128]{2,1,0:T(8,128)S(1)} %copy-done.1, f32[2,64,4352]{2,1,0:T(8,128)} %get-tuple-element.24.outer_ref, ...), custom_call_target="tpu_custom_call", output_to_operand_aliasing={{}: (11, {})} | custom-call | tf_op jit(solution)/shard_map/conv_outer/pallas_call | solution.py:435
  (4 shorter events, 0.1 us)
Async XLA Ops:
  0.7 1.0 copy-start.2
  1.7 0.9 copy-start.3
  2.6 0.7 copy-start.4
  3.3 0.7 copy-start.5
  3.9 0.7 copy-start.6
  125.8 33.3 %copy-start.1 = (f32[8,32,128]{2,1,0:T(8,128)S(1)}, f32[8,32,128]{2,1,0:T(8,128)}, u32[]{:S(2)}) copy-start(f32[8,32,128]{2,1,0:T(8,128)} %coef_ref.3) | copy-start | bytes 393220
  135.3 12.5 %collective-permute-start = (bf16[8,64,256]{2,1,0:T(8,128)(2,1)S(1)}, bf16[8,64,256]{2,1,0:T(8,128)(2,1)S(1)}, u32[]{:S(2)}, u32[]{:S(2)}) collective-permute-start(bf16[8,64,256]{2,1,0:T(8,128)(2,1)S(1)} %get-tuple-element.22), channel_id=1, source_target_pairs={{0,16},{16,32},{32,48},{48,64},{64,80},{80,96},{96,112},{1,17},{17... | collective-permute-start | bytes 786440 | tf_op jit(solution)/shard_map/ppermute | solution.py:457
  138.4 41.0 %collective-permute-start.2 = (bf16[2,64,4096]{2,1,0:T(8,128)(2,1)S(1)}, bf16[2,64,4096]{2,1,0:T(8,128)(2,1)S(1)}, u32[]{:S(2)}, u32[]{:S(2)}) collective-permute-start(bf16[2,64,4096]{2,1,0:T(8,128)(2,1)S(1)} %get-tuple-element.28), channel_id=1, source_target_pairs={{0,1},{1,2},{2,3},{3,4},{4,5},{5,6},{6,7},{7,8},{8,9},{9,10},{10,1... | collective-permute-start | bytes 3145736 | tf_op jit(solution)/shard_map/ppermute | solution.py:457
  140.7 38.7 %collective-permute-start.3 = (bf16[2,64,4096]{2,1,0:T(8,128)(2,1)S(1)}, bf16[2,64,4096]{2,1,0:T(8,128)(2,1)S(1)}, u32[]{:S(2)}, u32[]{:S(2)}) collective-permute-start(bf16[2,64,4096]{2,1,0:T(8,128)(2,1)S(1)} %get-tuple-element.29), channel_id=1, source_target_pairs={{1,0},{2,1},{3,2},{4,3},{5,4},{6,5},{7,6},{8,7},{9,8},{10,9},{11,1... | collective-permute-start | bytes 3145736 | tf_op jit(solution)/shard_map/ppermute | solution.py:457
  145.8 8.0 %collective-permute-start.1 = (bf16[8,64,256]{2,1,0:T(8,128)(2,1)S(1)}, bf16[8,64,256]{2,1,0:T(8,128)(2,1)S(1)}, u32[]{:S(2)}, u32[]{:S(2)}) collective-permute-start(bf16[8,64,256]{2,1,0:T(8,128)(2,1)S(1)} %get-tuple-element.23), channel_id=1, source_target_pairs={{16,0},{32,16},{48,32},{64,48},{80,64},{96,80},{112,96},{17,1},{33... | collective-permute-start | bytes 786440 | tf_op jit(solution)/shard_map/ppermute | solution.py:457
  153.8 25.5 %collective-permute-start.5 = (bf16[2,2,64,256]{3,2,1,0:T(8,128)(2,1)S(1)}, bf16[2,2,64,256]{3,2,1,0:T(8,128)(2,1)S(1)}, u32[]{:S(2)}, u32[]{:S(2)}) collective-permute-start(bf16[2,2,64,256]{3,2,1,0:T(8,128)(2,1)S(1)} %pad_maximum_fusion.1), channel_id=1, source_target_pairs={{1,0},{2,1},{3,2},{4,3},{5,4},{6,5},{7,6},{8,7},{9,8},{10,9},{11,1... | collective-permute-start | bytes 393224 | tf_op jit(solution)/shard_map/ppermute | solution.py:457
  155.8 23.6 %collective-permute-start.4 = (bf16[2,2,64,256]{3,2,1,0:T(8,128)(2,1)S(1)}, bf16[2,2,64,256]{3,2,1,0:T(8,128)(2,1)S(1)}, u32[]{:S(2)}, u32[]{:S(2)}) collective-permute-start(bf16[2,2,64,256]{3,2,1,0:T(8,128)(2,1)S(1)} %pad_maximum_fusion), channel_id=1, source_target_pairs={{0,1},{1,2},{2,3},{3,4},{4,5},{5,6},{6,7},{7,8},{8,9},{9,10},{10,1... | collective-permute-start | bytes 393224 | tf_op jit(solution)/shard_map/ppermute | solution.py:457
  178.0 1.4 copy-start

commit v6 on v5

--- a/solution.py
+++ b/solution.py
@@ -18,6 +18,7 @@
 WIDE = (BY + 4) * Z
 GATED = (BY + 2) * Z
 SEND = 16
+LIMIT = 32
 PACK = 4 * C + 8
 PITCH = 40
 
@@ -25,7 +26,7 @@
 def partial_kernel(
     pixel_ref, voxel_ref, count_ref, feats_ref, cw_ref, cb_ref, tiles_ref,
     out_ref, w_ref, bias_ref,
-    tiles, out, sems, done,
+    tiles, out, feats, cw, sems, done, small,
 ):
     chunks = tiles.shape[0] // SEND
 
@@ -37,13 +38,21 @@
         rows = pl.ds(pl.multiple_of(k * SEND, SEND), SEND)
         return pltpu.make_async_copy(out.at[rows], out_ref.at[rows], done.at[k])
 
+    early = [
+        pltpu.make_async_copy(cw_ref, cw, small.at[0]),
+        pltpu.make_async_copy(feats_ref, feats, small.at[1]),
+    ]
+    for copy in early:
+        copy.start()
     for k in range(chunks):
         load(k).start()
+    for copy in early:
+        copy.wait()
 
     taps = 9
     for dx in range(3):
         for q in range(0, taps, 2):
-            pieces = [cw_ref[dx * taps + r] for r in range(q, min(q + 2, taps))]
+            pieces = [cw[dx * taps + r] for r in range(q, min(q + 2, taps))]
             both = pieces[0] if len(pieces) == 1 else jnp.concatenate(pieces, axis=1)
             w_ref[dx * C : (dx + 1) * C, q * C : q * C + both.shape[1]] = both
     eye = lax.broadcasted_iota(jnp.int32, (C, C), 0) == lax.broadcasted_iota(jnp.int32, (C, C), 1)
@@ -59,7 +68,7 @@
         for i in range(SEND):
             slot = k * SEND + i
             p = jnp.dot(
-                feats_ref[pixel_ref[slot]], tiles[slot], preferred_element_type=jnp.float32
+                feats[pixel_ref[slot]], tiles[slot], preferred_element_type=jnp.float32
             )
             for q in range(4):
                 out[slot, q * C : (q + 1) * C, :] = p[:, q * Z : (q + 1) * Z].astype(jnp.bfloat16)
@@ -83,13 +92,16 @@
     hbm = pl.BlockSpec(memory_space=pl.ANY)
     return pl.pallas_call(
         partial_kernel,
-        in_specs=[smem, smem, smem, vmem, vmem, vmem, hbm],
+        in_specs=[smem, smem, smem, hbm, hbm, vmem, hbm],
         out_specs=[hbm, vmem, vmem],
         scratch_shapes=[
             pltpu.VMEM((n, PIX, VOXB), jnp.bfloat16),
             pltpu.VMEM((n, PACK, Z), jnp.bfloat16),
+            pltpu.VMEM(feats.shape, jnp.bfloat16),
+            pltpu.VMEM(conv_weight.shape, jnp.bfloat16),
             pltpu.SemaphoreType.DMA((n // SEND,)),
             pltpu.SemaphoreType.DMA((n // SEND,)),
+            pltpu.SemaphoreType.DMA((2,)),
         ],
         out_shape=[
             jax.ShapeDtypeStruct((n, PACK, Z), jnp.bfloat16),
@@ -102,7 +114,8 @@
 
 
 def lift_kernel(
-    part_ref, main_ref, lo_ref, hi_ref, ylo_ref, yhi_ref, acc, rows, ids, tgt_ref, sem, done
+    part_ref, main_ref, lo_ref, hi_ref, ylo_ref, yhi_ref, ll_ref, lh_ref, hl_ref, hh_ref,
+    acc, ids, tgt_ref, sem,
 ):
     n = part_ref.shape[0]
     lane = lax.broadcasted_iota(jnp.int32, (8, Z), 1)
@@ -126,24 +139,27 @@
 
     lax.fori_loop(0, n, add, 0)
 
-    stores = [pltpu.make_async_copy(rows.at[x], main_ref.at[x], done.at[x]) for x in range(BX)]
     for x in range(BX):
         for y in range(BY):
             v = acc[x * (BY // 4) + y // 4, (y % 4) * C : (y % 4 + 1) * C, :]
             v = jnp.maximum(v, 0.0).astype(jnp.bfloat16)
             cols = slice(y * Z, (y + 1) * Z)
-            rows[x, :, cols] = v
+            main_ref[x, :, cols] = v
             if x < 2:
                 lo_ref[x, :, cols] = v
             if x >= BX - 2:
                 hi_ref[x - BX + 2, :, cols] = v
-            if y < 2:
-                ylo_ref[x, :, cols] = v
-            if y >= BY - 2:
-                yhi_ref[x, :, (y - BY + 2) * Z : (y - BY + 3) * Z] = v
-        stores[x].start()
-    for copy in stores:
-        copy.wait()
+            for inside_y, first, face, low, high in (
+                (y < 2, 0, ylo_ref, ll_ref, hl_ref),
+                (y >= BY - 2, BY - 2, yhi_ref, lh_ref, hh_ref),
+            ):
+                if inside_y:
+                    strip = slice((y - first) * Z, (y - first + 1) * Z)
+                    face[x, :, strip] = v
+                    if x < 2:
+                        low[x, :, strip] = v
+                    if x >= BX - 2:
+                        high[x - BX + 2, :, strip] = v
 
 
 def lift(part):
@@ -151,14 +167,12 @@
     return pl.pallas_call(
         lift_kernel,
         in_specs=[vmem],
-        out_specs=[pl.BlockSpec(memory_space=pl.ANY)] + [vmem] * 4,
+        out_specs=[vmem] * 9,
         scratch_shapes=[
             pltpu.VMEM((BLK, 4 * C, Z), jnp.float32),
-            pltpu.VMEM((BX, C, ROW), jnp.bfloat16),
             pltpu.VMEM((8, Z), jnp.int32),
             pltpu.SMEM((8, Z), jnp.int32),
             pltpu.SemaphoreType.DMA,
-            pltpu.SemaphoreType.DMA((BX,)),
         ],
         out_shape=[
             jax.ShapeDtypeStruct((BX, C, ROW), jnp.bfloat16),
@@ -166,8 +180,9 @@
             jax.ShapeDtypeStruct((2, C, ROW), jnp.bfloat16),
             jax.ShapeDtypeStruct((BX, C, 2 * Z), jnp.bfloat16),
             jax.ShapeDtypeStruct((BX, C, 2 * Z), jnp.bfloat16),
-        ],
-        compiler_params=pltpu.CompilerParams(vmem_limit_bytes=48 << 20),
+        ]
+        + [jax.ShapeDtypeStruct((2, C, 2 * Z), jnp.bfloat16)] * 4,
+        compiler_params=pltpu.CompilerParams(vmem_limit_bytes=32 << 20),
         name="lift",
     )(part)
 
@@ -196,9 +211,15 @@
     return lane == 0, lane == Z - 1
 
 
-def stage(raw, p, xs, y, ends):
+def stage(pieces, xs, y, ends):
     cols = slice(y * Z, (y + 1) * Z)
-    v = raw[p, :, cols]
+    left, mid, right = pieces
+    if y < 2:
+        v = left[:, y * Z : (y + 1) * Z]
+    elif y < BY + 2:
+        v = mid[:, (y - 2) * Z : (y - 1) * Z]
+    else:
+        v = right[:, (y - BY - 2) * Z : (y - BY - 1) * Z]
     down, up = shifted(v.astype(jnp.float32), *ends)
     xs[0:C, cols] = down.astype(jnp.bfloat16)
     xs[C : 2 * C, cols] = v
@@ -224,49 +245,30 @@
     return rows
 
 
-def plane_copies(left, mid, right, to, sems):
-    return [
-        pltpu.make_async_copy(left, to.at[:, 0 : 2 * Z], sems.at[0]),
-        pltpu.make_async_copy(mid, to.at[:, 2 * Z : 2 * Z + ROW], sems.at[1]),
-        pltpu.make_async_copy(right, to.at[:, 2 * Z + ROW : WIDE], sems.at[2]),
-    ]
-
-
 def inner_kernel(
     w_ref, bias_ref, coef_ref, main_ref, ylo_ref, yhi_ref,
     out_ref, outer_ref, edge_ref, near_ref, pend_ref,
-    raw, xs_a, xs_b, acc_a, acc_b, prev, pend, flat_a, flat_b, packed, sems, done,
+    xs_a, xs_b, acc_a, acc_b, prev, pend, flat_a, flat_b, packed, done,
 ):
     ends, flags = edges(), inside()
-    copies = [
-        plane_copies(ylo_ref.at[x], main_ref.at[x], yhi_ref.at[x], raw.at[x], sems.at[x])
-        for x in range(BX)
-    ]
+    pieces = [(ylo_ref.at[x], main_ref.at[x], yhi_ref.at[x]) for x in range(BX)]
     stores = [
         pltpu.make_async_copy(packed.at[k], out_ref.at[:, k + 2], done.at[k])
         for k in range(BX - 4)
     ]
-    for group in copies:
-        for copy in group:
-            copy.start()
     bias = bias_ref[...]
     weights = w_ref[...]
     buffers, flats = (xs_a, xs_b), (flat_a, flat_b)
-    for copy in copies[0]:
-        copy.wait()
     for y in range(BY + 4):
-        stage(raw, 0, xs_a, y, ends)
+        stage(pieces[0], xs_a, y, ends)
     for x in range(BX):
         xs, xs_next, flat = buffers[x % 2], buffers[(x + 1) % 2], flats[x % 2]
-        if x + 1 < BX:
-            for copy in copies[x + 1]:
-                copy.wait()
         new = x - 1
         before = None
         for t in range((BY + 2) // 2):
             if x + 1 < BX:
                 for y in stage_rows(t):
-                    stage(raw, x + 1, xs_next, y, ends)
+                    stage(pieces[x + 1], xs_next, y, ends)
             cols = slice(t * 2 * Z, (t + 1) * 2 * Z)
             p = jnp.dot(weights, window(xs, t), preferred_element_type=jnp.float32)
             if x == 0:
@@ -319,20 +321,20 @@
 
 def outer_kernel(
     w_ref, bias_ref, coef_ref, outer_ref, edge_ref, near_ref, pend_ref,
-    xlo_ref, xhi_ref, clo_ref, chi_ref, part_ref,
+    xlo_ref, xhi_ref, ll_ref, lh_ref, hl_ref, hh_ref, part_ref,
     out_ref,
-    raw, xs_0, xs_1, xs_2, xs_3, flat_a, flat_b, packed, sems, done,
+    xs_0, xs_1, xs_2, xs_3, flat_a, flat_b, packed, done,
 ):
     ends, flags = edges(), inside()
-    copies = []
-    for p, (face, corner, q) in enumerate(
-        [(xlo_ref, clo_ref, 0), (xlo_ref, clo_ref, 1), (xhi_ref, chi_ref, 1), (xhi_ref, chi_ref, 0)]
-    ):
-        copies.append(
-            plane_copies(corner.at[0, q], face.at[q], corner.at[1, q], raw.at[p], sems.at[p])
+    pieces = [
+        (left.at[q], face.at[q], right.at[q])
+        for left, face, right, q in (
+            (ll_ref, xlo_ref, lh_ref, 0),
+            (ll_ref, xlo_ref, lh_ref, 1),
+            (hl_ref, xhi_ref, hh_ref, 1),
+            (hl_ref, xhi_ref, hh_ref, 0),
         )
-        for copy in copies[p]:
-            copy.start()
+    ]
     targets = [(0, 1), (BX - 1, BX - 2)]
     stores = [
         [
@@ -344,25 +346,19 @@
     bias = bias_ref[...]
     planes = (xs_0, xs_1, xs_2, xs_3)
     for p in range(2):
-        for copy in copies[p]:
-            copy.wait()
         for y in range(BY + 4):
-            stage(raw, p, planes[p], y, ends)
+            stage(pieces[p], planes[p], y, ends)
     for s in range(2):
         far, nearer = planes[2 * s], planes[2 * s + 1]
         w_side = w_ref[2 * s * C : (2 * s + 1) * C]
         w_both = jnp.concatenate([w_ref[C : 2 * C], w_side], axis=0)
         e, i = targets[s]
-        if s == 0:
-            for p in (2, 3):
-                for copy in copies[p]:
-                    copy.wait()
         before = None
         for t in range((BY + 2) // 2):
             if s == 0:
                 for p in (2, 3):
                     for y in stage_rows(t):
-                        stage(raw, p, planes[p], y, ends)
+                        stage(pieces[p], planes[p], y, ends)
             cols = slice(t * 2 * Z, (t + 1) * 2 * Z)
             a = jnp.dot(w_side, window(far, t), preferred_element_type=jnp.float32)
             b = jnp.dot(w_both, window(nearer, t), preferred_element_type=jnp.float32)
@@ -401,10 +397,9 @@
     state = lambda width: jax.ShapeDtypeStruct((2, C, width), jnp.float32)
     return pl.pallas_call(
         inner_kernel,
-        in_specs=[vmem, vmem, vmem, hbm, hbm, hbm],
+        in_specs=[vmem] * 6,
         out_specs=[hbm] + [vmem] * 4,
         scratch_shapes=[
-            pltpu.VMEM((BX, C, WIDE), jnp.bfloat16),
             pltpu.VMEM((3 * C, WIDE), jnp.bfloat16),
             pltpu.VMEM((3 * C, WIDE), jnp.bfloat16),
             pltpu.VMEM((C, GATED), jnp.float32),
@@ -414,7 +409,6 @@
             pltpu.VMEM((C * PITCH, Z), jnp.float32),
             pltpu.VMEM((C * PITCH, Z), jnp.float32),
             pltpu.VMEM((BX - 4, C, BY, Z), jnp.bfloat16),
-            pltpu.SemaphoreType.DMA((BX, 3)),
             pltpu.SemaphoreType.DMA((BX - 4,)),
         ],
         out_shape=[
@@ -424,37 +418,40 @@
             state(ROW),
             state(ROW),
         ],
-        compiler_params=pltpu.CompilerParams(vmem_limit_bytes=48 << 20),
+        compiler_params=pltpu.CompilerParams(vmem_limit_bytes=LIMIT << 20),
         name="conv_inner",
     )(weights, bias, coef, main, ylo, yhi)
 
 
-def conv_outer(weights, bias, coef, state, xlo, xhi, clo, chi, volume):
+def conv_outer(weights, bias, coef, state, faces, corners, volume):
     hbm = pl.BlockSpec(memory_space=pl.ANY)
     vmem = pl.BlockSpec(memory_space=pltpu.VMEM)
     return pl.pallas_call(
         outer_kernel,
-        in_specs=[vmem] * 7 + [hbm] * 5,
+        in_specs=[vmem] * 13 + [hbm],
         out_specs=hbm,
-        scratch_shapes=[pltpu.VMEM((4, C, WIDE), jnp.bfloat16)]
-        + [pltpu.VMEM((3 * C, WIDE), jnp.bfloat16)] * 4
+        scratch_shapes=[pltpu.VMEM((3 * C, WIDE), jnp.bfloat16)] * 4
         + [pltpu.VMEM((C * PITCH, Z), jnp.float32)] * 2
         + [
             pltpu.VMEM((4, C, BY, Z), jnp.bfloat16),
-            pltpu.SemaphoreType.DMA((4, 3)),
             pltpu.SemaphoreType.DMA((2, 2)),
         ],
         out_shape=jax.ShapeDtypeStruct((C, BX, BY, Z), jnp.bfloat16),
-        input_output_aliases={11: 0},
-        compiler_params=pltpu.CompilerParams(vmem_limit_bytes=48 << 20),
+        input_output_aliases={13: 0},
+        compiler_params=pltpu.CompilerParams(vmem_limit_bytes=LIMIT << 20),
         name="conv_outer",
-    )(weights, bias, coef, *state, xlo, xhi, clo, chi, volume)
-
-
-def shift(array, axis, by):
-    size = lax.axis_size(axis)
-    pairs = [(i, i + by) for i in range(size) if 0 <= i + by < size]
-    return lax.ppermute(array, axis, pairs)
+    )(weights, bias, coef, *state, *faces, *corners, volume)
+
+
+def shift(array, along_y, along_x):
+    views, bricks = lax.axis_size("views"), lax.axis_size("bricks")
+    pairs = [
+        (v * bricks + b, (v + along_y) * bricks + b + along_x)
+        for v in range(views)
+        for b in range(bricks)
+        if 0 <= v + along_y < views and 0 <= b + along_x < bricks
+    ]
+    return lax.ppermute(array, ("views", "bricks"), pairs)
 
 
 def on_device(
@@ -472,15 +469,13 @@
         tiles,
     )
     got = lax.all_to_all(packed, ("views", "bricks"), split_axis=0, concat_axis=0, tiled=True)
-    main, lo, hi, ylo, yhi = lift(got)
-    from_low = shift(yhi, "views", 1)
-    from_high = shift(ylo, "views", -1)
-    xlo = shift(hi, "bricks", 1)
-    xhi = shift(lo, "bricks", -1)
-    clo = shift(jnp.stack([from_low[BX - 2 :], from_high[BX - 2 :]]), "bricks", 1)
-    chi = shift(jnp.stack([from_low[:2], from_high[:2]]), "bricks", -1)
+    main, lo, hi, ylo, yhi, ll, lh, hl, hh = lift(got)
+    from_low = shift(yhi, 1, 0)
+    from_high = shift(ylo, -1, 0)
+    faces = shift(hi, 0, 1), shift(lo, 0, -1)
+    corners = shift(hh, 1, 1), shift(hl, -1, 1), shift(lh, 1, -1), shift(ll, -1, -1)
     volume, *state = conv_inner(weights, bias, smooth_coef, main, from_low, from_high)
-    return conv_outer(weights, bias, smooth_coef, state, xlo, xhi, clo, chi, volume)
+    return conv_outer(weights, bias, smooth_coef, state, faces, corners, volume)
 
 
 def solution(mesh):

time: 189 us -> 193 us (1.021)
  Pallas kernels: 47.8 us -> 35.9 us
  waiting for transfers between devices: 6.04 us -> 15.3 us
  starting transfers between devices: 17.7 us -> 25.6 us
    pallas_call x4, Pallas kernels: 47.8 us -> 35.9 us  [the longest x1 14.5 us: conv_inner(): pl.pallas_call(inner_kernel, in_specs=[vmem] * 6, out_specs=[hbm] + [vmem...]
    ppermute x6 -> x8, waiting for transfers between devices: 6.04 us -> 15.3 us  [shift(): return lax.ppermute(array, ('views', 'bricks'), pairs)]
    ppermute x6 -> x8, starting transfers between devices: 17.7 us -> 25.6 us  [shift(): return lax.ppermute(array, ('views', 'bricks'), pairs)]
    unnamed x14 -> x12, local copies, waits for them, and re-layouts: 5.3 us -> 3.92 us
  transfers between devices with their start and end apart: 6 -> 8, of which waited for: 1 -> 1; matrix products, arithmetic and copies ran while one was open for 0% -> 0% of each run, Pallas kernels for 10% -> 8%
where the time goes in v6:
time: 193 us
  blocking collectives  111 us (58%)
  Pallas kernels  35.9 us (19%)
  starting transfers between devices  25.6 us (13%)
  waiting for transfers between devices  15.3 us (8%)
  local copies, waits for them, and re-layouts  3.92 us (2%)
    all_to_all x1, blocking collectives, on_device(): lax.all_to_all(packed, ('views', 'bricks'), split_axis=0, concat_axis=0,...  111 us
    ppermute x8, starting transfers between devices, shift(): return lax.ppermute(array, ('views', 'bricks'), pairs)  25.6 us
    ppermute x8, waiting for transfers between devices, shift(): return lax.ppermute(array, ('views', 'bricks'), pairs)  15.3 us
    pallas_call x1, Pallas kernels, conv_inner(): pl.pallas_call(inner_kernel, in_specs=[vmem] * 6, out_specs=[hbm] + [vmem...  14.5 us
    pallas_call x1, Pallas kernels, partials(): pl.pallas_call(partial_kernel, in_specs=[smem, smem, smem, hbm, hbm, vmem...  10.7 us
    pallas_call x1, Pallas kernels, conv_outer(): pl.pallas_call(outer_kernel, in_specs=[vmem] * 13 + [hbm], out_specs=hbm,...  5.81 us
    pallas_call x1, Pallas kernels, lift(): pl.pallas_call(lift_kernel, in_specs=[vmem], out_specs=[vmem] * 9, scratc...  4.88 us
    unnamed x12, local copies, waits for them, and re-layouts  3.92 us
  transfers between devices with their start and end apart: 8, of which 1 were waited for; matrix products, arithmetic and copies ran while one was open for 0% of the time, Pallas kernels for 8%

profile of v6, /device:TPU:9, one launch (start us, length us, event | category | flops | bytes accessed | tf_op | source)
XLA Modules:
  0.0 192.5 jit_solution(1541307531791244448)
XLA Ops:
  0.7 0.0 copy-start.1
  0.7 1.0 copy-done.1
  1.7 0.0 copy-start.2
  1.7 0.9 copy-done.2
  2.6 0.0 copy-start.3
  2.6 0.7 copy-done.3
  3.3 0.0 copy-start.4
  3.3 0.7 copy-done.4
  3.9 0.0 copy-start.5
  3.9 0.7 copy-done.5
  4.6 10.7 %partials.1 = (bf16[128,264,128]{2,1,0:T(8,128)(2,1)}, bf16[192,576]{1,0:T(8,128)(2,1)S(1)}, f32[64,256]{1,0:T(8,128)S(1)}) custom-call(s32[128]{0:T(128)S(1)} %bitcast.10, s32[128]{0:T(128)S(1)} %bitcast.11, s32[1]{0:T(128)} %bitcast.7.count_ref, bf16[16,64,128]{2,1,0:T(8,128)(2,1)S(1)} %bitcast.9, bf16[27,64,64]{2,1,0:T(8,128)(2,1)S(1)} %bitcast.8, ...), custom_call_target="tpu_custom_call" | custom-call | tf_op jit(solution)/shard_map/partials/pallas_call | solution.py:93
  15.3 110.8 %all_to_all.5.part_ref = bf16[128,264,128]{2,1,0:T(8,128)(2,1)S(1)} all-to-all(bf16[128,264,128]{2,1,0:T(8,128)(2,1)} %get-tuple-element.24), channel_id=1, replica_groups=mesh['views'=8,'bricks'=16] {'views','bricks'}, dimensions={0} | all-to-all | bytes 17301504 | tf_op jit(solution)/shard_map/all_to_all | solution.py:471
  126.1 0.0 copy-start
  126.1 4.9 %lift.1 = (bf16[8,64,4096]{2,1,0:T(8,128)(2,1)S(1)}, bf16[2,64,4096]{2,1,0:T(8,128)(2,1)S(1)}, bf16[2,64,4096]{2,1,0:T(8,128)(2,1)S(1)}, bf16[8,64,256]{2,1,0:T(...) custom-call(bf16[128,264,128]{2,1,0:T(8,128)(2,1)S(1)} %all_to_all.5, ...), custom_call_target="tpu_custom_call" | custom-call | tf_op jit(solution)/shard_map/lift/pallas_call | solution.py:167
  131.0 2.2 %collective-permute-start.2 = (bf16[2,64,4096]{2,1,0:T(8,128)(2,1)S(1)}, bf16[2,64,4096]{2,1,0:T(8,128)(2,1)S(1)}, u32[]{:S(2)}, u32[]{:S(2)}) collective-permute-start(bf16[2,64,4096]{2,1,0:T(8,128)(2,1)S(1)} %get-tuple-element.32), channel_id=1, source_target_pairs={{0,1},{1,2},{2,3},{3,4},{4,5},{5,6},{6,7},{7,8},{8,9},{9,10},{10,1... | collective-permute-start | bytes 3145736 | tf_op jit(solution)/shard_map/ppermute | solution.py:454
  133.2 5.2 %collective-permute-start.3 = (bf16[2,64,4096]{2,1,0:T(8,128)(2,1)S(1)}, bf16[2,64,4096]{2,1,0:T(8,128)(2,1)S(1)}, u32[]{:S(2)}, u32[]{:S(2)}) collective-permute-start(bf16[2,64,4096]{2,1,0:T(8,128)(2,1)S(1)} %get-tuple-element.33), channel_id=1, source_target_pairs={{1,0},{2,1},{3,2},{4,3},{5,4},{6,5},{7,6},{8,7},{9,8},{10,9},{11,1... | collective-permute-start | bytes 3145736 | tf_op jit(solution)/shard_map/ppermute | solution.py:454
  138.4 3.7 %collective-permute-start = (bf16[8,64,256]{2,1,0:T(8,128)(2,1)S(1)}, bf16[8,64,256]{2,1,0:T(8,128)(2,1)S(1)}, u32[]{:S(2)}, u32[]{:S(2)}) collective-permute-start(bf16[8,64,256]{2,1,0:T(8,128)(2,1)S(1)} %get-tuple-element.26), channel_id=1, source_target_pairs={{0,16},{1,17},{2,18},{3,19},{4,20},{5,21},{6,22},{7,23},{8,24},{9,... | collective-permute-start | bytes 786440 | tf_op jit(solution)/shard_map/ppermute | solution.py:454
  142.1 1.9 collective-permute-start.1
  144.0 1.9 collective-permute-start.4
  145.9 15.3 %collective-permute-done.4.ll_ref = bf16[2,64,256]{2,1,0:T(8,128)(2,1)S(1)} collective-permute-done((bf16[2,64,256]{2,1,0:T(8,128)(2,1)S(1)}, bf16[2,64,256]{2,1,0:T(8,128)(2,1)S(1)}, u32[]{:S(2)}, u32[]{:S(2)}) %collective-permute-start.4) | collective-permute-done | bytes 65568 | tf_op jit(solution)/shard_map/ppermute | solution.py:454
  161.3 1.9 collective-permute-start.5
  163.2 0.0 collective-permute-done.ylo_ref
  163.2 6.7 %collective-permute-start.6 = (bf16[2,64,256]{2,1,0:T(8,128)(2,1)S(1)}, bf16[2,64,256]{2,1,0:T(8,128)(2,1)S(1)}, u32[]{:S(2)}, u32[]{:S(2)}) collective-permute-start(bf16[2,64,256]{2,1,0:T(8,128)(2,1)S(1)} %get-tuple-element.36), channel_id=1, source_target_pairs={{1,16},{2,17},{3,18},{4,19},{5,20},{6,21},{7,22},{8,23},{9,24},{10... | collective-permute-start | bytes 196616 | tf_op jit(solution)/shard_map/ppermute | solution.py:454
  169.8 0.0 collective-permute-done.1.yhi_ref
  169.9 2.1 %collective-permute-start.7 = (bf16[2,64,256]{2,1,0:T(8,128)(2,1)S(1)}, bf16[2,64,256]{2,1,0:T(8,128)(2,1)S(1)}, u32[]{:S(2)}, u32[]{:S(2)}) collective-permute-start(bf16[2,64,256]{2,1,0:T(8,128)(2,1)S(1)} %get-tuple-element.37), channel_id=1, source_target_pairs={{17,0},{18,1},{19,2},{20,3},{21,4},{22,5},{23,6},{24,7},{25,8},{26... | collective-permute-start | bytes 196616 | tf_op jit(solution)/shard_map/ppermute | solution.py:454
  172.0 0.0 copy-done
  172.0 14.5 %conv_inner.1 = (bf16[64,8,32,128]{3,2,1,0:T(8,128)(2,1)}, f32[2,64,4352]{2,1,0:T(8,128)S(1)}, f32[2,64,4352]{2,1,0:T(8,128)S(1)}, f32[2,64,4096]{2,1,0:T(8,128)S(1)}, f32[2,64,4096]{2,1,0:T(8,128)S(1)}) custom-call(bf16[192,576]{1,0:T(8,128)(2,1)S(1)} %get-tuple-element.22.w_ref, f32[64,256]{1,0:T(8,128)S(1)} %get-tuple-element.23.bias_ref, ...), custom_call_target="tpu_custom_call" | custom-call | tf_op jit(solution)/shard_map/conv_inner/pallas_call | solution.py:398
  186.5 0.0 collective-permute-done.5.lh_ref
  186.5 0.0 collective-permute-done.6.hl_ref
  186.5 0.0 collective-permute-done.7.hh_ref
  186.5 0.0 collective-permute-done.2.xlo_ref
  186.5 0.0 collective-permute-done.3.xhi_ref
  186.5 5.8 %conv_outer.1 = bf16[64,8,32,128]{3,2,1,0:T(8,128)(2,1)} custom-call(bf16[192,576]{1,0:T(8,128)(2,1)S(1)} %get-tuple-element.22.w_ref, f32[64,256]{1,0:T(8,128)S(1)} %get-tuple-element.23.bias_ref, f32[8,32,128]{2,1,0:T(8,128)S(1)} %copy-done, f32[2,64,4352]{2,1,0:T(8,128)S(1)} %get-tuple-element.28.outer_ref, ...), custom_call_target="tpu_custom_call", output_to_operand_aliasing={{}: (13, {})} | custom-call | tf_op jit(solution)/shard_map/conv_outer/pallas_call | solution.py:429
Async XLA Ops:
  0.7 1.0 copy-start.1
  1.7 0.9 copy-start.2
  2.6 0.7 copy-start.3
  3.3 0.7 copy-start.4
  3.9 0.7 copy-start.5
  126.1 45.9 %copy-start = (f32[8,32,128]{2,1,0:T(8,128)S(1)}, f32[8,32,128]{2,1,0:T(8,128)}, u32[]{:S(2)}) copy-start(f32[8,32,128]{2,1,0:T(8,128)} %coef_ref.3) | copy-start | bytes 393220
  131.0 55.5 %collective-permute-start.2 = (bf16[2,64,4096]{2,1,0:T(8,128)(2,1)S(1)}, bf16[2,64,4096]{2,1,0:T(8,128)(2,1)S(1)}, u32[]{:S(2)}, u32[]{:S(2)}) collective-permute-start(bf16[2,64,4096]{2,1,0:T(8,128)(2,1)S(1)} %get-tuple-element.32), channel_id=1, source_target_pairs={{0,1},{1,2},{2,3},{3,4},{4,5},{5,6},{6,7},{7,8},{8,9},{9,10},{10,1... | collective-permute-start | bytes 3145736 | tf_op jit(solution)/shard_map/ppermute | solution.py:454
  133.2 53.3 %collective-permute-start.3 = (bf16[2,64,4096]{2,1,0:T(8,128)(2,1)S(1)}, bf16[2,64,4096]{2,1,0:T(8,128)(2,1)S(1)}, u32[]{:S(2)}, u32[]{:S(2)}) collective-permute-start(bf16[2,64,4096]{2,1,0:T(8,128)(2,1)S(1)} %get-tuple-element.33), channel_id=1, source_target_pairs={{1,0},{2,1},{3,2},{4,3},{5,4},{6,5},{7,6},{8,7},{9,8},{10,9},{11,1... | collective-permute-start | bytes 3145736 | tf_op jit(solution)/shard_map/ppermute | solution.py:454
  138.4 24.8 %collective-permute-start = (bf16[8,64,256]{2,1,0:T(8,128)(2,1)S(1)}, bf16[8,64,256]{2,1,0:T(8,128)(2,1)S(1)}, u32[]{:S(2)}, u32[]{:S(2)}) collective-permute-start(bf16[8,64,256]{2,1,0:T(8,128)(2,1)S(1)} %get-tuple-element.26), channel_id=1, source_target_pairs={{0,16},{1,17},{2,18},{3,19},{4,20},{5,21},{6,22},{7,23},{8,24},{9,... | collective-permute-start | bytes 786440 | tf_op jit(solution)/shard_map/ppermute | solution.py:454
  142.1 27.8 %collective-permute-start.1 = (bf16[8,64,256]{2,1,0:T(8,128)(2,1)S(1)}, bf16[8,64,256]{2,1,0:T(8,128)(2,1)S(1)}, u32[]{:S(2)}, u32[]{:S(2)}) collective-permute-start(bf16[8,64,256]{2,1,0:T(8,128)(2,1)S(1)} %get-tuple-element.27), channel_id=1, source_target_pairs={{16,0},{17,1},{18,2},{19,3},{20,4},{21,5},{22,6},{23,7},{24,8},{25... | collective-permute-start | bytes 786440 | tf_op jit(solution)/shard_map/ppermute | solution.py:454
  144.0 17.3 %collective-permute-start.4 = (bf16[2,64,256]{2,1,0:T(8,128)(2,1)S(1)}, bf16[2,64,256]{2,1,0:T(8,128)(2,1)S(1)}, u32[]{:S(2)}, u32[]{:S(2)}) collective-permute-start(bf16[2,64,256]{2,1,0:T(8,128)(2,1)S(1)} %get-tuple-element.34), channel_id=1, source_target_pairs={{0,17},{1,18},{2,19},{3,20},{4,21},{5,22},{6,23},{7,24},{8,25},{9,... | collective-permute-start | bytes 196616 | tf_op jit(solution)/shard_map/ppermute | solution.py:454
  161.3 25.2 %collective-permute-start.5 = (bf16[2,64,256]{2,1,0:T(8,128)(2,1)S(1)}, bf16[2,64,256]{2,1,0:T(8,128)(2,1)S(1)}, u32[]{:S(2)}, u32[]{:S(2)}) collective-permute-start(bf16[2,64,256]{2,1,0:T(8,128)(2,1)S(1)} %get-tuple-element.35), channel_id=1, source_target_pairs={{16,1},{17,2},{18,3},{19,4},{20,5},{21,6},{22,7},{23,8},{24,9},{25... | collective-permute-start | bytes 196616 | tf_op jit(solution)/shard_map/ppermute | solution.py:454
  163.2 23.3 %collective-permute-start.6 = (bf16[2,64,256]{2,1,0:T(8,128)(2,1)S(1)}, bf16[2,64,256]{2,1,0:T(8,128)(2,1)S(1)}, u32[]{:S(2)}, u32[]{:S(2)}) collective-permute-start(bf16[2,64,256]{2,1,0:T(8,128)(2,1)S(1)} %get-tuple-element.36), channel_id=1, source_target_pairs={{1,16},{2,17},{3,18},{4,19},{5,20},{6,21},{7,22},{8,23},{9,24},{10... | collective-permute-start | bytes 196616 | tf_op jit(solution)/shard_map/ppermute | solution.py:454
  169.9 16.6 %collective-permute-start.7 = (bf16[2,64,256]{2,1,0:T(8,128)(2,1)S(1)}, bf16[2,64,256]{2,1,0:T(8,128)(2,1)S(1)}, u32[]{:S(2)}, u32[]{:S(2)}) collective-permute-start(bf16[2,64,256]{2,1,0:T(8,128)(2,1)S(1)} %get-tuple-element.37), channel_id=1, source_target_pairs={{17,0},{18,1},{19,2},{20,3},{21,4},{22,5},{23,6},{24,7},{25,8},{26... | collective-permute-start | bytes 196616 | tf_op jit(solution)/shard_map/ppermute | solution.py:454

commit v7 on v6

--- a/solution.py
+++ b/solution.py
@@ -114,7 +114,7 @@
 
 
 def lift_kernel(
-    part_ref, main_ref, lo_ref, hi_ref, ylo_ref, yhi_ref, ll_ref, lh_ref, hl_ref, hh_ref,
+    part_ref, main_ref, lo_ref, hi_ref, ylo_ref, yhi_ref,
     acc, ids, tgt_ref, sem,
 ):
     n = part_ref.shape[0]
@@ -149,17 +149,10 @@
                 lo_ref[x, :, cols] = v
             if x >= BX - 2:
                 hi_ref[x - BX + 2, :, cols] = v
-            for inside_y, first, face, low, high in (
-                (y < 2, 0, ylo_ref, ll_ref, hl_ref),
-                (y >= BY - 2, BY - 2, yhi_ref, lh_ref, hh_ref),
-            ):
-                if inside_y:
-                    strip = slice((y - first) * Z, (y - first + 1) * Z)
-                    face[x, :, strip] = v
-                    if x < 2:
-                        low[x, :, strip] = v
-                    if x >= BX - 2:
-                        high[x - BX + 2, :, strip] = v
+            if y < 2:
+                ylo_ref[x, :, cols] = v
+            if y >= BY - 2:
+                yhi_ref[x, :, (y - BY + 2) * Z : (y - BY + 3) * Z] = v
 
 
 def lift(part):
@@ -167,7 +160,7 @@
     return pl.pallas_call(
         lift_kernel,
         in_specs=[vmem],
-        out_specs=[vmem] * 9,
+        out_specs=[vmem] * 5,
         scratch_shapes=[
             pltpu.VMEM((BLK, 4 * C, Z), jnp.float32),
             pltpu.VMEM((8, Z), jnp.int32),
@@ -180,8 +173,7 @@
             jax.ShapeDtypeStruct((2, C, ROW), jnp.bfloat16),
             jax.ShapeDtypeStruct((BX, C, 2 * Z), jnp.bfloat16),
             jax.ShapeDtypeStruct((BX, C, 2 * Z), jnp.bfloat16),
-        ]
-        + [jax.ShapeDtypeStruct((2, C, 2 * Z), jnp.bfloat16)] * 4,
+        ],
         compiler_params=pltpu.CompilerParams(vmem_limit_bytes=32 << 20),
         name="lift",
     )(part)
@@ -321,18 +313,18 @@
 
 def outer_kernel(
     w_ref, bias_ref, coef_ref, outer_ref, edge_ref, near_ref, pend_ref,
-    xlo_ref, xhi_ref, ll_ref, lh_ref, hl_ref, hh_ref, part_ref,
+    xlo_ref, xhi_ref, clo_ref, chi_ref, part_ref,
     out_ref,
     xs_0, xs_1, xs_2, xs_3, flat_a, flat_b, packed, done,
 ):
     ends, flags = edges(), inside()
     pieces = [
-        (left.at[q], face.at[q], right.at[q])
-        for left, face, right, q in (
-            (ll_ref, xlo_ref, lh_ref, 0),
-            (ll_ref, xlo_ref, lh_ref, 1),
-            (hl_ref, xhi_ref, hh_ref, 1),
-            (hl_ref, xhi_ref, hh_ref, 0),
+        (corner.at[0, q], face.at[q], corner.at[1, q])
+        for face, corner, q in (
+            (xlo_ref, clo_ref, 0),
+            (xlo_ref, clo_ref, 1),
+            (xhi_ref, chi_ref, 1),
+            (xhi_ref, chi_ref, 0),
         )
     ]
     targets = [(0, 1), (BX - 1, BX - 2)]
@@ -428,7 +420,7 @@
     vmem = pl.BlockSpec(memory_space=pltpu.VMEM)
     return pl.pallas_call(
         outer_kernel,
-        in_specs=[vmem] * 13 + [hbm],
+        in_specs=[vmem] * 11 + [hbm],
         out_specs=hbm,
         scratch_shapes=[pltpu.VMEM((3 * C, WIDE), jnp.bfloat16)] * 4
         + [pltpu.VMEM((C * PITCH, Z), jnp.float32)] * 2
@@ -437,7 +429,7 @@
             pltpu.SemaphoreType.DMA((2, 2)),
         ],
         out_shape=jax.ShapeDtypeStruct((C, BX, BY, Z), jnp.bfloat16),
-        input_output_aliases={13: 0},
+        input_output_aliases={11: 0},
         compiler_params=pltpu.CompilerParams(vmem_limit_bytes=LIMIT << 20),
         name="conv_outer",
     )(weights, bias, coef, *state, *faces, *corners, volume)
@@ -469,11 +461,14 @@
         tiles,
     )
     got = lax.all_to_all(packed, ("views", "bricks"), split_axis=0, concat_axis=0, tiled=True)
-    main, lo, hi, ylo, yhi, ll, lh, hl, hh = lift(got)
+    main, lo, hi, ylo, yhi = lift(got)
     from_low = shift(yhi, 1, 0)
     from_high = shift(ylo, -1, 0)
     faces = shift(hi, 0, 1), shift(lo, 0, -1)
-    corners = shift(hh, 1, 1), shift(hl, -1, 1), shift(lh, 1, -1), shift(ll, -1, -1)
+    corners = (
+        shift(jnp.stack([from_low[BX - 2 :], from_high[BX - 2 :]]), 0, 1),
+        shift(jnp.stack([from_low[:2], from_high[:2]]), 0, -1),
+    )
     volume, *state = conv_inner(weights, bias, smooth_coef, main, from_low, from_high)
     return conv_outer(weights, bias, smooth_coef, state, faces, corners, volume)
 

time: 193 us -> 176 us (0.912)
  waiting for transfers between devices: 15.3 us -> 6.04 us
  starting transfers between devices: 25.6 us -> 17.9 us
    ppermute x8 -> x6, waiting for transfers between devices: 15.3 us -> 6.04 us  [shift(): return lax.ppermute(array, ('views', 'bricks'), pairs)]
    ppermute x8 -> x6, starting transfers between devices: 25.6 us -> 17.9 us  [shift(): return lax.ppermute(array, ('views', 'bricks'), pairs)]
  transfers between devices with their start and end apart: 8 -> 6, of which waited for: 1 -> 1; matrix products, arithmetic and copies ran while one was open for 0% -> 0% of each run, Pallas kernels for 8% -> 8%
where the time goes in v7:
time: 176 us; the launch traced here: 175 us
  blocking collectives  111 us (63%)
  Pallas kernels  35.7 us (20%)
  starting transfers between devices  17.9 us (10%)
  waiting for transfers between devices  6.04 us (3%)
  local copies, waits for them, and re-layouts  3.94 us (2%)
    all_to_all x1, blocking collectives, on_device(): lax.all_to_all(packed, ('views', 'bricks'), split_axis=0, concat_axis=0,...  111 us
    ppermute x6, starting transfers between devices, shift(): return lax.ppermute(array, ('views', 'bricks'), pairs)  17.9 us
    pallas_call x1, Pallas kernels, conv_inner(): pl.pallas_call(inner_kernel, in_specs=[vmem] * 6, out_specs=[hbm] + [vmem...  14.5 us
    pallas_call x1, Pallas kernels, partials(): pl.pallas_call(partial_kernel, in_specs=[smem, smem, smem, hbm, hbm, vmem...  10.7 us
    ppermute x6, waiting for transfers between devices, shift(): return lax.ppermute(array, ('views', 'bricks'), pairs)  6.04 us
    pallas_call x1, Pallas kernels, conv_outer(): pl.pallas_call(outer_kernel, in_specs=[vmem] * 11 + [hbm], out_specs=hbm,...  5.81 us
    pallas_call x1, Pallas kernels, lift(): pl.pallas_call(lift_kernel, in_specs=[vmem], out_specs=[vmem] * 5, scratc...  4.76 us
    unnamed x12, local copies, waits for them, and re-layouts  3.92 us
  transfers between devices with their start and end apart: 6, of which 1 were waited for; matrix products, arithmetic and copies ran while one was open for 0% of the time, Pallas kernels for 8%

profile of v7, /device:TPU:9, one launch (start us, length us, event | category | flops | bytes accessed | tf_op | source)
XLA Modules:
  0.0 175.4 jit_solution(16261624989777361011)
XLA Ops:
  0.7 0.0 copy-start.1
  0.7 1.0 copy-done.1
  1.7 0.0 copy-start.2
  1.7 0.9 copy-done.2
  2.6 0.0 copy-start.3
  2.6 0.7 copy-done.3
  3.3 0.0 copy-start.4
  3.3 0.7 copy-done.4
  3.9 0.0 copy-start.5
  3.9 0.7 copy-done.5
  4.6 10.7 %partials.1 = (bf16[128,264,128]{2,1,0:T(8,128)(2,1)}, bf16[192,576]{1,0:T(8,128)(2,1)S(1)}, f32[64,256]{1,0:T(8,128)S(1)}) custom-call(s32[128]{0:T(128)S(1)} %bitcast.18, s32[128]{0:T(128)S(1)} %bitcast.19, s32[1]{0:T(128)} %bitcast.15.count_ref, bf16[16,64,128]{2,1,0:T(8,128)(2,1)S(1)} %bitcast.17, bf16[27,64,64]{2,1,0:T(8,128)(2,1)S(1)} %bitcast.16, ...), custom_call_target="tpu_custom_call" | custom-call | tf_op jit(solution)/shard_map/partials/pallas_call | solution.py:93
  15.3 110.8 %all_to_all.5.part_ref = bf16[128,264,128]{2,1,0:T(8,128)(2,1)S(1)} all-to-all(bf16[128,264,128]{2,1,0:T(8,128)(2,1)} %get-tuple-element.20), channel_id=1, replica_groups=mesh['views'=8,'bricks'=16] {'views','bricks'}, dimensions={0} | all-to-all | bytes 17301504 | tf_op jit(solution)/shard_map/all_to_all | solution.py:463
  126.1 0.0 copy-start
  126.1 4.8 %lift.1 = (bf16[8,64,4096]{2,1,0:T(8,128)(2,1)S(1)}, bf16[2,64,4096]{2,1,0:T(8,128)(2,1)S(1)}, bf16[2,64,4096]{2,1,0:T(8,128)(2,1)S(1)}, bf16[8,64,256]{2,1,0:T(8,128)(2,1)S(1)}, bf16[8,64,256]{2,1,0:T(8,128)(2,1)S(1)}) custom-call(bf16[128,264,128]{2,1,0:T(8,128)(2,1)S(1)} %all_to_all.5.part_ref), custom_call_target="tpu_custom_call" | custom-call | tf_op jit(solution)/shard_map/lift/pallas_call | solution.py:160
  130.8 3.1 %collective-permute-start = (bf16[8,64,256]{2,1,0:T(8,128)(2,1)S(1)}, bf16[8,64,256]{2,1,0:T(8,128)(2,1)S(1)}, u32[]{:S(2)}, u32[]{:S(2)}) collective-permute-start(bf16[8,64,256]{2,1,0:T(8,128)(2,1)S(1)} %get-tuple-element.22), channel_id=1, source_target_pairs={{0,16},{1,17},{2,18},{3,19},{4,20},{5,21},{6,22},{7,23},{8,24},{9,... | collective-permute-start | bytes 786440 | tf_op jit(solution)/shard_map/ppermute | solution.py:446
  134.0 2.3 %collective-permute-start.2 = (bf16[2,64,4096]{2,1,0:T(8,128)(2,1)S(1)}, bf16[2,64,4096]{2,1,0:T(8,128)(2,1)S(1)}, u32[]{:S(2)}, u32[]{:S(2)}) collective-permute-start(bf16[2,64,4096]{2,1,0:T(8,128)(2,1)S(1)} %get-tuple-element.28), channel_id=1, source_target_pairs={{0,1},{1,2},{2,3},{3,4},{4,5},{5,6},{6,7},{7,8},{8,9},{9,10},{10,1... | collective-permute-start | bytes 3145736 | tf_op jit(solution)/shard_map/ppermute | solution.py:446
  136.2 5.1 %collective-permute-start.3 = (bf16[2,64,4096]{2,1,0:T(8,128)(2,1)S(1)}, bf16[2,64,4096]{2,1,0:T(8,128)(2,1)S(1)}, u32[]{:S(2)}, u32[]{:S(2)}) collective-permute-start(bf16[2,64,4096]{2,1,0:T(8,128)(2,1)S(1)} %get-tuple-element.29), channel_id=1, source_target_pairs={{1,0},{2,1},{3,2},{4,3},{5,4},{6,5},{7,6},{8,7},{9,8},{10,9},{11,1... | collective-permute-start | bytes 3145736 | tf_op jit(solution)/shard_map/ppermute | solution.py:446
  141.4 1.9 %collective-permute-start.1 = (bf16[8,64,256]{2,1,0:T(8,128)(2,1)S(1)}, bf16[8,64,256]{2,1,0:T(8,128)(2,1)S(1)}, u32[]{:S(2)}, u32[]{:S(2)}) collective-permute-start(bf16[8,64,256]{2,1,0:T(8,128)(2,1)S(1)} %get-tuple-element.23), channel_id=1, source_target_pairs={{16,0},{17,1},{18,2},{19,3},{20,4},{21,5},{22,6},{23,7},{24,8},{25... | collective-permute-start | bytes 786440 | tf_op jit(solution)/shard_map/ppermute | solution.py:446
  143.3 0.0 collective-permute-done.ylo_ref
  143.3 6.0 %collective-permute-done.1.yhi_ref = bf16[8,64,256]{2,1,0:T(8,128)(2,1)S(1)} collective-permute-done((bf16[8,64,256]{2,1,0:T(8,128)(2,1)S(1)}, bf16[8,64,256]{2,1,0:T(8,128)(2,1)S(1)}, u32[]{:S(2)}, u32[]{:S(2)}) %collective-permute-start.1) | collective-permute-done | bytes 262176 | tf_op jit(solution)/shard_map/ppermute | solution.py:446
  149.4 1.9 %collective-permute-start.5 = (bf16[2,2,64,256]{3,2,1,0:T(8,128)(2,1)S(1)}, bf16[2,2,64,256]{3,2,1,0:T(8,128)(2,1)S(1)}, u32[]{:S(2)}, u32[]{:S(2)}) collective-permute-start(bf16[2,2,64,256]{3,2,1,0:T(8,128)(2,1)S(1)} %pad_maximum_fusion.1), channel_id=1, source_target_pairs={{1,0},{2,1},{3,2},{4,3},{5,4},{6,5},{7,6},{8,7},{9,8},{10,9},{11,1... | collective-permute-start | bytes 393224 | tf_op jit(solution)/shard_map/ppermute | solution.py:446
  151.3 3.5 %collective-permute-start.4 = (bf16[2,2,64,256]{3,2,1,0:T(8,128)(2,1)S(1)}, bf16[2,2,64,256]{3,2,1,0:T(8,128)(2,1)S(1)}, u32[]{:S(2)}, u32[]{:S(2)}) collective-permute-start(bf16[2,2,64,256]{3,2,1,0:T(8,128)(2,1)S(1)} %pad_maximum_fusion), channel_id=1, source_target_pairs={{0,1},{1,2},{2,3},{3,4},{4,5},{5,6},{6,7},{7,8},{8,9},{9,10},{10,1... | collective-permute-start | bytes 393224 | tf_op jit(solution)/shard_map/ppermute | solution.py:446
  154.9 0.0 copy-done
  154.9 14.5 %conv_inner.1 = (bf16[64,8,32,128]{3,2,1,0:T(8,128)(2,1)}, f32[2,64,4352]{2,1,0:T(8,128)S(1)}, f32[2,64,4352]{2,1,0:T(8,128)S(1)}, f32[2,64,4096]{2,1,0:T(8,128)S(1)}, f32[2,64,4096]{2,1,0:T(8,128)S(1)}) custom-call(bf16[192,576]{1,0:T(8,128)(2,1)S(1)} %get-tuple-element.18.w_ref, f32[64,256]{1,0:T(8,128)S(1)} %get-tuple-element.19.bias_ref, ...), custom_call_target="tpu_custom_call" | custom-call | tf_op jit(solution)/shard_map/conv_inner/pallas_call | solution.py:390
  169.4 0.0 collective-permute-done.5.chi_ref
  169.4 0.0 collective-permute-done.4.clo_ref
  169.4 0.0 collective-permute-done.2.xlo_ref
  169.4 0.0 collective-permute-done.3.xhi_ref
  169.4 5.8 %conv_outer.1 = bf16[64,8,32,128]{3,2,1,0:T(8,128)(2,1)} custom-call(bf16[192,576]{1,0:T(8,128)(2,1)S(1)} %get-tuple-element.18.w_ref, f32[64,256]{1,0:T(8,128)S(1)} %get-tuple-element.19.bias_ref, f32[8,32,128]{2,1,0:T(8,128)S(1)} %copy-done, f32[2,64,4352]{2,1,0:T(8,128)S(1)} %get-tuple-element.24.outer_ref, ...), custom_call_target="tpu_custom_call", output_to_operand_aliasing={{}: (11, {})} | custom-call | tf_op jit(solution)/shard_map/conv_outer/pallas_call | solution.py:421
  (4 shorter events, 0.1 us)
Async XLA Ops:
  0.7 1.0 copy-start.1
  1.7 0.9 copy-start.2
  2.6 0.7 copy-start.3
  3.3 0.7 copy-start.4
  3.9 0.7 copy-start.5
  126.1 28.8 %copy-start = (f32[8,32,128]{2,1,0:T(8,128)S(1)}, f32[8,32,128]{2,1,0:T(8,128)}, u32[]{:S(2)}) copy-start(f32[8,32,128]{2,1,0:T(8,128)} %coef_ref.3) | copy-start | bytes 393220
  130.8 12.4 %collective-permute-start = (bf16[8,64,256]{2,1,0:T(8,128)(2,1)S(1)}, bf16[8,64,256]{2,1,0:T(8,128)(2,1)S(1)}, u32[]{:S(2)}, u32[]{:S(2)}) collective-permute-start(bf16[8,64,256]{2,1,0:T(8,128)(2,1)S(1)} %get-tuple-element.22), channel_id=1, source_target_pairs={{0,16},{1,17},{2,18},{3,19},{4,20},{5,21},{6,22},{7,23},{8,24},{9,... | collective-permute-start | bytes 786440 | tf_op jit(solution)/shard_map/ppermute | solution.py:446
  134.0 35.5 %collective-permute-start.2 = (bf16[2,64,4096]{2,1,0:T(8,128)(2,1)S(1)}, bf16[2,64,4096]{2,1,0:T(8,128)(2,1)S(1)}, u32[]{:S(2)}, u32[]{:S(2)}) collective-permute-start(bf16[2,64,4096]{2,1,0:T(8,128)(2,1)S(1)} %get-tuple-element.28), channel_id=1, source_target_pairs={{0,1},{1,2},{2,3},{3,4},{4,5},{5,6},{6,7},{7,8},{8,9},{9,10},{10,1... | collective-permute-start | bytes 3145736 | tf_op jit(solution)/shard_map/ppermute | solution.py:446
  136.2 33.2 %collective-permute-start.3 = (bf16[2,64,4096]{2,1,0:T(8,128)(2,1)S(1)}, bf16[2,64,4096]{2,1,0:T(8,128)(2,1)S(1)}, u32[]{:S(2)}, u32[]{:S(2)}) collective-permute-start(bf16[2,64,4096]{2,1,0:T(8,128)(2,1)S(1)} %get-tuple-element.29), channel_id=1, source_target_pairs={{1,0},{2,1},{3,2},{4,3},{5,4},{6,5},{7,6},{8,7},{9,8},{10,9},{11,1... | collective-permute-start | bytes 3145736 | tf_op jit(solution)/shard_map/ppermute | solution.py:446
  141.4 8.0 %collective-permute-start.1 = (bf16[8,64,256]{2,1,0:T(8,128)(2,1)S(1)}, bf16[8,64,256]{2,1,0:T(8,128)(2,1)S(1)}, u32[]{:S(2)}, u32[]{:S(2)}) collective-permute-start(bf16[8,64,256]{2,1,0:T(8,128)(2,1)S(1)} %get-tuple-element.23), channel_id=1, source_target_pairs={{16,0},{17,1},{18,2},{19,3},{20,4},{21,5},{22,6},{23,7},{24,8},{25... | collective-permute-start | bytes 786440 | tf_op jit(solution)/shard_map/ppermute | solution.py:446
  149.4 20.0 %collective-permute-start.5 = (bf16[2,2,64,256]{3,2,1,0:T(8,128)(2,1)S(1)}, bf16[2,2,64,256]{3,2,1,0:T(8,128)(2,1)S(1)}, u32[]{:S(2)}, u32[]{:S(2)}) collective-permute-start(bf16[2,2,64,256]{3,2,1,0:T(8,128)(2,1)S(1)} %pad_maximum_fusion.1), channel_id=1, source_target_pairs={{1,0},{2,1},{3,2},{4,3},{5,4},{6,5},{7,6},{8,7},{9,8},{10,9},{11,1... | collective-permute-start | bytes 393224 | tf_op jit(solution)/shard_map/ppermute | solution.py:446
  151.3 18.1 %collective-permute-start.4 = (bf16[2,2,64,256]{3,2,1,0:T(8,128)(2,1)S(1)}, bf16[2,2,64,256]{3,2,1,0:T(8,128)(2,1)S(1)}, u32[]{:S(2)}, u32[]{:S(2)}) collective-permute-start(bf16[2,2,64,256]{3,2,1,0:T(8,128)(2,1)S(1)} %pad_maximum_fusion), channel_id=1, source_target_pairs={{0,1},{1,2},{2,3},{3,4},{4,5},{5,6},{6,7},{7,8},{8,9},{9,10},{10,1... | collective-permute-start | bytes 393224 | tf_op jit(solution)/shard_map/ppermute | solution.py:446
